TPU v7x, 512 devices: a whole 4x4x16 slice. The times are simulated.
512 devices in a mesh: gx: 32 (over z, y_lo), row: 8 (over x, core), th: 2 (over y_hi).
Axes of the slice: x: 4, y: 4 (y_hi: 2, y_lo: 2; y = y_hi * 2 + y_lo), z: 16, core: 2. Of those that a mesh axis runs over, the one named last changes fastest.
Arguments:
- state: float32 [5, 1024, 128, 256], P(None, 'gx', 'row', 'th'), may hold values from -2 to 4, as said below
- adjoint_seed: float32 [5, 1024, 128, 256], P(None, 'gx', 'row', 'th'), may hold values from -6 to 6
- coef_x: float32 [9], replicated, may hold values from -1.75 to 1.75
- coef_r: float32 [9], replicated, may hold values from -1.75 to 1.75
- coef_t: float32 [9], replicated, may hold values from -1.75 to 1.75
- coef_filter: float32 [9], replicated, may hold values from -0.625 to 0.625
- metric: float32 [128], P('row'), may hold values from 0.5 to 2
Outputs:
- new_state: float32 [5, 1024, 128, 256], P(None, 'gx', 'row', 'th')
- adjoint_state: float32 [5, 1024, 128, 256], P(None, 'gx', 'row', 'th')
Inputs may be any that keep to these rules, and one draw needn't show every extreme that they name: `state`: component 0 (density) lies in [0.5, 1.5], components 1 to 3 (momenta) in [-2, 2], component 4 (total energy) in [2, 4].
All inputs are finite; a program needn't handle non-finite values.
Results may differ from a plain program's by a relative error of at most 0.0001.
Values sent between devices are 32-bit elements; how exact they have to be, the bound alone decides.
No kernel may reach another device: no remote copies, remote signals or barrier semaphores. Data moves between devices by JAX's collectives and lax.ppermute only.
A program may use at most 64 MiB of HBM per device.

v0:
```python
import jax
import jax.numpy as jnp
from jax import lax
from jax.sharding import PartitionSpec as P

section_dt = 0.1
gamma_less = 0.4
highest = lax.Precision.HIGHEST


def extended(cells, sides, width):
    for axis, dim in sides:
        count = lax.axis_size(axis)
        ends = count - 1
        head = lax.slice_in_dim(cells, 0, width, axis=dim)
        tail = lax.slice_in_dim(cells, cells.shape[dim] - width, cells.shape[dim], axis=dim)
        cells = jnp.concatenate(
            [
                lax.ppermute(tail, axis, [(i, (i + 1) % count) for i in range(ends)]),
                cells,
                lax.ppermute(head, axis, [((i + 1) % count, i) for i in range(ends)]),
            ],
            axis=dim,
        )
    return cells


def from_partner(value, axis, bit):
    mask = 2**bit
    pairs = [(source, source ^ mask) for source in range(lax.axis_size(axis))]
    return lax.ppermute(value, axis, pairs)


def fluxes(state):
    density = state[0]
    velocity = state[1:4] / density
    pressure = gamma_less * (state[4] - 0.5 * jnp.sum(state[1:4] * velocity, axis=0))
    enthalpy = state[4] + pressure
    result = []
    for direction in range(3):
        speed = velocity[direction]
        moment = state[1:4] * speed
        moment = moment.at[direction].add(pressure)
        result.append(
            jnp.concatenate([state[1 + direction][None], moment, (enthalpy * speed)[None]], axis=0)
        )
    return result


def band_matrix(coef, count):
    taps = coef.shape[0]
    rows = lax.broadcasted_iota(jnp.int32, (count + taps - 1, count), 0)
    cols = lax.broadcasted_iota(jnp.int32, (count + taps - 1, count), 1)
    offset = rows - cols
    picks = jnp.arange(taps, dtype=jnp.int32)
    hits = offset[None, :, :] == picks[:, None, None]
    return jnp.sum(jnp.where(hits, coef[:, None, None], 0.0), axis=0)


def along_x(ext, band):
    return jnp.einsum("vard,ai->vird", ext, band, precision=highest)


def along_r(ext, band):
    return jnp.einsum("vxad,ai->vxid", ext, band, precision=highest)


def along_t(ext, band):
    return jnp.einsum("vxra,ai->vxri", ext, band, precision=highest)


def shards(state, adjoint_seed, coef_x, coef_r, coef_t, coef_filter, metric):
    cells_x = state.shape[1]
    cells_r = state.shape[2]
    cells_t = state.shape[3]
    reach = (coef_x.shape[0] - 1) // 2
    weight_r = metric[None, None, :, None]
    flux_x, flux_r, flux_t = fluxes(state)
    wide_x = extended(flux_x, (("gx", 1),), reach)
    wide_r = extended(flux_r, (("row", 2),), reach)
    rims = jnp.concatenate([flux_t[..., cells_t - reach :], flux_t[..., :reach]], axis=3)
    other = from_partner(rims, "th", 0)
    wide_t = jnp.concatenate([other[..., :reach], flux_t, other[..., reach:]], axis=3)
    resid = -(
        along_x(wide_x, band_matrix(coef_x, cells_x))
        + along_r(wide_r, band_matrix(coef_r, cells_r))
        + weight_r * along_t(wide_t, band_matrix(coef_t, cells_t))
    )
    section = state + section_dt * resid
    wide_section = extended(section, (("gx", 1),), reach)
    new_state = section - along_x(wide_section, band_matrix(coef_filter, cells_x))
    flip_filter = coef_filter[::-1]
    flip_x = coef_x[::-1]
    wide_seed = extended(adjoint_seed, (("gx", 1),), reach)
    lam_section = adjoint_seed - along_x(wide_seed, band_matrix(flip_filter, cells_x))
    lam_resid = section_dt * lam_section
    wide_lam = extended(lam_resid, (("gx", 1),), reach)
    grad_x = -along_x(wide_lam, band_matrix(flip_x, cells_x))
    wide_lam_r = extended(lam_resid, (("row", 2),), reach)
    grad_r = -along_r(wide_lam_r, band_matrix(coef_r[::-1], cells_r))
    weighted = weight_r * lam_resid
    rims_back = jnp.concatenate([weighted[..., cells_t - reach :], weighted[..., :reach]], axis=3)
    other_back = from_partner(rims_back, "th", 0)
    wide_lam_t = jnp.concatenate(
        [other_back[..., :reach], weighted, other_back[..., reach:]], axis=3
    )
    grad_t = -along_t(wide_lam_t, band_matrix(coef_t[::-1], cells_t))
    _, pull = jax.vjp(fluxes, state)
    (flux_grad,) = pull([grad_x, grad_r, grad_t])
    adjoint_state = lam_section + flux_grad
    return (new_state, adjoint_state)


def solution(mesh):
    placed = (P(None, "gx", "row", "th"), P(None, "gx", "row", "th"), P(), P(), P(), P(), P("row"))
    return jax.shard_map(
        shards,
        mesh=mesh,
        in_specs=placed,
        out_specs=(P(None, "gx", "row", "th"), P(None, "gx", "row", "th")),
        check_vma=False,
    )
```

profile of v0, /device:TPU:232, one launch (start us, length us, event | category | flops | bytes accessed | tf_op | source)
XLA Modules:
  0.0 131.4 jit_solution(5369517840451919222)
XLA Ops:
  0.7 1.8 %copy.79 = f32[5,32,16,128]{3,1,2,0:T(8,128)S(1)} copy(f32[5,32,16,128]{3,2,1,0:T(8,128)} %param.14) | data formatting | bytes 2621440 | tf_op args[1]
  2.5 1.0 copy-done
  3.6 4.9 %collective-permute-start.7 = (f32[5,4,16,128]{3,1,2,0:T(4,128)S(1)}, f32[5,4,16,128]{3,1,2,0:T(4,128)S(1)}, u32[]{:S(2)}, u32[]{:S(2)}) collective-permute-start(f32[5,4,16,128]{3,1,2,0:T(4,128)S(1)} %get-tuple-element.95), channel_id=1, source_target_pairs={{0,16},{16,32},{32,48},{48,64},{64,80},{80,96},{96,112},{112,128},... | collective-permute-start | bytes 491528 | tf_op jit(solution)/shard_map/ppermute | solution.py:19
  8.6 1.9 %collective-permute-start.8 = (f32[5,4,16,128]{3,1,2,0:T(4,128)S(1)}, f32[5,4,16,128]{3,1,2,0:T(4,128)S(1)}, u32[]{:S(2)}, u32[]{:S(2)}) collective-permute-start(f32[5,4,16,128]{3,1,2,0:T(4,128)S(1)} %get-tuple-element.96), channel_id=1, source_target_pairs={{16,0},{32,16},{48,32},{64,48},{80,64},{96,80},{112,96},{128,112},... | collective-permute-start | bytes 491528 | tf_op jit(solution)/shard_map/ppermute | solution.py:21
  12.3 1.5 %copy.75 = f32[5,32,16,128]{3,1,2,0:T(8,128)} copy(f32[5,32,16,128]{3,2,1,0:T(8,128)S(1)} %copy-done.2) | data formatting | bytes 2621440 | tf_op args[0]
  15.6 2.6 %collective-permute-done.8 = f32[5,4,16,128]{3,1,2,0:T(4,128)S(1)} collective-permute-done((f32[5,4,16,128]{3,1,2,0:T(4,128)S(1)}, f32[5,4,16,128]{3,1,2,0:T(4,128)S(1)}, u32[]{:S(2)}, u32[]{:S(2)}) %collective-permute-start.8) | collective-permute-done | bytes 163872 | tf_op jit(solution)/shard_map/ppermute | solution.py:21
  18.2 4.3 %broadcast_multiply_fusion.1 = (f32[5,32,16,128]{3,1,2,0:T(8,128)S(1)}, f32[5,32,16,128]{3,1,2,0:T(8,128)S(1)}, f32[5,32,16,128]{3,1,2,0:T(8,128)}) fusion(f32[16]{0:T(128)S(1)} %broadcast_multiply_fusion.6, f32[5,32,16,128]{3,1,2,0:T(8,128)} %copy-done, f32[5,4,16,128]{3,1,2,0:T(4,128)S(1)} %collective-permute-done.8, ...), kind=kOutput, calls=%fused_computation.78 | convolution fusion | flops 159088640 | bytes 5575744 | tf_op jit(solution)/shard_map/vard,ai->vird/dot_general | solution.py:61
  23.3 2.0 %fusion.122 = (f32[5,32,16,4]{3,1,2,0:T(8,128)}, f32[5,32,16,4]{3,1,2,0:T(8,128)}) fusion(f32[5,32,16,128]{3,1,2,0:T(8,128)S(1)} %get-tuple-element.92), kind=kLoop, calls=%fused_computation.161 | loop fusion | bytes 163840 | tf_op jit(solution)/shard_map/slice | solution.py:102
  25.2 1.9 %copy.80 = f32[5,32,16,4]{1,3,2,0:T(4,128)S(1)} copy(f32[5,32,16,4]{3,1,2,0:T(8,128)} %get-tuple-element.93) | data formatting | bytes 81920 | tf_op jit(solution)/shard_map/slice | solution.py:102
  27.1 1.9 %copy.81 = f32[5,32,16,4]{1,3,2,0:T(4,128)S(1)} copy(f32[5,32,16,4]{3,1,2,0:T(8,128)} %get-tuple-element.94) | data formatting | bytes 81920 | tf_op jit(solution)/shard_map/slice | solution.py:102
  29.1 4.5 %collective-permute-start.9 = (f32[5,32,16,8]{1,3,2,0:T(8,128)S(1)}, f32[5,32,16,8]{1,3,2,0:T(8,128)S(1)}, u32[]{:S(2)}, u32[]{:S(2)}) collective-permute-start(f32[5,32,16,8]{1,3,2,0:T(8,128)S(1)} %pad_maximum_fusion.7), channel_id=1, source_target_pairs={{0,1},{1,0},{2,3},{3,2},{4,5},{5,4},{6,7},{7,6},{8,9},{9,8},{10,11... | collective-permute-start | bytes 245768 | tf_op jit(solution)/shard_map/ppermute | solution.py:31
  34.4 4.4 %collective-permute-start.12 = (f32[5,4,16,128]{3,1,2,0:T(4,128)}, f32[5,4,16,128]{3,1,2,0:T(4,128)}, u32[]{:S(2)}, u32[]{:S(2)}) collective-permute-start(f32[5,4,16,128]{3,1,2,0:T(4,128)} %get-tuple-element.87), channel_id=1, source_target_pairs={{0,16},{16,32},{32,48},{48,64},{64,80},{80,96},{96,112},{112,128},... | collective-permute-start | bytes 491528 | tf_op jit(solution)/shard_map/ppermute | solution.py:19
  38.8 1.9 %collective-permute-start.13 = (f32[5,4,16,128]{3,1,2,0:T(4,128)}, f32[5,4,16,128]{3,1,2,0:T(4,128)}, u32[]{:S(2)}, u32[]{:S(2)}) collective-permute-start(f32[5,4,16,128]{3,1,2,0:T(4,128)} %get-tuple-element.88), channel_id=1, source_target_pairs={{16,0},{32,16},{48,32},{64,48},{80,64},{96,80},{112,96},{128,112},... | collective-permute-start | bytes 491528 | tf_op jit(solution)/shard_map/ppermute | solution.py:21
  40.7 2.1 %collective-permute-start.10 = (f32[5,32,4,128]{3,1,2,0:T(8,128)}, f32[5,32,4,128]{3,1,2,0:T(8,128)}, u32[]{:S(2)}, u32[]{:S(2)}) collective-permute-start(f32[5,32,4,128]{3,1,2,0:T(8,128)} %get-tuple-element.89), channel_id=1, source_target_pairs={{0,2},{2,4},{4,6},{6,8},{8,10},{10,12},{12,14},{1,3},{3,5},{5,7},{... | collective-permute-start | bytes 983048 | tf_op jit(solution)/shard_map/ppermute | solution.py:19
  42.8 1.5 %collective-permute-start.11 = (f32[5,32,4,128]{3,1,2,0:T(8,128)S(1)}, f32[5,32,4,128]{3,1,2,0:T(8,128)}, u32[]{:S(2)}, u32[]{:S(2)}) collective-permute-start(f32[5,32,4,128]{3,1,2,0:T(8,128)S(1)} %get-tuple-element.90), channel_id=1, source_target_pairs={{2,0},{4,2},{6,4},{8,6},{10,8},{12,10},{14,12},{3,1},{5,3},{7,5},{... | collective-permute-start | bytes 983048 | tf_op jit(solution)/shard_map/ppermute | solution.py:21
  44.3 1.5 %collective-permute-done.9 = f32[5,32,16,8]{1,3,2,0:T(8,128)S(1)} collective-permute-done((f32[5,32,16,8]{1,3,2,0:T(8,128)S(1)}, f32[5,32,16,8]{1,3,2,0:T(8,128)S(1)}, u32[]{:S(2)}, u32[]{:S(2)}) %collective-permute-start.9) | collective-permute-done | bytes 81952 | tf_op jit(solution)/shard_map/ppermute | solution.py:31
  45.9 1.6 %copy.105 = f32[5,32,16,4]{3,1,2,0:T(8,128)} copy(f32[5,32,16,4]{1,3,2,0:T(4,128)S(1)} %get-tuple-element.105) | data formatting | bytes 81920
  47.5 1.6 %copy.106 = f32[5,32,16,4]{3,1,2,0:T(8,128)} copy(f32[5,32,16,4]{1,3,2,0:T(4,128)S(1)} %get-tuple-element.106) | data formatting | bytes 81920
  49.1 4.3 %fusion.63 = f32[5,32,16,128]{3,1,2,0:T(8,128)S(1)} fusion(f32[5,32,16,4]{3,1,2,0:T(8,128)} %copy.106, f32[5,32,16,128]{3,1,2,0:T(8,128)S(1)} %get-tuple-element.92, f32[5,32,16,4]{3,1,2,0:T(8,128)} %copy.105, f32[136,128]{1,0:T(8,128)S(1)} %copy-done.25), kind=kOutput, calls=%fused_computation.55 | convolution fusion | flops 535797760 | bytes 2772992 | tf_op jit(solution)/shard_map/vxra,ai->vxri/dot_general | solution.py:69
  53.5 2.3 %fusion.51 = f32[5,32,16,128]{3,1,2,0:T(8,128)S(1)} fusion(f32[5,4,16,128]{3,1,2,0:T(4,128)} %collective-permute-done.13, f32[5,32,16,128]{3,1,2,0:T(8,128)S(1)} %get-tuple-element.91, f32[5,4,16,128]{3,1,2,0:T(4,128)} %collective-permute-done.12, f32[40,32]{0,1:T(8,128)S(1)} %copy-done.28), kind=kOutput, calls=%fused_computation.51 | convolution fusion | flops 158433280 | bytes 2954240 | tf_op jit(solution)/shard_map/vard,ai->vird/dot_general | solution.py:61
  55.8 1.2 pad_maximum_fusion.1
  57.1 2.4 %fusion.16 = f32[16,5,32,128]{3,0,2,1:T(8,128)S(1)} fusion(f32[5,32,24,128]{3,1,2,0:T(8,128)S(1)} %pad_maximum_fusion.1, f32[24,16]{0,1:T(8,128)S(1)} %copy-done.30), kind=kOutput, calls=%fused_computation.18 | convolution fusion | flops 94371840 | bytes 3278336 | tf_op jit(solution)/shard_map/vxad,ai->vxid/dot_general | solution.py:65
  62.6 1.4 %slice_multiply_fusion = (f32[3,32,16,128]{3,1,2,0:T(8,128)}, f32[3,32,16,128]{3,1,2,0:T(8,128)}) fusion(f32[5,32,16,128]{3,1,2,0:T(8,128)S(1)} %fusion.51, f32[32,16,128]{2,0,1:T(8,128)S(1)} %get-tuple-element.102, f32[3,32,16,128]{3,1,2,0:T(8,128)S(1)} %get-tuple-element.61, f32[32,16,128]{2,0,1:T(8,128)S(1)} %fusion.99), kind=kLoop, calls=%fused_computation.74 | loop fusion | flops 393216 | bytes 3670016 | tf_op jit(solution)/shard_map/transpose(jvp())/mul | solution.py:42
  64.0 1.5 %fusion.117 = (f32[1,32,16,128]{3,1,2,0:T(8,128)}, f32[1,32,16,128]{3,1,2,0:T(8,128)S(1)}, f32[1,32,16,128]{3,1,2,0:T(8,128)}, f32[1,32,16,128]{3,1,2,0:T(8,128)...) fusion(f32[5,32,16,128]{3,1,2,0:T(8,128)S(1)} %fusion.90, ...), kind=kLoop, calls=%fused_computation.156 | loop fusion | flops 1048576 | bytes 6029312 | tf_op jit(solution)/shard_map/transpose(jvp())/split | solution.py:45
  65.5 1.8 %fusion.91 = (f32[3,32,16,128]{3,1,2,0:T(8,128)}, f32[32,16,128]{2,0,1:T(8,128)S(1)}, f32[3,32,16,128]{3,1,2,0:T(8,128)S(1)}, f32[3,32,16,128]{3,1,2,0:T(8,128)S...) fusion(f32[1,32,16,128]{3,1,2,0:T(8,128)S(1)} %get-tuple-element.72, ...), kind=kLoop, calls=%fused_computation.82 | loop fusion | flops 2490368 | bytes 9699328 | tf_op jit(solution)/shard_map/transpose(jvp())/div | solution.py:36
  69.1 4.5 %collective-permute-start = (f32[5,4,16,128]{3,1,2,0:T(4,128)}, f32[5,4,16,128]{3,1,2,0:T(4,128)}, u32[]{:S(2)}, u32[]{:S(2)}) collective-permute-start(f32[5,4,16,128]{3,1,2,0:T(4,128)} %get-tuple-element.83), channel_id=1, source_target_pairs={{0,16},{16,32},{32,48},{48,64},{64,80},{80,96},{96,112},{112,128},... | collective-permute-start | bytes 491528 | tf_op jit(solution)/shard_map/ppermute | solution.py:19
  73.6 1.9 %collective-permute-start.1 = (f32[5,4,16,128]{3,1,2,0:T(4,128)}, f32[5,4,16,128]{3,1,2,0:T(4,128)}, u32[]{:S(2)}, u32[]{:S(2)}) collective-permute-start(f32[5,4,16,128]{3,1,2,0:T(4,128)} %get-tuple-element.84), channel_id=1, source_target_pairs={{16,0},{32,16},{48,32},{64,48},{80,64},{96,80},{112,96},{128,112},... | collective-permute-start | bytes 491528 | tf_op jit(solution)/shard_map/ppermute | solution.py:21
  75.7 1.5 %fusion.119 = (f32[5,32,16,4]{3,1,2,0:T(8,128)}, f32[5,32,16,4]{3,1,2,0:T(8,128)S(1)}) fusion(f32[5,32,16,128]{3,1,2,0:T(8,128)S(1)} %pad_maximum_fusion.2), kind=kLoop, calls=%fused_computation.158 | loop fusion | bytes 163840 | tf_op jit(solution)/shard_map/slice | solution.py:81
  77.2 2.5 %copy.69 = f32[5,32,16,4]{1,3,2,0:T(4,128)} copy(f32[5,32,16,4]{3,1,2,0:T(8,128)} %get-tuple-element.85) | data formatting | bytes 81920 | tf_op jit(solution)/shard_map/slice | solution.py:81
  79.7 1.2 copy.70
  80.9 1.1 pad_maximum_fusion.6
  82.0 4.7 %collective-permute-start.4 = (f32[5,32,16,8]{1,3,2,0:T(8,128)S(1)}, f32[5,32,16,8]{1,3,2,0:T(8,128)S(1)}, u32[]{:S(2)}, u32[]{:S(2)}) collective-permute-start(f32[5,32,16,8]{1,3,2,0:T(8,128)S(1)} %pad_maximum_fusion.6), channel_id=1, source_target_pairs={{0,1},{1,0},{2,3},{3,2},{4,5},{5,4},{6,7},{7,6},{8,9},{9,8},{10,11... | collective-permute-start | bytes 245768 | tf_op jit(solution)/shard_map/ppermute | solution.py:31
  86.8 1.8 %pad_maximum_fusion.5 = (f32[5,32,4,128]{3,1,2,0:T(8,128)}, f32[5,32,4,128]{3,1,2,0:T(8,128)}) fusion(f32[1,32,16,128]{3,1,2,0:T(8,128)S(1)} %get-tuple-element.98, f32[3,32,16,128]{3,1,2,0:T(8,128)S(1)} %get-tuple-element.109, f32[1,32,16,128]{3,1,2,0:T(8,128)} %get-tuple-element.65), kind=kLoop, calls=%fused_computation.90 | loop fusion | flops 327680 | bytes 1966080 | tf_op jit(solution)/shard_map/slice | solution.py:16
  88.5 2.0 %collective-permute-start.2 = (f32[5,32,4,128]{3,1,2,0:T(8,128)}, f32[5,32,4,128]{3,1,2,0:T(8,128)}, u32[]{:S(2)}, u32[]{:S(2)}) collective-permute-start(f32[5,32,4,128]{3,1,2,0:T(8,128)} %get-tuple-element.81), channel_id=1, source_target_pairs={{0,2},{2,4},{4,6},{6,8},{8,10},{10,12},{12,14},{1,3},{3,5},{5,7},{... | collective-permute-start | bytes 983048 | tf_op jit(solution)/shard_map/ppermute | solution.py:19
  90.5 1.3 collective-permute-start.3
  91.8 3.4 %collective-permute-done.4 = f32[5,32,16,8]{1,3,2,0:T(8,128)S(1)} collective-permute-done((f32[5,32,16,8]{1,3,2,0:T(8,128)S(1)}, f32[5,32,16,8]{1,3,2,0:T(8,128)S(1)}, u32[]{:S(2)}, u32[]{:S(2)}) %collective-permute-start.4) | collective-permute-done | bytes 81952 | tf_op jit(solution)/shard_map/ppermute | solution.py:31
  96.0 2.6 %copy.103 = f32[5,32,16,4]{3,1,2,0:T(8,128)} copy(f32[5,32,16,4]{1,3,2,0:T(4,128)} %get-tuple-element.103) | data formatting | bytes 81920
  98.6 1.6 %copy.104 = f32[5,32,16,4]{3,1,2,0:T(8,128)} copy(f32[5,32,16,4]{1,3,2,0:T(4,128)S(1)} %get-tuple-element.104) | data formatting | bytes 81920
  100.2 4.4 %fusion.87 = f32[5,32,16,128]{3,1,2,0:T(8,128)S(1)} fusion(f32[5,32,16,4]{3,1,2,0:T(8,128)} %copy.104, f32[1,32,16,128]{3,1,2,0:T(8,128)S(1)} %copy-done.20, f32[3,32,16,128]{3,1,2,0:T(8,128)S(1)} %copy-done.6, f32[1,32,16,128]{3,1,2,0:T(8,128)} %copy-done.24, f32[5,32,16,4]{3,1,2,0:T(8,128)} %copy.103, f32[16]{0:T(128)S(1)} %copy-done.36, ...), kind=kOutput, calls=%fused_computation.63 | convolution fusion | flops 536494080 | bytes 2773056 | tf_op jit(solution)/shard_map/vxra,ai->vxri/dot_general | solution.py:69
  104.7 1.2 pad_maximum_fusion
  106.0 2.3 %fusion.18 = f32[16,5,32,128]{3,0,2,1:T(8,128)S(1)} fusion(f32[5,32,24,128]{3,1,2,0:T(8,128)S(1)} %pad_maximum_fusion, f32[24,16]{0,1:T(8,128)S(1)} %copy-done.29), kind=kOutput, calls=%fused_computation.20 | convolution fusion | flops 94371840 | bytes 3278336 | tf_op jit(solution)/shard_map/vxad,ai->vxid/dot_general | solution.py:65
  108.5 3.3 %fusion.84 = f32[5,32,16,128]{3,1,2,0:T(8,128)S(1)} fusion(f32[5,32,16,128]{3,1,2,0:T(8,128)S(1)} %fusion.87, f32[5,4,16,128]{3,1,2,0:T(4,128)} %collective-permute-done.1, f32[1,32,16,128]{3,1,2,0:T(8,128)S(1)} %get-tuple-element.99, f32[3,32,16,128]{3,1,2,0:T(8,128)S(1)} %get-tuple-element.111, f32[1,32,16,128]{3,1,2,0:T(8,128)S(1)} %copy-done.13, ...), kind=kOutput, calls=%fused_computation.62 | convolution fusion | flops 160563200 | bytes 6886400 | tf_op jit(solution)/shard_map/vard,ai->vird/dot_general | solution.py:61
  111.9 6.3 %collective-permute-start.5 = (f32[5,4,16,128]{3,1,2,0:T(4,128)S(1)}, f32[5,4,16,128]{3,1,2,0:T(4,128)S(1)}, u32[]{:S(2)}, u32[]{:S(2)}) collective-permute-start(f32[5,4,16,128]{3,1,2,0:T(4,128)S(1)} %get-tuple-element.79), channel_id=1, source_target_pairs={{0,16},{16,32},{32,48},{48,64},{64,80},{80,96},{96,112},{112,128},... | collective-permute-start | bytes 491528 | tf_op jit(solution)/shard_map/ppermute | solution.py:19
  118.2 2.2 %collective-permute-start.6 = (f32[5,4,16,128]{3,1,2,0:T(4,128)S(1)}, f32[5,4,16,128]{3,1,2,0:T(4,128)S(1)}, u32[]{:S(2)}, u32[]{:S(2)}) collective-permute-start(f32[5,4,16,128]{3,1,2,0:T(4,128)S(1)} %get-tuple-element.80), channel_id=1, source_target_pairs={{16,0},{32,16},{48,32},{64,48},{80,64},{96,80},{112,96},{128,112},... | collective-permute-start | bytes 491528 | tf_op jit(solution)/shard_map/ppermute | solution.py:21
  121.3 1.8 %copy.90 = f32[5,32,16,128]{3,2,1,0:T(8,128)} copy(f32[5,32,16,128]{3,1,2,0:T(8,128)S(1)} %add_add_fusion) | data formatting | bytes 2621440
  123.1 5.2 %collective-permute-done.6 = f32[5,4,16,128]{3,1,2,0:T(4,128)S(1)} collective-permute-done((f32[5,4,16,128]{3,1,2,0:T(4,128)S(1)}, f32[5,4,16,128]{3,1,2,0:T(4,128)S(1)}, u32[]{:S(2)}, u32[]{:S(2)}) %collective-permute-start.6) | collective-permute-done | bytes 163872 | tf_op jit(solution)/shard_map/ppermute | solution.py:21
  128.3 1.3 fusion.69
  129.6 1.8 %copy.89 = f32[5,32,16,128]{3,2,1,0:T(8,128)} copy(f32[5,32,16,128]{3,1,2,0:T(8,128)S(1)} %fusion.69) | data formatting | bytes 2621440
  (114 shorter events, 12.2 us)
Async XLA Ops:
  0.6 9.9 %copy-start.31 = (f32[9]{0:T(128)S(1)}, f32[9]{0:T(128)}, u32[]{:S(2)}) copy-start(f32[9]{0:T(128)} %param.15) | copy-start | bytes 112
  0.6 10.0 %copy-start.34 = (f32[9]{0:T(128)S(1)}, f32[9]{0:T(128)}, u32[]{:S(2)}) copy-start(f32[9]{0:T(128)} %param.16) | copy-start | bytes 112
  0.7 10.1 %copy-start.32 = (f32[9]{0:T(128)S(1)}, f32[9]{0:T(128)}, u32[]{:S(2)}) copy-start(f32[9]{0:T(128)} %param.18) | copy-start | bytes 112
  0.7 10.2 %copy-start.35 = (f32[16]{0:T(128)S(1)}, f32[16]{0:T(128)}, u32[]{:S(2)}) copy-start(f32[16]{0:T(128)} %param.19) | copy-start | bytes 196
  0.7 10.2 %copy-start.2 = (f32[5,32,16,128]{3,2,1,0:T(8,128)S(1)}, f32[5,32,16,128]{3,2,1,0:T(8,128)}, u32[]{:S(2)}) copy-start(f32[5,32,16,128]{3,2,1,0:T(8,128)} %param.13) | copy-start | bytes 3932164
  3.6 12.0 %collective-permute-start.7 = (f32[5,4,16,128]{3,1,2,0:T(4,128)S(1)}, f32[5,4,16,128]{3,1,2,0:T(4,128)S(1)}, u32[]{:S(2)}, u32[]{:S(2)}) collective-permute-start(f32[5,4,16,128]{3,1,2,0:T(4,128)S(1)} %get-tuple-element.95), channel_id=1, source_target_pairs={{0,16},{16,32},{32,48},{48,64},{64,80},{80,96},{96,112},{112,128},... | collective-permute-start | bytes 491528 | tf_op jit(solution)/shard_map/ppermute | solution.py:19
  8.6 9.7 %collective-permute-start.8 = (f32[5,4,16,128]{3,1,2,0:T(4,128)S(1)}, f32[5,4,16,128]{3,1,2,0:T(4,128)S(1)}, u32[]{:S(2)}, u32[]{:S(2)}) collective-permute-start(f32[5,4,16,128]{3,1,2,0:T(4,128)S(1)} %get-tuple-element.96), channel_id=1, source_target_pairs={{16,0},{32,16},{48,32},{64,48},{80,64},{96,80},{112,96},{128,112},... | collective-permute-start | bytes 491528 | tf_op jit(solution)/shard_map/ppermute | solution.py:21
  12.3 1.5 %copy-start.33 = (f32[9]{0:T(128)S(1)}, f32[9]{0:T(128)}, u32[]{:S(2)}) copy-start(f32[9]{0:T(128)} %param.17) | copy-start | bytes 112
  29.1 16.7 %collective-permute-start.9 = (f32[5,32,16,8]{1,3,2,0:T(8,128)S(1)}, f32[5,32,16,8]{1,3,2,0:T(8,128)S(1)}, u32[]{:S(2)}, u32[]{:S(2)}) collective-permute-start(f32[5,32,16,8]{1,3,2,0:T(8,128)S(1)} %pad_maximum_fusion.7), channel_id=1, source_target_pairs={{0,1},{1,0},{2,3},{3,2},{4,5},{5,4},{6,7},{7,6},{8,9},{9,8},{10,11... | collective-permute-start | bytes 245768 | tf_op jit(solution)/shard_map/ppermute | solution.py:31
  34.4 19.0 %collective-permute-start.12 = (f32[5,4,16,128]{3,1,2,0:T(4,128)}, f32[5,4,16,128]{3,1,2,0:T(4,128)}, u32[]{:S(2)}, u32[]{:S(2)}) collective-permute-start(f32[5,4,16,128]{3,1,2,0:T(4,128)} %get-tuple-element.87), channel_id=1, source_target_pairs={{0,16},{16,32},{32,48},{48,64},{64,80},{80,96},{96,112},{112,128},... | collective-permute-start | bytes 491528 | tf_op jit(solution)/shard_map/ppermute | solution.py:19
  38.8 14.7 %collective-permute-start.13 = (f32[5,4,16,128]{3,1,2,0:T(4,128)}, f32[5,4,16,128]{3,1,2,0:T(4,128)}, u32[]{:S(2)}, u32[]{:S(2)}) collective-permute-start(f32[5,4,16,128]{3,1,2,0:T(4,128)} %get-tuple-element.88), channel_id=1, source_target_pairs={{16,0},{32,16},{48,32},{64,48},{80,64},{96,80},{112,96},{128,112},... | collective-permute-start | bytes 491528 | tf_op jit(solution)/shard_map/ppermute | solution.py:21
  40.7 15.1 %collective-permute-start.10 = (f32[5,32,4,128]{3,1,2,0:T(8,128)}, f32[5,32,4,128]{3,1,2,0:T(8,128)}, u32[]{:S(2)}, u32[]{:S(2)}) collective-permute-start(f32[5,32,4,128]{3,1,2,0:T(8,128)} %get-tuple-element.89), channel_id=1, source_target_pairs={{0,2},{2,4},{4,6},{6,8},{8,10},{10,12},{12,14},{1,3},{3,5},{5,7},{... | collective-permute-start | bytes 983048 | tf_op jit(solution)/shard_map/ppermute | solution.py:19
  42.8 13.0 %collective-permute-start.11 = (f32[5,32,4,128]{3,1,2,0:T(8,128)S(1)}, f32[5,32,4,128]{3,1,2,0:T(8,128)}, u32[]{:S(2)}, u32[]{:S(2)}) collective-permute-start(f32[5,32,4,128]{3,1,2,0:T(8,128)S(1)} %get-tuple-element.90), channel_id=1, source_target_pairs={{2,0},{4,2},{6,4},{8,6},{10,8},{12,10},{14,12},{3,1},{5,3},{7,5},{... | collective-permute-start | bytes 983048 | tf_op jit(solution)/shard_map/ppermute | solution.py:21
  47.5 1.6 %copy-start.25 = (f32[136,128]{1,0:T(8,128)S(1)}, f32[136,128]{1,0:T(8,128)}, u32[]{:S(2)}) copy-start(f32[136,128]{1,0:T(8,128)} %get-tuple-element.48) | copy-start | bytes 208900
  49.1 4.4 %copy-start.28 = (f32[40,32]{0,1:T(8,128)S(1)}, f32[40,32]{0,1:T(8,128)}, u32[]{:S(2)}) copy-start(f32[40,32]{0,1:T(8,128)} %get-tuple-element.50) | copy-start | bytes 15364
  59.4 1.3 %copy-start.1 = (f32[5,32,16,128]{3,1,2,0:T(8,128)S(1)}, f32[5,32,16,128]{3,1,2,0:T(8,128)}, u32[]{:S(2)}) copy-start(f32[5,32,16,128]{3,1,2,0:T(8,128)} %copy.75) | copy-start | bytes 3932164
  62.6 5.6 %copy-start.12 = (f32[1,32,16,128]{3,1,2,0:T(8,128)}, f32[1,32,16,128]{3,1,2,0:T(8,128)S(1)}, u32[]{:S(2)}) copy-start(f32[1,32,16,128]{3,1,2,0:T(8,128)S(1)} %get-tuple-element.66) | copy-start | bytes 786436
  62.6 13.0 %copy-start.24 = (f32[1,32,16,128]{3,1,2,0:T(8,128)}, f32[1,32,16,128]{3,1,2,0:T(8,128)S(1)}, u32[]{:S(2)}) copy-start(f32[1,32,16,128]{3,1,2,0:T(8,128)S(1)} %get-tuple-element.67) | copy-start | bytes 786436
  64.0 1.5 %copy-start.21 = (f32[32,16,128]{2,0,1:T(8,128)S(1)}, f32[32,16,128]{2,0,1:T(8,128)}, u32[]{:S(2)}) copy-start(f32[32,16,128]{2,0,1:T(8,128)} %copy.88) | copy-start | bytes 786436
  65.5 10.1 %copy-start.19 = (f32[1,32,16,128]{3,1,2,0:T(8,128)}, f32[1,32,16,128]{3,1,2,0:T(8,128)S(1)}, u32[]{:S(2)}) copy-start(f32[1,32,16,128]{3,1,2,0:T(8,128)S(1)} %get-tuple-element.97) | copy-start | bytes 786436
  68.2 7.5 %copy-start.5 = (f32[3,32,16,128]{3,1,2,0:T(8,128)}, f32[3,32,16,128]{3,1,2,0:T(8,128)S(1)}, u32[]{:S(2)}) copy-start(f32[3,32,16,128]{3,1,2,0:T(8,128)S(1)} %get-tuple-element.110) | copy-start | bytes 2359300
  69.1 39.3 %collective-permute-start = (f32[5,4,16,128]{3,1,2,0:T(4,128)}, f32[5,4,16,128]{3,1,2,0:T(4,128)}, u32[]{:S(2)}, u32[]{:S(2)}) collective-permute-start(f32[5,4,16,128]{3,1,2,0:T(4,128)} %get-tuple-element.83), channel_id=1, source_target_pairs={{0,16},{16,32},{32,48},{48,64},{64,80},{80,96},{96,112},{112,128},... | collective-permute-start | bytes 491528 | tf_op jit(solution)/shard_map/ppermute | solution.py:19
  73.6 34.7 %collective-permute-start.1 = (f32[5,4,16,128]{3,1,2,0:T(4,128)}, f32[5,4,16,128]{3,1,2,0:T(4,128)}, u32[]{:S(2)}, u32[]{:S(2)}) collective-permute-start(f32[5,4,16,128]{3,1,2,0:T(4,128)} %get-tuple-element.84), channel_id=1, source_target_pairs={{16,0},{32,16},{48,32},{64,48},{80,64},{96,80},{112,96},{128,112},... | collective-permute-start | bytes 491528 | tf_op jit(solution)/shard_map/ppermute | solution.py:21
  82.0 13.2 %collective-permute-start.4 = (f32[5,32,16,8]{1,3,2,0:T(8,128)S(1)}, f32[5,32,16,8]{1,3,2,0:T(8,128)S(1)}, u32[]{:S(2)}, u32[]{:S(2)}) collective-permute-start(f32[5,32,16,8]{1,3,2,0:T(8,128)S(1)} %pad_maximum_fusion.6), channel_id=1, source_target_pairs={{0,1},{1,0},{2,3},{3,2},{4,5},{5,4},{6,7},{7,6},{8,9},{9,8},{10,11... | collective-permute-start | bytes 245768 | tf_op jit(solution)/shard_map/ppermute | solution.py:31
  88.5 16.1 %collective-permute-start.2 = (f32[5,32,4,128]{3,1,2,0:T(8,128)}, f32[5,32,4,128]{3,1,2,0:T(8,128)}, u32[]{:S(2)}, u32[]{:S(2)}) collective-permute-start(f32[5,32,4,128]{3,1,2,0:T(8,128)} %get-tuple-element.81), channel_id=1, source_target_pairs={{0,2},{2,4},{4,6},{6,8},{8,10},{10,12},{12,14},{1,3},{3,5},{5,7},{... | collective-permute-start | bytes 983048 | tf_op jit(solution)/shard_map/ppermute | solution.py:19
  90.5 14.1 %collective-permute-start.3 = (f32[5,32,4,128]{3,1,2,0:T(8,128)}, f32[5,32,4,128]{3,1,2,0:T(8,128)}, u32[]{:S(2)}, u32[]{:S(2)}) collective-permute-start(f32[5,32,4,128]{3,1,2,0:T(8,128)} %get-tuple-element.82), channel_id=1, source_target_pairs={{2,0},{4,2},{6,4},{8,6},{10,8},{12,10},{14,12},{3,1},{5,3},{7,5},{... | collective-permute-start | bytes 983048 | tf_op jit(solution)/shard_map/ppermute | solution.py:21
  95.9 4.2 %copy-start.6 = (f32[3,32,16,128]{3,1,2,0:T(8,128)S(1)}, f32[3,32,16,128]{3,1,2,0:T(8,128)}, u32[]{:S(2)}) copy-start(f32[3,32,16,128]{3,1,2,0:T(8,128)} %copy-done.5) | copy-start | bytes 2359300
  96.0 4.2 %copy-start.20 = (f32[1,32,16,128]{3,1,2,0:T(8,128)S(1)}, f32[1,32,16,128]{3,1,2,0:T(8,128)}, u32[]{:S(2)}) copy-start(f32[1,32,16,128]{3,1,2,0:T(8,128)} %copy-done.19) | copy-start | bytes 786436
  96.0 4.2 %copy-start.26 = (f32[136,128]{1,0:T(8,128)S(1)}, f32[136,128]{1,0:T(8,128)}, u32[]{:S(2)}) copy-start(f32[136,128]{1,0:T(8,128)} %get-tuple-element.49) | copy-start | bytes 208900
  96.0 4.2 %copy-start.36 = (f32[16]{0:T(128)S(1)}, f32[16]{0:T(128)}, u32[]{:S(2)}) copy-start(f32[16]{0:T(128)} %param.19) | copy-start | bytes 196
  100.2 4.5 %copy-start.14 = (f32[1,32,16,128]{3,1,2,0:T(8,128)S(1)}, f32[1,32,16,128]{3,1,2,0:T(8,128)}, u32[]{:S(2)}) copy-start(f32[1,32,16,128]{3,1,2,0:T(8,128)} %get-tuple-element.65) | copy-start | bytes 786436
  106.0 2.4 %copy-start.3 = (f32[5,32,16,128]{3,2,1,0:T(8,128)S(1)}, f32[5,32,16,128]{3,2,1,0:T(8,128)}, u32[]{:S(2)}) copy-start(f32[5,32,16,128]{3,2,1,0:T(8,128)} %param.13) | copy-start | bytes 3932164
  106.0 2.4 %copy-start.13 = (f32[1,32,16,128]{3,1,2,0:T(8,128)S(1)}, f32[1,32,16,128]{3,1,2,0:T(8,128)}, u32[]{:S(2)}) copy-start(f32[1,32,16,128]{3,1,2,0:T(8,128)} %copy-done.12) | copy-start | bytes 786436
  106.0 2.4 %copy-start.27 = (f32[40,32]{0,1:T(8,128)S(1)}, f32[40,32]{0,1:T(8,128)}, u32[]{:S(2)}) copy-start(f32[40,32]{0,1:T(8,128)} %get-tuple-element.53) | copy-start | bytes 15364
  108.4 12.0 %copy-start.4 = (f32[5,32,16,128]{3,1,2,0:T(8,128)S(1)}, f32[5,32,16,128]{3,1,2,0:T(8,128)}, u32[]{:S(2)}) copy-start(f32[5,32,16,128]{3,1,2,0:T(8,128)} %get-tuple-element.112) | copy-start | bytes 3932164
  108.4 12.0 %copy-start.7 = (f32[3,32,16,128]{3,1,2,0:T(8,128)S(1)}, f32[3,32,16,128]{3,1,2,0:T(8,128)}, u32[]{:S(2)}) copy-start(f32[3,32,16,128]{3,1,2,0:T(8,128)} %get-tuple-element.113) | copy-start | bytes 2359300
  108.4 12.0 %copy-start.8 = (f32[3,32,16,128]{3,1,2,0:T(8,128)S(1)}, f32[3,32,16,128]{3,1,2,0:T(8,128)}, u32[]{:S(2)}) copy-start(f32[3,32,16,128]{3,1,2,0:T(8,128)} %get-tuple-element.114) | copy-start | bytes 2359300
  108.4 12.0 %copy-start.9 = (f32[3,32,16,128]{3,1,2,0:T(8,128)S(1)}, f32[3,32,16,128]{3,1,2,0:T(8,128)}, u32[]{:S(2)}) copy-start(f32[3,32,16,128]{3,1,2,0:T(8,128)} %get-tuple-element.62) | copy-start | bytes 2359300
  108.4 12.0 %copy-start.10 = (f32[3,32,16,128]{3,1,2,0:T(8,128)S(1)}, f32[3,32,16,128]{3,1,2,0:T(8,128)}, u32[]{:S(2)}) copy-start(f32[3,32,16,128]{3,1,2,0:T(8,128)} %get-tuple-element.107) | copy-start | bytes 2359300
  108.4 12.0 %copy-start.11 = (f32[3,32,16,128]{3,1,2,0:T(8,128)S(1)}, f32[3,32,16,128]{3,1,2,0:T(8,128)}, u32[]{:S(2)}) copy-start(f32[3,32,16,128]{3,1,2,0:T(8,128)} %get-tuple-element.108) | copy-start | bytes 2359300
  108.5 12.0 %copy-start.15 = (f32[1,32,16,128]{3,1,2,0:T(8,128)S(1)}, f32[1,32,16,128]{3,1,2,0:T(8,128)}, u32[]{:S(2)}) copy-start(f32[1,32,16,128]{3,1,2,0:T(8,128)} %get-tuple-element.68) | copy-start | bytes 786436
  108.5 12.0 %copy-start.16 = (f32[1,32,16,128]{3,1,2,0:T(8,128)S(1)}, f32[1,32,16,128]{3,1,2,0:T(8,128)}, u32[]{:S(2)}) copy-start(f32[1,32,16,128]{3,1,2,0:T(8,128)} %get-tuple-element.70) | copy-start | bytes 786436
  108.5 12.0 %copy-start.17 = (f32[1,32,16,128]{3,1,2,0:T(8,128)S(1)}, f32[1,32,16,128]{3,1,2,0:T(8,128)}, u32[]{:S(2)}) copy-start(f32[1,32,16,128]{3,1,2,0:T(8,128)} %get-tuple-element.71) | copy-start | bytes 786436
  108.5 12.0 %copy-start.18 = (f32[1,32,16,128]{3,1,2,0:T(8,128)S(1)}, f32[1,32,16,128]{3,1,2,0:T(8,128)}, u32[]{:S(2)}) copy-start(f32[1,32,16,128]{3,1,2,0:T(8,128)} %get-tuple-element.73) | copy-start | bytes 786436
  108.5 12.0 %copy-start.22 = (f32[1,32,16,128]{3,1,2,0:T(8,128)S(1)}, f32[1,32,16,128]{3,1,2,0:T(8,128)}, u32[]{:S(2)}) copy-start(f32[1,32,16,128]{3,1,2,0:T(8,128)} %negate_bitcast_fusion) | copy-start | bytes 786436
  108.5 12.0 %copy-start.23 = (f32[1,32,16,128]{3,1,2,0:T(8,128)S(1)}, f32[1,32,16,128]{3,1,2,0:T(8,128)}, u32[]{:S(2)}) copy-start(f32[1,32,16,128]{3,1,2,0:T(8,128)} %get-tuple-element.64) | copy-start | bytes 786436
  111.9 11.3 %collective-permute-start.5 = (f32[5,4,16,128]{3,1,2,0:T(4,128)S(1)}, f32[5,4,16,128]{3,1,2,0:T(4,128)S(1)}, u32[]{:S(2)}, u32[]{:S(2)}) collective-permute-start(f32[5,4,16,128]{3,1,2,0:T(4,128)S(1)} %get-tuple-element.79), channel_id=1, source_target_pairs={{0,16},{16,32},{32,48},{48,64},{64,80},{80,96},{96,112},{112,128},... | collective-permute-start | bytes 491528 | tf_op jit(solution)/shard_map/ppermute | solution.py:19
  118.2 10.1 %collective-permute-start.6 = (f32[5,4,16,128]{3,1,2,0:T(4,128)S(1)}, f32[5,4,16,128]{3,1,2,0:T(4,128)S(1)}, u32[]{:S(2)}, u32[]{:S(2)}) collective-permute-start(f32[5,4,16,128]{3,1,2,0:T(4,128)S(1)} %get-tuple-element.80), channel_id=1, source_target_pairs={{16,0},{32,16},{48,32},{64,48},{80,64},{96,80},{112,96},{128,112},... | collective-permute-start | bytes 491528 | tf_op jit(solution)/shard_map/ppermute | solution.py:21
  (3 other events, 3.6 us)
where the time goes:
time: 132 us; the launch traced here: 131 us
  starting transfers between devices  44.2 us (33%)
  local copies, waits for them, and re-layouts  31.1 us (24%)
  matrix products  24.6 us (19%)
  other arithmetic  17.4 us (13%)
  waiting for transfers between devices  12.7 us (10%)
  between operations  1.38 us (1%)
    ppermute x6, starting transfers between devices, extended(): lax.ppermute(tail, axis, [(i, (i + 1) % count) for i in range(ends)])  24.3 us
    unnamed x82, local copies, waits for them, and re-layouts  16.5 us
    dot_general x4, matrix products, along_x(): return jnp.einsum('vard,ai->vird', ext, band, precision=highest)  11.1 us
    ppermute x6, starting transfers between devices, extended(): lax.ppermute(head, axis, [((i + 1) % count, i) for i in range(ends)])  10.7 us
    ppermute x2, starting transfers between devices, from_partner(): return lax.ppermute(value, axis, pairs)  9.22 us
    dot_general x2, matrix products, along_t(): return jnp.einsum('vxra,ai->vxri', ext, band, precision=highest)  8.77 us
    ppermute x6, waiting for transfers between devices, extended(): lax.ppermute(head, axis, [((i + 1) % count, i) for i in range(ends)])  7.8 us
    ppermute x2, waiting for transfers between devices, from_partner(): return lax.ppermute(value, axis, pairs)  4.9 us
  transfers between devices with their start and end apart: 14, of which 4 were waited for; matrix products, arithmetic and copies ran while one was open for 30% of the time, Pallas kernels for 0%

commit v1 on v0

v1 whole, which is shorter than its diff:
```python
import functools

import jax
import jax.numpy as jnp
from jax import lax
from jax.experimental import pallas as pl
from jax.experimental.pallas import tpu as pltpu
from jax.sharding import PartitionSpec as P

DT = 0.1
GAM = 0.4
W = 4
TAPS = 9
C = 5
NX, NR, NT = 32, 16, 128
F32 = jnp.float32
BF16 = jnp.bfloat16
VM = pl.BlockSpec(memory_space=pltpu.VMEM)
SM = pl.BlockSpec(memory_space=pltpu.SMEM)
ANY = pl.BlockSpec(memory_space=pl.ANY)


def prims(q):
    inv = 1.0 / q[0]
    u, v, w = q[1] * inv, q[2] * inv, q[3] * inv
    p = GAM * (q[4] - 0.5 * (q[1] * u + q[2] * v + q[3] * w))
    return inv, u, v, w, p, q[4] + p


def flux_x(q, pr):
    _, u, _, _, p, h = pr
    return [q[1], q[1] * u + p, q[2] * u, q[3] * u, h * u]


def flux_r(q, pr):
    _, _, v, _, p, h = pr
    return [q[2], q[1] * v, q[2] * v + p, q[3] * v, h * v]


def flux_t(q, pr):
    _, _, _, w, p, h = pr
    return [q[3], q[1] * w, q[2] * w, q[3] * w + p, h * w]


def pull(q, pr, a, b, c):
    inv, u, v, w, _, h = pr
    ub = a[1] * q[1] + a[2] * q[2] + a[3] * q[3] + a[4] * h
    vb = b[1] * q[1] + b[2] * q[2] + b[3] * q[3] + b[4] * h
    wb = c[1] * q[1] + c[2] * q[2] + c[3] * q[3] + c[4] * h
    hb = a[4] * u + b[4] * v + c[4] * w
    pb = a[1] + b[2] + c[3] + hb
    s = (-0.5 * GAM) * pb
    ub = (ub + s * q[1]) * inv
    vb = (vb + s * q[2]) * inv
    wb = (wb + s * q[3]) * inv
    o1 = a[0] + (a[1] + s) * u + b[1] * v + c[1] * w + ub
    o2 = b[0] + a[2] * u + (b[2] + s) * v + c[2] * w + vb
    o3 = c[0] + a[3] * u + b[3] * v + (c[3] + s) * w + wb
    o4 = hb + GAM * pb
    o0 = -(ub * u + vb * v + wb * w)
    return [o0, o1, o2, o3, o4]


def pull_x(q, pr, a):
    inv, u, v, w, _, h = pr
    hb = a[4] * u
    pb = a[1] + hb
    s = (-0.5 * GAM) * pb
    ub = (a[1] * q[1] + a[2] * q[2] + a[3] * q[3] + a[4] * h + s * q[1]) * inv
    vb = s * v
    wb = s * w
    o1 = a[0] + (a[1] + s) * u + ub
    o2 = a[2] * u + s * v + vb
    o3 = a[3] * u + s * w + wb
    o4 = hb + GAM * pb
    o0 = -(ub * u + vb * v + wb * w)
    return [o0, o1, o2, o3, o4]


def iota(shape, dim):
    return lax.broadcasted_iota(jnp.int32, shape, dim)


def metric_tile(met):
    row = iota((NR, NT), 0)
    tile = jnp.zeros((NR, NT), F32)
    for r in range(NR):
        tile = jnp.where(row == r, met[r], tile)
    return tile


def is_even(par):
    return jnp.full((NR, NT), par, jnp.int32) == 0


def split(x):
    hi = x.astype(BF16)
    return hi, (x - hi.astype(F32)).astype(BF16)


def band(coef):
    offset = iota((NT, NT), 0) - iota((NT, NT), 1) + W
    mat = jnp.zeros((NT, NT), F32)
    for j in range(TAPS):
        mat = jnp.where(offset == j, coef[j], mat)
    return mat


def t_own(hi, lo, coef, out):
    bhi, blo = split(band(coef))
    both = jnp.concatenate([bhi, blo], axis=1)
    step = 8
    for g in range(NX // step):
        h = hi[pl.ds(g * step, step)].reshape(step * C * NR, NT)
        l = lo[pl.ds(g * step, step)].reshape(step * C * NR, NT)
        first = jnp.dot(h, both, preferred_element_type=F32)
        second = jnp.dot(l, bhi, preferred_element_type=F32)
        total = first[:, :NT] + first[:, NT:] + second
        out[pl.ds(g * step, step)] = total.reshape(step, C, NR, NT)


def t_pack_coefs(coef):
    lane = iota((NR, NT), 1) % 8
    masks = {}
    for j in range(W):
        masks[j] = jnp.where((lane >= 4) & (lane < 8 - j), coef[j], 0.0)
    for j in range(W + 1, TAPS):
        masks[j] = jnp.where((lane >= 8 - j) & (lane < 4), coef[j], 0.0)
    return masks


def t_halo_packed(rims, masks):
    total = None
    for j, m in masks.items():
        term = m * pltpu.roll(rims, (4 - j) % NT, 1)
        total = term if total is None else total + term
    return total


def t_unpack(packed, k):
    lane = iota((NR, NT), 1)
    moved = pltpu.roll(packed, 124 - 8 * k, 1)
    return jnp.where((lane < 4) | (lane >= 124), moved, 0.0)


def t_pack_into(ref, fields, xx, k):
    lane = iota((NR, NT), 1)
    for c in range(C):
        moved = pltpu.roll(fields[c], 8 * k + 4, 1)
        ref[c, xx] = jnp.where(lane // 8 == k, moved, ref[c, xx])


def r_pack(first, second, even):
    sub = iota((8, NT), 0)
    low = jnp.where(sub < 4, first[:8], pltpu.roll(second[:8], 4, 0))
    high = jnp.where(sub < 4, pltpu.roll(first[8:], 4, 0), second[8:])
    ev = even[:8]
    return jnp.where(ev, high, low), jnp.where(ev, low, high)


def r_coefs(coef):
    sub = iota((8, NT), 0)
    low = [jnp.where(sub < 4 - j, coef[j], 0.0) for j in range(W)]
    high = {j: jnp.where(sub >= 12 - j, coef[j], 0.0) for j in range(W + 1, TAPS)}
    return low, high


def r_halo(low, high, xx, coefs):
    lo_c, hi_c = coefs
    top = None
    for j in range(W):
        shift = (8 - (4 * xx + j)) % 8
        term = lo_c[j] * (pltpu.roll(low, shift, 0) if shift else low)
        top = term if top is None else top + term
    bottom = None
    for j in range(W + 1, TAPS):
        shift = (12 - j - 4 * xx) % 8
        term = hi_c[j] * (pltpu.roll(high, shift, 0) if shift else high)
        bottom = term if bottom is None else bottom + term
    return jnp.concatenate([top, bottom], axis=0)


def x_taps(read, x, coef):
    total = None
    for j in range(TAPS):
        at = x + j - W
        if isinstance(x, int) and not 0 <= at < NX:
            continue
        term = coef[j] * read(at)
        total = term if total is None else total + term
    return total


def x_halo(planes, i, low, coef):
    total = None
    for j in range(TAPS):
        at = i + j if low else i + j - 8
        if not 0 <= at < W:
            continue
        term = coef[j] * planes[at]
        total = term if total is None else total + term
    return total


def over_planes(body):
    for x in range(W):
        body(x)

    def step(x, carry):
        body(x)
        return carry

    lax.fori_loop(W, NX - W, step, 0)
    for x in range(NX - W, NX):
        body(x)


def loop(lo, hi, body):
    def step(k, carry):
        body(k)
        return carry

    lax.fori_loop(lo, hi, step, 0)


def rims_x(par, state, seed, xe, xo):
    even = par[0] == 0
    first = jnp.where(even, NX - W, 0)
    second = jnp.where(even, 0, NX - W)
    for start, out in ((first, xe), (second, xo)):
        for i in range(W):
            q = [state[c, start + i] for c in range(C)]
            f = flux_x(q, prims(q))
            for c in range(C):
                out[c, i] = f[c]
                out[C + c, i] = seed[c, start + i]


def rims_rt(par, state, re, ro, th):
    even = is_even(par[1])
    th[...] = jnp.zeros(th.shape, F32)

    def pair(k):
        keep = []
        for xx in range(2):
            q = [state[c, 2 * k + xx] for c in range(C)]
            pr = prims(q)
            keep.append(flux_r(q, pr))
            t_pack_into(th, flux_t(q, pr), xx, k)
        for c in range(C):
            re[c, k], ro[c, k] = r_pack(keep[0][c], keep[1][c], even)

    loop(0, NX // 2, pair)


def own(cx, cr, ct, cf, met, state, seed, psec, plam, fx, fr, hi, lo, tt):
    mt = metric_tile(met)
    zero = jnp.zeros((8, NT), F32)

    def fill(x):
        q = [state[c, x] for c in range(C)]
        pr = prims(q)
        f, g, h = flux_x(q, pr), flux_r(q, pr), flux_t(q, pr)
        for c in range(C):
            fx[c, x] = f[c]
            fr[c, x, 0:8] = zero
            fr[c, x, 8:24] = g[c]
            fr[c, x, 24:32] = zero
            hi[x, c], lo[x, c] = split(h[c])

    loop(0, NX, fill)
    t_own(hi, lo, ct, tt)
    fc = [cf[TAPS - 1 - j] for j in range(TAPS)]
    xc = [cx[j] for j in range(TAPS)]

    def plane(x):
        for c in range(C):
            acc = x_taps(lambda at: fx[c, at], x, xc) + mt * tt[x, c]
            for j in range(TAPS):
                acc += cr[j] * fr[c, x, 4 + j : 20 + j]
            psec[c, x] = state[c, x] - DT * acc
            plam[c, x] = seed[c, x] - x_taps(lambda at: seed[c, at], x, fc)

    over_planes(plane)


def join(par, cx, cr, ct, cf, met, psec, plam, xe, xo, re, ro, th, sec, lam, xe2, xo2, re2, ro2, th2):
    mt = metric_tile(met)
    evx, evr = is_even(par[0]), is_even(par[1])
    fc = [cf[TAPS - 1 - j] for j in range(TAPS)]
    xc = [cx[j] for j in range(TAPS)]
    for low in (True, False):
        base = 0 if low else NX - W
        for c in range(2 * C):
            near, far = (xo, xe) if low else (xe, xo)
            planes = [jnp.where(evx, near[c, i], far[c, i]) for i in range(W)]
            for i in range(W):
                if c < C:
                    sec[c, base + i] = psec[c, base + i] - DT * x_halo(planes, i, low, xc)
                else:
                    lam[c - C, base + i] = plam[c - C, base + i] - x_halo(planes, i, low, fc)
    th2[...] = jnp.zeros(th2.shape, F32)
    rc = r_coefs(cr)
    tc = t_pack_coefs(ct)
    packed = [[mt * t_halo_packed(th[c, xx], tc) for xx in range(2)] for c in range(C)]
    ev8 = evr[:8]

    def pair(k, s_ref, l_ref):
        lams = [[], []]
        for c in range(C):
            a, b = re[c, k], ro[c, k]
            low, high = jnp.where(ev8, b, a), jnp.where(ev8, a, b)
            for xx in range(2):
                x = 2 * k + xx
                share = r_halo(low, high, xx, rc) + t_unpack(packed[c][xx], k)
                sec[c, x] = s_ref[c, x] - DT * share
                value = l_ref[c, x]
                lam[c, x] = value
                lams[xx].append(value)
        for c in range(C):
            re2[c, k], ro2[c, k] = r_pack(lams[0][c], lams[1][c], evr)
        for xx in range(2):
            t_pack_into(th2, [mt * v for v in lams[xx]], xx, k)

    loop(0, 2, functools.partial(pair, s_ref=sec, l_ref=lam))
    loop(2, 14, functools.partial(pair, s_ref=psec, l_ref=plam))
    loop(14, 16, functools.partial(pair, s_ref=sec, l_ref=lam))
    even = par[0] == 0
    first = jnp.where(even, NX - W, 0)
    second = jnp.where(even, 0, NX - W)
    for start, out in ((first, xe2), (second, xo2)):
        for i in range(W):
            for c in range(C):
                out[c, i] = sec[c, start + i]
                out[C + c, i] = lam[c, start + i]


def finish(par, cx, cr, ct, cf, met, state, sec, lam, re2, ro2, th2, new, adj, lr, hi, lo, tt):
    mt = metric_tile(met)
    evr = is_even(par[1])
    ev8 = evr[:8]
    rx = [-DT * cx[TAPS - 1 - j] for j in range(TAPS)]
    rr = [-DT * cr[TAPS - 1 - j] for j in range(TAPS)]
    rt = [-DT * ct[TAPS - 1 - j] for j in range(TAPS)]
    tc = t_pack_coefs(rt)
    packed = [[t_halo_packed(th2[c, xx], tc) for xx in range(2)] for c in range(C)]

    def fill(k):
        for c in range(C):
            a, b = re2[c, k], ro2[c, k]
            low, high = jnp.where(ev8, b, a), jnp.where(ev8, a, b)
            for xx in range(2):
                x = 2 * k + xx
                value = lam[c, x]
                lr[c, x, 0:8] = low if xx else pltpu.roll(low, 4, 0)
                lr[c, x, 8:24] = value
                lr[c, x, 24:32] = pltpu.roll(high, 4, 0) if xx else high
                hi[x, c], lo[x, c] = split(mt * value)

    loop(0, NX // 2, fill)
    t_own(hi, lo, rt, tt)

    def add(k):
        for c in range(C):
            for xx in range(2):
                tt[2 * k + xx, c] += t_unpack(packed[c][xx], k)

    loop(0, NX // 2, add)
    fcs = [cf[j] for j in range(TAPS)]

    def plane(x):
        q = [state[c, x] for c in range(C)]
        pr = prims(q)
        a, b, g = [], [], []
        for c in range(C):
            a.append(x_taps(lambda at: lam[c, at], x, rx))
            acc = None
            for j in range(TAPS):
                term = rr[j] * lr[c, x, 4 + j : 20 + j]
                acc = term if acc is None else acc + term
            b.append(acc)
            g.append(tt[x, c])
        out = pull(q, pr, a, b, g)
        for c in range(C):
            adj[c, x] = lam[c, x] + out[c]
            new[c, x] = sec[c, x] - x_taps(lambda at: sec[c, at], x, fcs)

    over_planes(plane)


def edges(par, cx, cf, state, xe2, xo2, nin, ain, nout, aout, nb, ab, sems):
    evx = is_even(par[0])
    rx = [-DT * cx[TAPS - 1 - j] for j in range(TAPS)]
    fcs = [cf[j] for j in range(TAPS)]
    starts = (0, NX - W)

    def moves(src, dst, buf, back, first):
        out = []
        for i, at in enumerate(starts):
            if back:
                out.append(pltpu.make_async_copy(buf.at[i], dst.at[:, pl.ds(at, W)], sems.at[first + i]))
            else:
                out.append(pltpu.make_async_copy(src.at[:, pl.ds(at, W)], buf.at[i], sems.at[first + i]))
        return out

    loads = moves(nin, None, nb, False, 0) + moves(ain, None, ab, False, 2)
    for m in loads:
        m.start()
    for m in loads:
        m.wait()
    for side, at in enumerate(starts):
        low = side == 0
        near, far = (xo2, xe2) if low else (xe2, xo2)
        for c in range(C):
            planes = [jnp.where(evx, near[c, i], far[c, i]) for i in range(W)]
            for i in range(W):
                nb[side, c, i] -= x_halo(planes, i, low, fcs)
        halos = [
            [jnp.where(evx, near[C + c, i], far[C + c, i]) for i in range(W)] for c in range(C)
        ]
        for i in range(W):
            q = [state[c, at + i] for c in range(C)]
            a = [x_halo(halos[c], i, low, rx) for c in range(C)]
            out = pull_x(q, prims(q), a)
            for c in range(C):
                ab[side, c, i] += out[c]
    stores = moves(None, nout, nb, True, 0) + moves(None, aout, ab, True, 2)
    for m in stores:
        m.start()
    for m in stores:
        m.wait()


def f32(*shape):
    return jax.ShapeDtypeStruct(shape, F32)


FULL = (C, NX, NR, NT)
XPAY = (2 * C, W, NR, NT)
RPAY = (C, NX // 2, 8, NT)
TPAY = (C, 2, NR, NT)


def call(kernel, ins, outs, scratch=(), out_specs=None, **kw):
    return pl.pallas_call(
        kernel,
        in_specs=ins,
        out_specs=out_specs or [VM] * len(outs),
        out_shape=[f32(*s) for s in outs],
        scratch_shapes=list(scratch),
        name=kernel.__name__,
        **kw,
    )


def swap(value, axis, odd):
    count = lax.axis_size(axis)
    pairs = []
    for i in range(odd, count - 1, 2):
        pairs += [(i, i + 1), (i + 1, i)]
    return lax.ppermute(value, axis, pairs)


def across(value):
    return lax.ppermute(value, "th", [(0, 1), (1, 0)])


SPLIT = [pltpu.VMEM((NX, C, NR, NT), BF16), pltpu.VMEM((NX, C, NR, NT), BF16), pltpu.VMEM((NX, C, NR, NT), F32)]
WIDE_R = pltpu.VMEM((C, NX, 32, NT), F32)


def shards(state, seed, cx, cr, ct, cf, met):
    par = jnp.stack([lax.axis_index("gx") % 2, lax.axis_index("row") % 2]).astype(jnp.int32)
    xe, xo = call(rims_x, [SM, VM, VM], [XPAY, XPAY])(par, state, seed)
    xe, xo = swap(xe, "gx", 0), swap(xo, "gx", 1)
    re, ro, th = call(rims_rt, [SM, VM], [RPAY, RPAY, TPAY])(par, state)
    re, ro, th = swap(re, "row", 0), swap(ro, "row", 1), across(th)
    psec, plam = call(
        own,
        [SM] * 5 + [VM] * 2,
        [FULL, FULL],
        [pltpu.VMEM(FULL, F32), WIDE_R] + SPLIT,
    )(cx, cr, ct, cf, met, state, seed)
    sec, lam, xe2, xo2, re2, ro2, th2 = call(
        join, [SM] * 6 + [VM] * 7, [FULL, FULL, XPAY, XPAY, RPAY, RPAY, TPAY]
    )(par, cx, cr, ct, cf, met, psec, plam, xe, xo, re, ro, th)
    xe2, xo2 = swap(xe2, "gx", 0), swap(xo2, "gx", 1)
    re2, ro2, th2 = swap(re2, "row", 0), swap(ro2, "row", 1), across(th2)
    new, adj = call(
        finish, [SM] * 6 + [VM] * 6, [FULL, FULL], [WIDE_R] + SPLIT
    )(par, cx, cr, ct, cf, met, state, sec, lam, re2, ro2, th2)
    rim = pltpu.VMEM((2, C, W, NR, NT), F32)
    new, adj = call(
        edges,
        [SM] * 3 + [VM] * 3 + [ANY] * 2,
        [FULL, FULL],
        [rim, rim, pltpu.SemaphoreType.DMA((4,))],
        out_specs=[ANY, ANY],
        input_output_aliases={6: 0, 7: 1},
    )(par, cx, cf, state, xe2, xo2, new, adj)
    return new, adj


def solution(mesh):
    whole = P(None, "gx", "row", "th")
    return jax.shard_map(
        shards,
        mesh=mesh,
        in_specs=(whole, whole, P(), P(), P(), P(), P("row")),
        out_specs=(whole, whole),
        check_vma=False,
    )
```

time: 132 us -> 82.8 us (0.63)
  the two profiles are of different devices: /device:TPU:232 before, /device:TPU:99 now
where the time goes in v1:
time: 82.8 us; the launch traced here: 82.3 us
  Pallas kernels  33.5 us (40%)
  starting transfers between devices  31.6 us (38%)
  waiting for transfers between devices  13 us (16%)
  local copies, waits for them, and re-layouts  2.72 us (3%)
  between operations  0.84 us (1%)
    ppermute x8, starting transfers between devices, swap(): return lax.ppermute(value, axis, pairs)  23.3 us
    ppermute x2, waiting for transfers between devices, across(): return lax.ppermute(value, 'th', [(0, 1), (1, 0)])  13 us
    pallas_call x1, Pallas kernels, shards(): call(finish, [SM] * 6 + [VM] * 6, [FULL, FULL], [WIDE_R] + SPLIT)  9.99 us
    ppermute x2, starting transfers between devices, across(): return lax.ppermute(value, 'th', [(0, 1), (1, 0)])  8.27 us
    pallas_call x1, Pallas kernels, shards(): call(own, [SM] * 5 + [VM] * 2, [FULL, FULL], [pltpu.VMEM(FULL, F32), WIDE...  7.55 us
    pallas_call x1, Pallas kernels, shards(): call(join, [SM] * 6 + [VM] * 7, [FULL, FULL, XPAY, XPAY, RPAY, RPAY, TPAY])  6.08 us
    pallas_call x1, Pallas kernels, shards(): re, ro, th = call(rims_rt, [SM, VM], [RPAY, RPAY, TPAY])(par, state)  3.67 us
    pallas_call x1, Pallas kernels, shards(): call(edges, [SM] * 3 + [VM] * 3 + [ANY] * 2, [FULL, FULL], [rim, rim, plt...  3.63 us
  transfers between devices with their start and end apart: 10, of which 1 were waited for; matrix products, arithmetic and copies ran while one was open for 0% of the time, Pallas kernels for 26%

profile of v1, /device:TPU:99, one launch (start us, length us, event | category | flops | bytes accessed | tf_op | source)
XLA Modules:
  0.0 82.3 jit_solution(2370723089702235225)
XLA Ops:
  0.6 0.6 pad_add_fusion.par
  1.2 2.6 %rims_x.1 = (f32[10,4,16,128]{3,2,1,0:T(8,128)}, f32[10,4,16,128]{3,2,1,0:T(8,128)}) custom-call(s32[2]{0:T(128)} %pad_add_fusion.par, f32[5,32,16,128]{3,2,1,0:T(8,128)} %state.9, f32[5,32,16,128]{3,2,1,0:T(8,128)} %seed.3), custom_call_target="tpu_custom_call" | custom-call | tf_op jit(solution)/shard_map/rims_x/pallas_call | solution.py:474
  3.8 3.2 %collective-permute-start = (f32[10,4,16,128]{3,2,1,0:T(8,128)}, f32[10,4,16,128]{3,2,1,0:T(8,128)S(1)}, u32[]{:S(2)}, u32[]{:S(2)}) collective-permute-start(f32[10,4,16,128]{3,2,1,0:T(8,128)} %get-tuple-element.20), channel_id=1, source_target_pairs={{0,16},{16,0},{32,48},{48,32},{64,80},{80,64},{96,112},{112,96},{1... | collective-permute-start | bytes 983048 | tf_op jit(solution)/shard_map/ppermute | solution.py:461
  7.0 1.9 %collective-permute-start.1 = (f32[10,4,16,128]{3,2,1,0:T(8,128)}, f32[10,4,16,128]{3,2,1,0:T(8,128)S(1)}, u32[]{:S(2)}, u32[]{:S(2)}) collective-permute-start(f32[10,4,16,128]{3,2,1,0:T(8,128)} %get-tuple-element.21), channel_id=1, source_target_pairs={{16,32},{32,16},{48,64},{64,48},{80,96},{96,80},{112,128},{128,112... | collective-permute-start | bytes 983048 | tf_op jit(solution)/shard_map/ppermute | solution.py:461
  8.9 3.7 %rims_rt.1 = (f32[5,16,8,128]{3,2,1,0:T(8,128)}, f32[5,16,8,128]{3,2,1,0:T(8,128)}, f32[5,2,16,128]{3,2,1,0:T(8,128)}) custom-call(s32[2]{0:T(128)} %pad_add_fusion.par, f32[5,32,16,128]{3,2,1,0:T(8,128)} %state.9), custom_call_target="tpu_custom_call" | custom-call | tf_op jit(solution)/shard_map/rims_rt/pallas_call | solution.py:476
  12.6 2.9 %collective-permute-start.2 = (f32[5,16,8,128]{3,2,1,0:T(8,128)}, f32[5,16,8,128]{3,2,1,0:T(8,128)S(1)}, u32[]{:S(2)}, u32[]{:S(2)}) collective-permute-start(f32[5,16,8,128]{3,2,1,0:T(8,128)} %get-tuple-element.22), channel_id=1, source_target_pairs={{0,2},{2,0},{4,6},{6,4},{8,10},{10,8},{12,14},{14,12},{1,3},{3,1},... | collective-permute-start | bytes 983048 | tf_op jit(solution)/shard_map/ppermute | solution.py:461
  15.5 3.0 %collective-permute-start.3 = (f32[5,16,8,128]{3,2,1,0:T(8,128)}, f32[5,16,8,128]{3,2,1,0:T(8,128)S(1)}, u32[]{:S(2)}, u32[]{:S(2)}) collective-permute-start(f32[5,16,8,128]{3,2,1,0:T(8,128)} %get-tuple-element.23), channel_id=1, source_target_pairs={{2,4},{4,2},{6,8},{8,6},{10,12},{12,10},{3,5},{5,3},{7,9},{9,7},{1... | collective-permute-start | bytes 983048 | tf_op jit(solution)/shard_map/ppermute | solution.py:461
  18.5 4.8 %collective-permute-start.4 = (f32[5,2,16,128]{3,2,1,0:T(8,128)}, f32[5,2,16,128]{3,2,1,0:T(8,128)S(1)}, u32[]{:S(2)}, u32[]{:S(2)}) collective-permute-start(f32[5,2,16,128]{3,2,1,0:T(8,128)} %get-tuple-element.24), channel_id=1, source_target_pairs={{0,1},{1,0},{2,3},{3,2},{4,5},{5,4},{6,7},{7,6},{8,9},{9,8},{10,11... | collective-permute-start | bytes 245768 | tf_op jit(solution)/shard_map/ppermute | solution.py:465
  23.3 7.5 %own.1 = (f32[5,32,16,128]{3,2,1,0:T(8,128)}, f32[5,32,16,128]{3,2,1,0:T(8,128)}) custom-call(f32[9]{0:T(128)} %cx.7, f32[9]{0:T(128)} %cr.5, f32[9]{0:T(128)} %ct.5, f32[9]{0:T(128)} %cf.7, f32[16]{0:T(128)} %met.5, f32[5,32,16,128]{3,2,1,0:T(8,128)} %state.9, f32[5,32,16,128]{3,2,1,0:T(8,128)} %seed.3), custom_call_target="tpu_custom_call" | custom-call | tf_op jit(solution)/shard_map/own/pallas_call | solution.py:478
  30.9 0.0 collective-permute-done.4.th
  30.9 0.0 copy-start.8
  30.9 0.0 collective-permute-done.xe
  30.9 0.0 copy-start
  30.9 0.0 collective-permute-done.1.xo
  30.9 0.0 copy-start.1
  30.9 0.0 collective-permute-done.2.re
  30.9 0.0 copy-start.2
  30.9 0.0 collective-permute-done.3.ro
  30.9 0.0 copy-start.3
  31.0 0.5 copy-done.8
  31.5 0.1 copy-done
  31.6 0.1 copy-done.1
  31.7 0.1 copy-done.2
  31.9 0.1 copy-done.3
  32.0 6.1 %join.1 = (f32[5,32,16,128]{3,2,1,0:T(8,128)}, f32[5,32,16,128]{3,2,1,0:T(8,128)}, f32[10,4,16,128]{3,2,1,0:T(8,128)}, f32[10,4,16,128]{3,2,1,0:T(8,128)}, f32[5...) custom-call(s32[2]{0:T(128)} %pad_add_fusion.par, f32[9]{0:T(128)} %cx.7, f32[9]{0:T(128)} %cr.5, ...), custom_call_target="tpu_custom_call" | custom-call | tf_op jit(solution)/shard_map/join/pallas_call | solution.py:484
  38.1 1.9 %collective-permute-start.7 = (f32[5,16,8,128]{3,2,1,0:T(8,128)}, f32[5,16,8,128]{3,2,1,0:T(8,128)S(1)}, u32[]{:S(2)}, u32[]{:S(2)}) collective-permute-start(f32[5,16,8,128]{3,2,1,0:T(8,128)} %get-tuple-element.29), channel_id=1, source_target_pairs={{0,2},{2,0},{4,6},{6,4},{8,10},{10,8},{12,14},{14,12},{1,3},{3,1},... | collective-permute-start | bytes 983048 | tf_op jit(solution)/shard_map/ppermute | solution.py:461
  40.0 3.2 %collective-permute-start.8 = (f32[5,16,8,128]{3,2,1,0:T(8,128)}, f32[5,16,8,128]{3,2,1,0:T(8,128)S(1)}, u32[]{:S(2)}, u32[]{:S(2)}) collective-permute-start(f32[5,16,8,128]{3,2,1,0:T(8,128)} %get-tuple-element.30), channel_id=1, source_target_pairs={{2,4},{4,2},{6,8},{8,6},{10,12},{12,10},{3,5},{5,3},{7,9},{9,7},{1... | collective-permute-start | bytes 983048 | tf_op jit(solution)/shard_map/ppermute | solution.py:461
  43.2 5.3 %collective-permute-start.5 = (f32[10,4,16,128]{3,2,1,0:T(8,128)}, f32[10,4,16,128]{3,2,1,0:T(8,128)S(1)}, u32[]{:S(2)}, u32[]{:S(2)}) collective-permute-start(f32[10,4,16,128]{3,2,1,0:T(8,128)} %get-tuple-element.25), channel_id=1, source_target_pairs={{0,16},{16,0},{32,48},{48,32},{64,80},{80,64},{96,112},{112,96},{1... | collective-permute-start | bytes 983048 | tf_op jit(solution)/shard_map/ppermute | solution.py:461
  48.5 1.9 %collective-permute-start.6 = (f32[10,4,16,128]{3,2,1,0:T(8,128)}, f32[10,4,16,128]{3,2,1,0:T(8,128)S(1)}, u32[]{:S(2)}, u32[]{:S(2)}) collective-permute-start(f32[10,4,16,128]{3,2,1,0:T(8,128)} %get-tuple-element.26), channel_id=1, source_target_pairs={{16,32},{32,16},{48,64},{64,48},{80,96},{96,80},{112,128},{128,112... | collective-permute-start | bytes 983048 | tf_op jit(solution)/shard_map/ppermute | solution.py:461
  50.5 3.5 %collective-permute-start.9 = (f32[5,2,16,128]{3,2,1,0:T(8,128)}, f32[5,2,16,128]{3,2,1,0:T(8,128)S(1)}, u32[]{:S(2)}, u32[]{:S(2)}) collective-permute-start(f32[5,2,16,128]{3,2,1,0:T(8,128)} %get-tuple-element.31), channel_id=1, source_target_pairs={{0,1},{1,0},{2,3},{3,2},{4,5},{5,4},{6,7},{7,6},{8,9},{9,8},{10,11... | collective-permute-start | bytes 245768 | tf_op jit(solution)/shard_map/ppermute | solution.py:465
  53.9 13.0 %collective-permute-done.9.th2 = f32[5,2,16,128]{3,2,1,0:T(8,128)S(1)} collective-permute-done((f32[5,2,16,128]{3,2,1,0:T(8,128)}, f32[5,2,16,128]{3,2,1,0:T(8,128)S(1)}, u32[]{:S(2)}, u32[]{:S(2)}) %collective-permute-start.9) | collective-permute-done | bytes 81952 | tf_op jit(solution)/shard_map/ppermute | solution.py:465
  66.9 0.0 copy-start.9
  66.9 0.0 collective-permute-done.7.re2
  66.9 0.0 copy-start.4
  66.9 0.0 collective-permute-done.8.ro2
  66.9 0.0 copy-start.5
  67.0 0.6 copy-done.9
  67.6 0.1 copy-done.4
  67.7 0.1 copy-done.5
  67.8 10.0 %finish.1 = (f32[5,32,16,128]{3,2,1,0:T(8,128)}, f32[5,32,16,128]{3,2,1,0:T(8,128)}) custom-call(s32[2]{0:T(128)} %pad_add_fusion.par, f32[9]{0:T(128)} %cx.7, f32[9]{0:T(128)} %cr.5, f32[9]{0:T(128)} %ct.5, f32[9]{0:T(128)} %cf.7, f32[16]{0:T(128)} %met.5, f32[5,32,16,128]{3,2,1,0:T(8,128)} %state.9, f32[5,32,16,128]{3,2,1,0:T(8,128)} %get-tuple-element.27.sec, ...), custom_call_target="tpu_custom_call" | custom-call | tf_op jit(solution)/shard_map/finish/pallas_call | solution.py:489
  77.8 0.0 collective-permute-done.5.xe2
  77.8 0.0 copy-start.6
  77.8 0.0 collective-permute-done.6.xo2
  77.8 0.0 copy-start.7
  77.8 0.7 copy-done.6
  78.5 0.1 copy-done.7
  78.7 3.6 %edges.1 = (f32[5,32,16,128]{3,2,1,0:T(8,128)}, f32[5,32,16,128]{3,2,1,0:T(8,128)}) custom-call(s32[2]{0:T(128)} %pad_add_fusion.par, f32[9]{0:T(128)} %cx.7, f32[9]{0:T(128)} %cf.7, f32[5,32,16,128]{3,2,1,0:T(8,128)} %state.9, f32[10,4,16,128]{3,2,1,0:T(8,128)} %copy-done.6, ...), custom_call_target="tpu_custom_call", output_to_operand_aliasing={{0}: (6, {}), {1}: (7, {})} | custom-call | tf_op jit(solution)/shard_map/edges/pallas_call | solution.py:493
Async XLA Ops:
  3.8 27.1 %collective-permute-start = (f32[10,4,16,128]{3,2,1,0:T(8,128)}, f32[10,4,16,128]{3,2,1,0:T(8,128)S(1)}, u32[]{:S(2)}, u32[]{:S(2)}) collective-permute-start(f32[10,4,16,128]{3,2,1,0:T(8,128)} %get-tuple-element.20), channel_id=1, source_target_pairs={{0,16},{16,0},{32,48},{48,32},{64,80},{80,64},{96,112},{112,96},{1... | collective-permute-start | bytes 983048 | tf_op jit(solution)/shard_map/ppermute | solution.py:461
  7.0 23.9 %collective-permute-start.1 = (f32[10,4,16,128]{3,2,1,0:T(8,128)}, f32[10,4,16,128]{3,2,1,0:T(8,128)S(1)}, u32[]{:S(2)}, u32[]{:S(2)}) collective-permute-start(f32[10,4,16,128]{3,2,1,0:T(8,128)} %get-tuple-element.21), channel_id=1, source_target_pairs={{16,32},{32,16},{48,64},{64,48},{80,96},{96,80},{112,128},{128,112... | collective-permute-start | bytes 983048 | tf_op jit(solution)/shard_map/ppermute | solution.py:461
  12.6 18.3 %collective-permute-start.2 = (f32[5,16,8,128]{3,2,1,0:T(8,128)}, f32[5,16,8,128]{3,2,1,0:T(8,128)S(1)}, u32[]{:S(2)}, u32[]{:S(2)}) collective-permute-start(f32[5,16,8,128]{3,2,1,0:T(8,128)} %get-tuple-element.22), channel_id=1, source_target_pairs={{0,2},{2,0},{4,6},{6,4},{8,10},{10,8},{12,14},{14,12},{1,3},{3,1},... | collective-permute-start | bytes 983048 | tf_op jit(solution)/shard_map/ppermute | solution.py:461
  15.5 15.5 %collective-permute-start.3 = (f32[5,16,8,128]{3,2,1,0:T(8,128)}, f32[5,16,8,128]{3,2,1,0:T(8,128)S(1)}, u32[]{:S(2)}, u32[]{:S(2)}) collective-permute-start(f32[5,16,8,128]{3,2,1,0:T(8,128)} %get-tuple-element.23), channel_id=1, source_target_pairs={{2,4},{4,2},{6,8},{8,6},{10,12},{12,10},{3,5},{5,3},{7,9},{9,7},{1... | collective-permute-start | bytes 983048 | tf_op jit(solution)/shard_map/ppermute | solution.py:461
  18.5 12.4 %collective-permute-start.4 = (f32[5,2,16,128]{3,2,1,0:T(8,128)}, f32[5,2,16,128]{3,2,1,0:T(8,128)S(1)}, u32[]{:S(2)}, u32[]{:S(2)}) collective-permute-start(f32[5,2,16,128]{3,2,1,0:T(8,128)} %get-tuple-element.24), channel_id=1, source_target_pairs={{0,1},{1,0},{2,3},{3,2},{4,5},{5,4},{6,7},{7,6},{8,9},{9,8},{10,11... | collective-permute-start | bytes 245768 | tf_op jit(solution)/shard_map/ppermute | solution.py:465
  30.9 0.6 copy-start.8
  30.9 0.7 copy-start
  30.9 0.8 %copy-start.1 = (f32[10,4,16,128]{3,2,1,0:T(8,128)}, f32[10,4,16,128]{3,2,1,0:T(8,128)S(1)}, u32[]{:S(2)}) copy-start(f32[10,4,16,128]{3,2,1,0:T(8,128)S(1)} %collective-permute-done.1.xo) | copy-start | bytes 983044
  30.9 0.9 %copy-start.2 = (f32[5,16,8,128]{3,2,1,0:T(8,128)}, f32[5,16,8,128]{3,2,1,0:T(8,128)S(1)}, u32[]{:S(2)}) copy-start(f32[5,16,8,128]{3,2,1,0:T(8,128)S(1)} %collective-permute-done.2.re) | copy-start | bytes 983044
  30.9 1.0 %copy-start.3 = (f32[5,16,8,128]{3,2,1,0:T(8,128)}, f32[5,16,8,128]{3,2,1,0:T(8,128)S(1)}, u32[]{:S(2)}) copy-start(f32[5,16,8,128]{3,2,1,0:T(8,128)S(1)} %collective-permute-done.3.ro) | copy-start | bytes 983044
  38.1 28.9 %collective-permute-start.7 = (f32[5,16,8,128]{3,2,1,0:T(8,128)}, f32[5,16,8,128]{3,2,1,0:T(8,128)S(1)}, u32[]{:S(2)}, u32[]{:S(2)}) collective-permute-start(f32[5,16,8,128]{3,2,1,0:T(8,128)} %get-tuple-element.29), channel_id=1, source_target_pairs={{0,2},{2,0},{4,6},{6,4},{8,10},{10,8},{12,14},{14,12},{1,3},{3,1},... | collective-permute-start | bytes 983048 | tf_op jit(solution)/shard_map/ppermute | solution.py:461
  40.0 27.0 %collective-permute-start.8 = (f32[5,16,8,128]{3,2,1,0:T(8,128)}, f32[5,16,8,128]{3,2,1,0:T(8,128)S(1)}, u32[]{:S(2)}, u32[]{:S(2)}) collective-permute-start(f32[5,16,8,128]{3,2,1,0:T(8,128)} %get-tuple-element.30), channel_id=1, source_target_pairs={{2,4},{4,2},{6,8},{8,6},{10,12},{12,10},{3,5},{5,3},{7,9},{9,7},{1... | collective-permute-start | bytes 983048 | tf_op jit(solution)/shard_map/ppermute | solution.py:461
  43.2 34.6 %collective-permute-start.5 = (f32[10,4,16,128]{3,2,1,0:T(8,128)}, f32[10,4,16,128]{3,2,1,0:T(8,128)S(1)}, u32[]{:S(2)}, u32[]{:S(2)}) collective-permute-start(f32[10,4,16,128]{3,2,1,0:T(8,128)} %get-tuple-element.25), channel_id=1, source_target_pairs={{0,16},{16,0},{32,48},{48,32},{64,80},{80,64},{96,112},{112,96},{1... | collective-permute-start | bytes 983048 | tf_op jit(solution)/shard_map/ppermute | solution.py:461
  48.5 29.3 %collective-permute-start.6 = (f32[10,4,16,128]{3,2,1,0:T(8,128)}, f32[10,4,16,128]{3,2,1,0:T(8,128)S(1)}, u32[]{:S(2)}, u32[]{:S(2)}) collective-permute-start(f32[10,4,16,128]{3,2,1,0:T(8,128)} %get-tuple-element.26), channel_id=1, source_target_pairs={{16,32},{32,16},{48,64},{64,48},{80,96},{96,80},{112,128},{128,112... | collective-permute-start | bytes 983048 | tf_op jit(solution)/shard_map/ppermute | solution.py:461
  50.5 16.5 %collective-permute-start.9 = (f32[5,2,16,128]{3,2,1,0:T(8,128)}, f32[5,2,16,128]{3,2,1,0:T(8,128)S(1)}, u32[]{:S(2)}, u32[]{:S(2)}) collective-permute-start(f32[5,2,16,128]{3,2,1,0:T(8,128)} %get-tuple-element.31), channel_id=1, source_target_pairs={{0,1},{1,0},{2,3},{3,2},{4,5},{5,4},{6,7},{7,6},{8,9},{9,8},{10,11... | collective-permute-start | bytes 245768 | tf_op jit(solution)/shard_map/ppermute | solution.py:465
  66.9 0.6 copy-start.9
  66.9 0.7 copy-start.4
  66.9 0.9 %copy-start.5 = (f32[5,16,8,128]{3,2,1,0:T(8,128)}, f32[5,16,8,128]{3,2,1,0:T(8,128)S(1)}, u32[]{:S(2)}) copy-start(f32[5,16,8,128]{3,2,1,0:T(8,128)S(1)} %collective-permute-done.8.ro2) | copy-start | bytes 983044
  77.8 0.7 copy-start.6
  77.8 0.8 %copy-start.7 = (f32[10,4,16,128]{3,2,1,0:T(8,128)}, f32[10,4,16,128]{3,2,1,0:T(8,128)S(1)}, u32[]{:S(2)}) copy-start(f32[10,4,16,128]{3,2,1,0:T(8,128)S(1)} %collective-permute-done.6.xo2) | copy-start | bytes 983044

commit v2 on v1

--- a/solution.py
+++ b/solution.py
@@ -6,6 +6,7 @@
 from jax.experimental import pallas as pl
 from jax.experimental.pallas import tpu as pltpu
 from jax.sharding import PartitionSpec as P
+
 
 DT = 0.1
 GAM = 0.4
@@ -89,8 +90,12 @@
     return tile
 
 
-def is_even(par):
-    return jnp.full((NR, NT), par, jnp.int32) == 0
+def parity(axis):
+    return lax.axis_index(axis) % 2
+
+
+def is_even(axis):
+    return jnp.full((NR, NT), parity(axis), jnp.int32) == 0
 
 
 def split(x):
@@ -223,8 +228,8 @@
     lax.fori_loop(lo, hi, step, 0)
 
 
-def rims_x(par, state, seed, xe, xo):
-    even = par[0] == 0
+def rims_x(state, seed, xe, xo):
+    even = parity("gx") == 0
     first = jnp.where(even, NX - W, 0)
     second = jnp.where(even, 0, NX - W)
     for start, out in ((first, xe), (second, xo)):
@@ -236,8 +241,8 @@
                 out[C + c, i] = seed[c, start + i]
 
 
-def rims_rt(par, state, re, ro, th):
-    even = is_even(par[1])
+def rims_rt(state, re, ro, th):
+    even = is_even("row")
     th[...] = jnp.zeros(th.shape, F32)
 
     def pair(k):
@@ -284,9 +289,9 @@
     over_planes(plane)
 
 
-def join(par, cx, cr, ct, cf, met, psec, plam, xe, xo, re, ro, th, sec, lam, xe2, xo2, re2, ro2, th2):
+def join(cx, cr, ct, cf, met, psec, plam, xe, xo, re, ro, th, sec, lam, xe2, xo2, re2, ro2, th2):
     mt = metric_tile(met)
-    evx, evr = is_even(par[0]), is_even(par[1])
+    evx, evr = is_even("gx"), is_even("row")
     fc = [cf[TAPS - 1 - j] for j in range(TAPS)]
     xc = [cx[j] for j in range(TAPS)]
     for low in (True, False):
@@ -325,7 +330,7 @@
     loop(0, 2, functools.partial(pair, s_ref=sec, l_ref=lam))
     loop(2, 14, functools.partial(pair, s_ref=psec, l_ref=plam))
     loop(14, 16, functools.partial(pair, s_ref=sec, l_ref=lam))
-    even = par[0] == 0
+    even = parity("gx") == 0
     first = jnp.where(even, NX - W, 0)
     second = jnp.where(even, 0, NX - W)
     for start, out in ((first, xe2), (second, xo2)):
@@ -335,9 +340,9 @@
                 out[C + c, i] = lam[c, start + i]
 
 
-def finish(par, cx, cr, ct, cf, met, state, sec, lam, re2, ro2, th2, new, adj, lr, hi, lo, tt):
+def finish(cx, cr, ct, cf, met, state, sec, lam, re2, ro2, th2, new, adj, nrim, arim, lr, hi, lo, tt, nb, ab, sems):
     mt = metric_tile(met)
-    evr = is_even(par[1])
+    evr = is_even("row")
     ev8 = evr[:8]
     rx = [-DT * cx[TAPS - 1 - j] for j in range(TAPS)]
     rr = [-DT * cr[TAPS - 1 - j] for j in range(TAPS)]
@@ -382,75 +387,85 @@
             g.append(tt[x, c])
         out = pull(q, pr, a, b, g)
         for c in range(C):
-            adj[c, x] = lam[c, x] + out[c]
-            new[c, x] = sec[c, x] - x_taps(lambda at: sec[c, at], x, fcs)
-
-    over_planes(plane)
-
-
-def edges(par, cx, cf, state, xe2, xo2, nin, ain, nout, aout, nb, ab, sems):
-    evx = is_even(par[0])
+            av = lam[c, x] + out[c]
+            nv = sec[c, x] - x_taps(lambda at: sec[c, at], x, fcs)
+            if isinstance(x, int):
+                side, at = (0, x) if x < W else (1, x - NX + W)
+                arim[side, c, at], nrim[side, c, at] = av, nv
+            else:
+                ab[c, x - W], nb[c, x - W] = av, nv
+
+    lax.fori_loop(W, NX - W, lambda x, carry: (plane(x), carry)[1], 0)
+    inside = pl.ds(W, NX - 2 * W)
+    moves = [
+        pltpu.make_async_copy(ab, adj.at[:, inside], sems.at[0]),
+        pltpu.make_async_copy(nb, new.at[:, inside], sems.at[1]),
+    ]
+    for move in moves:
+        move.start()
+    for x in (*range(W), *range(NX - W, NX)):
+        plane(x)
+    for move in moves:
+        move.wait()
+
+
+def edges(cx, cf, state, xe2, xo2, nrim, arim, nin, ain, nout, aout, nb, ab, sems):
+    evx = is_even("gx")
     rx = [-DT * cx[TAPS - 1 - j] for j in range(TAPS)]
     fcs = [cf[j] for j in range(TAPS)]
     starts = (0, NX - W)
-
-    def moves(src, dst, buf, back, first):
-        out = []
-        for i, at in enumerate(starts):
-            if back:
-                out.append(pltpu.make_async_copy(buf.at[i], dst.at[:, pl.ds(at, W)], sems.at[first + i]))
-            else:
-                out.append(pltpu.make_async_copy(src.at[:, pl.ds(at, W)], buf.at[i], sems.at[first + i]))
-        return out
-
-    loads = moves(nin, None, nb, False, 0) + moves(ain, None, ab, False, 2)
-    for m in loads:
-        m.start()
-    for m in loads:
-        m.wait()
+    moves = []
+
+    def put(buf, dst, side, slot):
+        move = pltpu.make_async_copy(
+            buf.at[side], dst.at[:, pl.ds(starts[side], W)], sems.at[slot + side]
+        )
+        move.start()
+        moves.append(move)
+
     for side, at in enumerate(starts):
         low = side == 0
-        near, far = (xo2, xe2) if low else (xe2, xo2)
-        for c in range(C):
-            planes = [jnp.where(evx, near[c, i], far[c, i]) for i in range(W)]
-            for i in range(W):
-                nb[side, c, i] -= x_halo(planes, i, low, fcs)
-        halos = [
-            [jnp.where(evx, near[C + c, i], far[C + c, i]) for i in range(W)] for c in range(C)
-        ]
+        mine, other = (xo2, xe2) if low else (xe2, xo2)
         for i in range(W):
             q = [state[c, at + i] for c in range(C)]
-            a = [x_halo(halos[c], i, low, rx) for c in range(C)]
+            a = []
+            for c in range(C):
+                planes = [jnp.where(evx, mine[C + c, h], other[C + c, h]) for h in range(W)]
+                a.append(x_halo(planes, i, low, rx))
             out = pull_x(q, prims(q), a)
             for c in range(C):
-                ab[side, c, i] += out[c]
-    stores = moves(None, nout, nb, True, 0) + moves(None, aout, ab, True, 2)
-    for m in stores:
-        m.start()
-    for m in stores:
-        m.wait()
-
-
-def f32(*shape):
-    return jax.ShapeDtypeStruct(shape, F32)
-
-
+                ab[side, c, i] = arim[side, c, i] + out[c]
+        put(ab, aout, side, 2)
+        for c in range(C):
+            planes = [jnp.where(evx, mine[c, i], other[c, i]) for i in range(W)]
+            for i in range(W):
+                nb[side, c, i] = nrim[side, c, i] - x_halo(planes, i, low, fcs)
+        put(nb, nout, side, 0)
+    for move in moves:
+        move.wait()
+
+
+def near(value):
+    return pltpu.with_memory_space_constraint(value, pltpu.VMEM)
+
+
+LIMIT = pltpu.CompilerParams(vmem_limit_bytes=24 << 20)
 FULL = (C, NX, NR, NT)
 XPAY = (2 * C, W, NR, NT)
 RPAY = (C, NX // 2, 8, NT)
 TPAY = (C, 2, NR, NT)
 
 
-def call(kernel, ins, outs, scratch=(), out_specs=None, **kw):
-    return pl.pallas_call(
+def call(kernel, smem, vmem, outs, scratch=()):
+    run = pl.pallas_call(
         kernel,
-        in_specs=ins,
-        out_specs=out_specs or [VM] * len(outs),
-        out_shape=[f32(*s) for s in outs],
+        in_specs=[SM] * len(smem) + [VM] * len(vmem),
+        out_specs=[VM] * len(outs),
+        out_shape=[pltpu.VMEM(s, F32) for s in outs],
         scratch_shapes=list(scratch),
-        name=kernel.__name__,
-        **kw,
+        compiler_params=LIMIT,
     )
+    return run(*smem, *[near(v) for v in vmem])
 
 
 def swap(value, axis, odd):
@@ -470,39 +485,55 @@
 
 
 def shards(state, seed, cx, cr, ct, cf, met):
-    par = jnp.stack([lax.axis_index("gx") % 2, lax.axis_index("row") % 2]).astype(jnp.int32)
-    xe, xo = call(rims_x, [SM, VM, VM], [XPAY, XPAY])(par, state, seed)
+    xe, xo = call(rims_x, [], [state, seed], [XPAY, XPAY])
     xe, xo = swap(xe, "gx", 0), swap(xo, "gx", 1)
-    re, ro, th = call(rims_rt, [SM, VM], [RPAY, RPAY, TPAY])(par, state)
+    re, ro, th = call(rims_rt, [], [state], [RPAY, RPAY, TPAY])
     re, ro, th = swap(re, "row", 0), swap(ro, "row", 1), across(th)
     psec, plam = call(
         own,
-        [SM] * 5 + [VM] * 2,
+        [cx, cr, ct, cf, met],
+        [state, seed],
         [FULL, FULL],
         [pltpu.VMEM(FULL, F32), WIDE_R] + SPLIT,
-    )(cx, cr, ct, cf, met, state, seed)
+    )
     sec, lam, xe2, xo2, re2, ro2, th2 = call(
-        join, [SM] * 6 + [VM] * 7, [FULL, FULL, XPAY, XPAY, RPAY, RPAY, TPAY]
-    )(par, cx, cr, ct, cf, met, psec, plam, xe, xo, re, ro, th)
-    xe2, xo2 = swap(xe2, "gx", 0), swap(xo2, "gx", 1)
-    re2, ro2, th2 = swap(re2, "row", 0), swap(ro2, "row", 1), across(th2)
-    new, adj = call(
-        finish, [SM] * 6 + [VM] * 6, [FULL, FULL], [WIDE_R] + SPLIT
-    )(par, cx, cr, ct, cf, met, state, sec, lam, re2, ro2, th2)
-    rim = pltpu.VMEM((2, C, W, NR, NT), F32)
-    new, adj = call(
+        join,
+        [cx, cr, ct, cf, met],
+        [psec, plam, xe, xo, re, ro, th],
+        [FULL, FULL, XPAY, XPAY, RPAY, RPAY, TPAY],
+    )
+    th2 = across(th2)
+    re2 = swap(re2, "row", 0)
+    ro2 = swap(ro2, "row", 1)
+    xe2 = swap(xe2, "gx", 0)
+    xo2 = swap(xo2, "gx", 1)
+    rim = (2, C, W, NR, NT)
+    inner = pltpu.VMEM((C, NX - 2 * W, NR, NT), F32)
+    whole = jax.ShapeDtypeStruct(FULL, F32)
+    new, adj, nrim, arim = pl.pallas_call(
+        finish,
+        in_specs=[SM] * 5 + [VM] * 6,
+        out_specs=[ANY, ANY, VM, VM],
+        out_shape=[whole, whole, pltpu.VMEM(rim, F32), pltpu.VMEM(rim, F32)],
+        scratch_shapes=[WIDE_R] + SPLIT + [inner, inner, pltpu.SemaphoreType.DMA((2,))],
+        name="finish",
+        compiler_params=LIMIT,
+    )(cx, cr, ct, cf, met, *map(near, (state, sec, lam, re2, ro2, th2)))
+    return pl.pallas_call(
         edges,
-        [SM] * 3 + [VM] * 3 + [ANY] * 2,
-        [FULL, FULL],
-        [rim, rim, pltpu.SemaphoreType.DMA((4,))],
+        in_specs=[SM] * 2 + [VM] * 5 + [ANY] * 2,
         out_specs=[ANY, ANY],
-        input_output_aliases={6: 0, 7: 1},
-    )(par, cx, cf, state, xe2, xo2, new, adj)
-    return new, adj
+        out_shape=[whole, whole],
+        scratch_shapes=[pltpu.VMEM(rim, F32), pltpu.VMEM(rim, F32), pltpu.SemaphoreType.DMA((4,))],
+        input_output_aliases={7: 0, 8: 1},
+        name="edges",
+        compiler_params=LIMIT,
+    )(cx, cf, *map(near, (state, xe2, xo2, nrim, arim)), new, adj)
 
 
 def solution(mesh):
     whole = P(None, "gx", "row", "th")
+
     return jax.shard_map(
         shards,
         mesh=mesh,

time: 82.8 us -> 67.4 us (0.81)
  Pallas kernels: 33.5 us -> 18.8 us
    pallas_call x6, Pallas kernels: 33.5 us -> 18.8 us  [the longest x4 9.61 us: call(): return run(*smem, *[near(v) for v in vmem])]
    unnamed x20 -> x18, local copies, waits for them, and re-layouts: 2.72 us -> 2.67 us
  transfers between devices with their start and end apart: 10 -> 10, of which waited for: 1 -> 1; matrix products, arithmetic and copies ran while one was open for 0% -> 0% of each run, Pallas kernels for 26% -> 22%
where the time goes in v2:
time: 67.4 us; the launch traced here: 67 us
  starting transfers between devices  31.8 us (47%)
  Pallas kernels  18.8 us (28%)
  waiting for transfers between devices  12.8 us (19%)
  local copies, waits for them, and re-layouts  2.67 us (4%)
  between operations  0.91 us (1%)
    ppermute x8, starting transfers between devices, swap(): return lax.ppermute(value, axis, pairs)  23.5 us
    ppermute x2, waiting for transfers between devices, across(): return lax.ppermute(value, 'th', [(0, 1), (1, 0)])  12.8 us
    pallas_call x4, Pallas kernels, call(): return run(*smem, *[near(v) for v in vmem])  9.61 us
    ppermute x2, starting transfers between devices, across(): return lax.ppermute(value, 'th', [(0, 1), (1, 0)])  8.27 us
    pallas_call x1, Pallas kernels, shards(): pl.pallas_call(finish, in_specs=[SM] * 5 + [VM] * 6, out_specs=[ANY, ANY,...  7.64 us
    unnamed x18, local copies, waits for them, and re-layouts  2.67 us
    pallas_call x1, Pallas kernels, shards(): pl.pallas_call(edges, in_specs=[SM] * 2 + [VM] * 5 + [ANY] * 2, out_specs...  1.55 us
  transfers between devices with their start and end apart: 10, of which 1 were waited for; matrix products, arithmetic and copies ran while one was open for 0% of the time, Pallas kernels for 22%

profile of v2, /device:TPU:99, one launch (start us, length us, event | category | flops | bytes accessed | tf_op | source)
XLA Modules:
  0.0 67.0 jit_solution(3907929605573843400)
XLA Ops:
  0.6 0.0 copy-start
  0.6 1.3 %copy-done = f32[5,32,16,128]{3,2,1,0:T(8,128)S(1)} copy-done((f32[5,32,16,128]{3,2,1,0:T(8,128)S(1)}, f32[5,32,16,128]{3,2,1,0:T(8,128)}, u32[]{:S(2)}) %copy-start) | copy-done | bytes 1310744
  1.9 0.0 copy-start.2
  2.0 1.3 %copy-done.2 = f32[5,32,16,128]{3,2,1,0:T(8,128)S(1)} copy-done((f32[5,32,16,128]{3,2,1,0:T(8,128)S(1)}, f32[5,32,16,128]{3,2,1,0:T(8,128)}, u32[]{:S(2)}) %copy-start.2) | copy-done | bytes 1310744
  3.3 0.0 copy-start.3
  3.3 0.1 shard_map.87
  3.3 0.0 copy-start.1
  3.3 0.0 copy-start.4
  3.4 0.0 copy-start.5
  3.4 0.0 copy-start.6
  3.4 0.0 copy-start.7
  3.4 0.0 copy-start.8
  3.4 3.3 %collective-permute-start = (f32[10,4,16,128]{3,2,1,0:T(8,128)S(1)}, f32[10,4,16,128]{3,2,1,0:T(8,128)S(1)}, u32[]{:S(2)}, u32[]{:S(2)}) collective-permute-start(f32[10,4,16,128]{3,2,1,0:T(8,128)S(1)} %get-tuple-element.22), channel_id=1, source_target_pairs={{0,16},{16,0},{32,48},{48,32},{64,80},{80,64},{96,112},{112,96},{1... | collective-permute-start | bytes 983048 | tf_op jit(solution)/shard_map/ppermute | solution.py:476
  6.7 1.9 %collective-permute-start.1 = (f32[10,4,16,128]{3,2,1,0:T(8,128)S(1)}, f32[10,4,16,128]{3,2,1,0:T(8,128)S(1)}, u32[]{:S(2)}, u32[]{:S(2)}) collective-permute-start(f32[10,4,16,128]{3,2,1,0:T(8,128)S(1)} %get-tuple-element.23), channel_id=1, source_target_pairs={{16,32},{32,16},{48,64},{64,48},{80,96},{96,80},{112,128},{128,112... | collective-permute-start | bytes 983048 | tf_op jit(solution)/shard_map/ppermute | solution.py:476
  8.7 1.5 %shard_map.88 = (f32[5,16,8,128]{3,2,1,0:T(8,128)S(1)}, f32[5,16,8,128]{3,2,1,0:T(8,128)S(1)}, f32[5,2,16,128]{3,2,1,0:T(8,128)S(1)}) custom-call(f32[5,32,16,128]{3,2,1,0:T(8,128)S(1)} %copy-done), custom_call_target="tpu_custom_call" | custom-call | tf_op jit(solution)/shard_map/pallas_call | solution.py:468
  10.2 2.9 %collective-permute-start.2 = (f32[5,16,8,128]{3,2,1,0:T(8,128)S(1)}, f32[5,16,8,128]{3,2,1,0:T(8,128)S(1)}, u32[]{:S(2)}, u32[]{:S(2)}) collective-permute-start(f32[5,16,8,128]{3,2,1,0:T(8,128)S(1)} %get-tuple-element.24), channel_id=1, source_target_pairs={{0,2},{2,0},{4,6},{6,4},{8,10},{10,8},{12,14},{14,12},{1,3},{3,1},... | collective-permute-start | bytes 983048 | tf_op jit(solution)/shard_map/ppermute | solution.py:476
  13.1 3.0 %collective-permute-start.3 = (f32[5,16,8,128]{3,2,1,0:T(8,128)S(1)}, f32[5,16,8,128]{3,2,1,0:T(8,128)S(1)}, u32[]{:S(2)}, u32[]{:S(2)}) collective-permute-start(f32[5,16,8,128]{3,2,1,0:T(8,128)S(1)} %get-tuple-element.25), channel_id=1, source_target_pairs={{2,4},{4,2},{6,8},{8,6},{10,12},{12,10},{3,5},{5,3},{7,9},{9,7},{1... | collective-permute-start | bytes 983048 | tf_op jit(solution)/shard_map/ppermute | solution.py:476
  16.1 4.8 %collective-permute-start.4 = (f32[5,2,16,128]{3,2,1,0:T(8,128)S(1)}, f32[5,2,16,128]{3,2,1,0:T(8,128)S(1)}, u32[]{:S(2)}, u32[]{:S(2)}) collective-permute-start(f32[5,2,16,128]{3,2,1,0:T(8,128)S(1)} %get-tuple-element.26), channel_id=1, source_target_pairs={{0,1},{1,0},{2,3},{3,2},{4,5},{5,4},{6,7},{7,6},{8,9},{9,8},{10,11... | collective-permute-start | bytes 245768 | tf_op jit(solution)/shard_map/ppermute | solution.py:480
  20.9 0.0 copy-done.3
  20.9 0.0 copy-done.1
  21.0 0.0 copy-done.4
  21.0 0.0 copy-done.5
  21.0 0.0 copy-done.6
  21.0 0.0 copy-done.7
  21.0 0.0 copy-done.8
  21.0 5.3 %shard_map.86 = (f32[5,32,16,128]{3,2,1,0:T(8,128)S(1)}, f32[5,32,16,128]{3,2,1,0:T(8,128)S(1)}) custom-call(f32[9]{0:T(128)S(1)} %copy-done.4, f32[9]{0:T(128)S(1)} %copy-done.6, f32[9]{0:T(128)S(1)} %copy-done.7, f32[9]{0:T(128)S(1)} %copy-done.5, f32[16]{0:T(128)S(1)} %copy-done.8, f32[5,32,16,128]{3,2,1,0:T(8,128)S(1)} %copy-done.1, ...), custom_call_target="tpu_custom_call" | custom-call | tf_op jit(solution)/shard_map/pallas_call | solution.py:468
  26.3 0.0 collective-permute-done.4.th
  26.3 0.0 collective-permute-done.xe
  26.3 0.0 collective-permute-done.1.xo
  26.3 0.0 collective-permute-done.2.re
  26.3 0.0 collective-permute-done.3.ro
  26.3 2.7 %shard_map.89 = (f32[5,32,16,128]{3,2,1,0:T(8,128)S(1)}, f32[5,32,16,128]{3,2,1,0:T(8,128)S(1)}, f32[10,4,16,128]{3,2,1,0:T(8,128)S(1)}, f32[10,4,16,128]{3,2,1,...) custom-call(f32[9]{0:T(128)S(1)} %copy-done.4, ...), custom_call_target="tpu_custom_call" | custom-call | tf_op jit(solution)/shard_map/pallas_call | solution.py:468
  29.1 2.4 %collective-permute-start.7 = (f32[5,16,8,128]{3,2,1,0:T(8,128)S(1)}, f32[5,16,8,128]{3,2,1,0:T(8,128)S(1)}, u32[]{:S(2)}, u32[]{:S(2)}) collective-permute-start(f32[5,16,8,128]{3,2,1,0:T(8,128)S(1)} %get-tuple-element.31), channel_id=1, source_target_pairs={{0,2},{2,0},{4,6},{6,4},{8,10},{10,8},{12,14},{14,12},{1,3},{3,1},... | collective-permute-start | bytes 983048 | tf_op jit(solution)/shard_map/ppermute | solution.py:476
  31.5 3.0 %collective-permute-start.8 = (f32[5,16,8,128]{3,2,1,0:T(8,128)S(1)}, f32[5,16,8,128]{3,2,1,0:T(8,128)S(1)}, u32[]{:S(2)}, u32[]{:S(2)}) collective-permute-start(f32[5,16,8,128]{3,2,1,0:T(8,128)S(1)} %get-tuple-element.32), channel_id=1, source_target_pairs={{2,4},{4,2},{6,8},{8,6},{10,12},{12,10},{3,5},{5,3},{7,9},{9,7},{1... | collective-permute-start | bytes 983048 | tf_op jit(solution)/shard_map/ppermute | solution.py:476
  34.5 5.1 %collective-permute-start.5 = (f32[10,4,16,128]{3,2,1,0:T(8,128)S(1)}, f32[10,4,16,128]{3,2,1,0:T(8,128)S(1)}, u32[]{:S(2)}, u32[]{:S(2)}) collective-permute-start(f32[10,4,16,128]{3,2,1,0:T(8,128)S(1)} %get-tuple-element.27), channel_id=1, source_target_pairs={{0,16},{16,0},{32,48},{48,32},{64,80},{80,64},{96,112},{112,96},{1... | collective-permute-start | bytes 983048 | tf_op jit(solution)/shard_map/ppermute | solution.py:476
  39.6 1.9 %collective-permute-start.6 = (f32[10,4,16,128]{3,2,1,0:T(8,128)S(1)}, f32[10,4,16,128]{3,2,1,0:T(8,128)S(1)}, u32[]{:S(2)}, u32[]{:S(2)}) collective-permute-start(f32[10,4,16,128]{3,2,1,0:T(8,128)S(1)} %get-tuple-element.28), channel_id=1, source_target_pairs={{16,32},{32,16},{48,64},{64,48},{80,96},{96,80},{112,128},{128,112... | collective-permute-start | bytes 983048 | tf_op jit(solution)/shard_map/ppermute | solution.py:476
  41.5 3.5 %collective-permute-start.9 = (f32[5,2,16,128]{3,2,1,0:T(8,128)S(1)}, f32[5,2,16,128]{3,2,1,0:T(8,128)S(1)}, u32[]{:S(2)}, u32[]{:S(2)}) collective-permute-start(f32[5,2,16,128]{3,2,1,0:T(8,128)S(1)} %get-tuple-element.33), channel_id=1, source_target_pairs={{0,1},{1,0},{2,3},{3,2},{4,5},{5,4},{6,7},{7,6},{8,9},{9,8},{10,11... | collective-permute-start | bytes 245768 | tf_op jit(solution)/shard_map/ppermute | solution.py:480
  45.0 12.8 %collective-permute-done.9.th2 = f32[5,2,16,128]{3,2,1,0:T(8,128)S(1)} collective-permute-done((f32[5,2,16,128]{3,2,1,0:T(8,128)S(1)}, f32[5,2,16,128]{3,2,1,0:T(8,128)S(1)}, u32[]{:S(2)}, u32[]{:S(2)}) %collective-permute-start.9) | collective-permute-done | bytes 81952 | tf_op jit(solution)/shard_map/ppermute | solution.py:480
  57.7 0.0 collective-permute-done.7.re2
  57.8 0.0 collective-permute-done.8.ro2
  57.8 7.6 %finish.1 = (f32[5,32,16,128]{3,2,1,0:T(8,128)}, f32[5,32,16,128]{3,2,1,0:T(8,128)}, f32[2,5,4,16,128]{4,3,2,1,0:T(8,128)S(1)}, f32[2,5,4,16,128]{4,3,2,1,0:T(8,128)S(1)}) custom-call(f32[9]{0:T(128)S(1)} %copy-done.4, f32[9]{0:T(128)S(1)} %copy-done.6, f32[9]{0:T(128)S(1)} %copy-done.7, f32[9]{0:T(128)S(1)} %copy-done.5, f32[16]{0:T(128)S(1)} %copy-done.8, ...), custom_call_target="tpu_custom_call" | custom-call | tf_op jit(solution)/shard_map/finish/pallas_call | solution.py:513
  65.4 0.0 collective-permute-done.5.xe2
  65.4 0.0 collective-permute-done.6.xo2
  65.4 1.5 %edges.1 = (f32[5,32,16,128]{3,2,1,0:T(8,128)}, f32[5,32,16,128]{3,2,1,0:T(8,128)}) custom-call(f32[9]{0:T(128)S(1)} %copy-done.4, f32[9]{0:T(128)S(1)} %copy-done.5, f32[5,32,16,128]{3,2,1,0:T(8,128)S(1)} %copy-done.1, f32[10,4,16,128]{3,2,1,0:T(8,128)S(1)} %collective-permute-done.5.xe2, ...), custom_call_target="tpu_custom_call", output_to_operand_aliasing={{0}: (7, {}), {1}: (8, {})} | custom-call | tf_op jit(solution)/shard_map/edges/pallas_call | solution.py:522
Async XLA Ops:
  0.6 1.3 %copy-start = (f32[5,32,16,128]{3,2,1,0:T(8,128)S(1)}, f32[5,32,16,128]{3,2,1,0:T(8,128)}, u32[]{:S(2)}) copy-start(f32[5,32,16,128]{3,2,1,0:T(8,128)} %state.9) | copy-start | bytes 3932164
  1.9 1.3 %copy-start.2 = (f32[5,32,16,128]{3,2,1,0:T(8,128)S(1)}, f32[5,32,16,128]{3,2,1,0:T(8,128)}, u32[]{:S(2)}) copy-start(f32[5,32,16,128]{3,2,1,0:T(8,128)} %seed.3) | copy-start | bytes 3932164
  3.3 17.7 %copy-start.3 = (f32[5,32,16,128]{3,2,1,0:T(8,128)S(1)}, f32[5,32,16,128]{3,2,1,0:T(8,128)}, u32[]{:S(2)}) copy-start(f32[5,32,16,128]{3,2,1,0:T(8,128)} %seed.3) | copy-start | bytes 3932164
  3.3 17.6 %copy-start.1 = (f32[5,32,16,128]{3,2,1,0:T(8,128)S(1)}, f32[5,32,16,128]{3,2,1,0:T(8,128)}, u32[]{:S(2)}) copy-start(f32[5,32,16,128]{3,2,1,0:T(8,128)} %state.9) | copy-start | bytes 3932164
  3.3 17.6 %copy-start.4 = (f32[9]{0:T(128)S(1)}, f32[9]{0:T(128)}, u32[]{:S(2)}) copy-start(f32[9]{0:T(128)} %cx.7) | copy-start | bytes 112
  3.4 17.6 %copy-start.5 = (f32[9]{0:T(128)S(1)}, f32[9]{0:T(128)}, u32[]{:S(2)}) copy-start(f32[9]{0:T(128)} %cf.7) | copy-start | bytes 112
  3.4 17.6 %copy-start.6 = (f32[9]{0:T(128)S(1)}, f32[9]{0:T(128)}, u32[]{:S(2)}) copy-start(f32[9]{0:T(128)} %cr.5) | copy-start | bytes 112
  3.4 17.6 %copy-start.7 = (f32[9]{0:T(128)S(1)}, f32[9]{0:T(128)}, u32[]{:S(2)}) copy-start(f32[9]{0:T(128)} %ct.5) | copy-start | bytes 112
  3.4 17.6 %copy-start.8 = (f32[16]{0:T(128)S(1)}, f32[16]{0:T(128)}, u32[]{:S(2)}) copy-start(f32[16]{0:T(128)} %met.5) | copy-start | bytes 196
  3.4 22.9 %collective-permute-start = (f32[10,4,16,128]{3,2,1,0:T(8,128)S(1)}, f32[10,4,16,128]{3,2,1,0:T(8,128)S(1)}, u32[]{:S(2)}, u32[]{:S(2)}) collective-permute-start(f32[10,4,16,128]{3,2,1,0:T(8,128)S(1)} %get-tuple-element.22), channel_id=1, source_target_pairs={{0,16},{16,0},{32,48},{48,32},{64,80},{80,64},{96,112},{112,96},{1... | collective-permute-start | bytes 983048 | tf_op jit(solution)/shard_map/ppermute | solution.py:476
  6.7 19.6 %collective-permute-start.1 = (f32[10,4,16,128]{3,2,1,0:T(8,128)S(1)}, f32[10,4,16,128]{3,2,1,0:T(8,128)S(1)}, u32[]{:S(2)}, u32[]{:S(2)}) collective-permute-start(f32[10,4,16,128]{3,2,1,0:T(8,128)S(1)} %get-tuple-element.23), channel_id=1, source_target_pairs={{16,32},{32,16},{48,64},{64,48},{80,96},{96,80},{112,128},{128,112... | collective-permute-start | bytes 983048 | tf_op jit(solution)/shard_map/ppermute | solution.py:476
  10.2 16.1 %collective-permute-start.2 = (f32[5,16,8,128]{3,2,1,0:T(8,128)S(1)}, f32[5,16,8,128]{3,2,1,0:T(8,128)S(1)}, u32[]{:S(2)}, u32[]{:S(2)}) collective-permute-start(f32[5,16,8,128]{3,2,1,0:T(8,128)S(1)} %get-tuple-element.24), channel_id=1, source_target_pairs={{0,2},{2,0},{4,6},{6,4},{8,10},{10,8},{12,14},{14,12},{1,3},{3,1},... | collective-permute-start | bytes 983048 | tf_op jit(solution)/shard_map/ppermute | solution.py:476
  13.1 13.2 %collective-permute-start.3 = (f32[5,16,8,128]{3,2,1,0:T(8,128)S(1)}, f32[5,16,8,128]{3,2,1,0:T(8,128)S(1)}, u32[]{:S(2)}, u32[]{:S(2)}) collective-permute-start(f32[5,16,8,128]{3,2,1,0:T(8,128)S(1)} %get-tuple-element.25), channel_id=1, source_target_pairs={{2,4},{4,2},{6,8},{8,6},{10,12},{12,10},{3,5},{5,3},{7,9},{9,7},{1... | collective-permute-start | bytes 983048 | tf_op jit(solution)/shard_map/ppermute | solution.py:476
  16.1 10.2 %collective-permute-start.4 = (f32[5,2,16,128]{3,2,1,0:T(8,128)S(1)}, f32[5,2,16,128]{3,2,1,0:T(8,128)S(1)}, u32[]{:S(2)}, u32[]{:S(2)}) collective-permute-start(f32[5,2,16,128]{3,2,1,0:T(8,128)S(1)} %get-tuple-element.26), channel_id=1, source_target_pairs={{0,1},{1,0},{2,3},{3,2},{4,5},{5,4},{6,7},{7,6},{8,9},{9,8},{10,11... | collective-permute-start | bytes 245768 | tf_op jit(solution)/shard_map/ppermute | solution.py:480
  29.1 28.7 %collective-permute-start.7 = (f32[5,16,8,128]{3,2,1,0:T(8,128)S(1)}, f32[5,16,8,128]{3,2,1,0:T(8,128)S(1)}, u32[]{:S(2)}, u32[]{:S(2)}) collective-permute-start(f32[5,16,8,128]{3,2,1,0:T(8,128)S(1)} %get-tuple-element.31), channel_id=1, source_target_pairs={{0,2},{2,0},{4,6},{6,4},{8,10},{10,8},{12,14},{14,12},{1,3},{3,1},... | collective-permute-start | bytes 983048 | tf_op jit(solution)/shard_map/ppermute | solution.py:476
  31.5 26.3 %collective-permute-start.8 = (f32[5,16,8,128]{3,2,1,0:T(8,128)S(1)}, f32[5,16,8,128]{3,2,1,0:T(8,128)S(1)}, u32[]{:S(2)}, u32[]{:S(2)}) collective-permute-start(f32[5,16,8,128]{3,2,1,0:T(8,128)S(1)} %get-tuple-element.32), channel_id=1, source_target_pairs={{2,4},{4,2},{6,8},{8,6},{10,12},{12,10},{3,5},{5,3},{7,9},{9,7},{1... | collective-permute-start | bytes 983048 | tf_op jit(solution)/shard_map/ppermute | solution.py:476
  34.5 30.9 %collective-permute-start.5 = (f32[10,4,16,128]{3,2,1,0:T(8,128)S(1)}, f32[10,4,16,128]{3,2,1,0:T(8,128)S(1)}, u32[]{:S(2)}, u32[]{:S(2)}) collective-permute-start(f32[10,4,16,128]{3,2,1,0:T(8,128)S(1)} %get-tuple-element.27), channel_id=1, source_target_pairs={{0,16},{16,0},{32,48},{48,32},{64,80},{80,64},{96,112},{112,96},{1... | collective-permute-start | bytes 983048 | tf_op jit(solution)/shard_map/ppermute | solution.py:476
  39.6 25.9 %collective-permute-start.6 = (f32[10,4,16,128]{3,2,1,0:T(8,128)S(1)}, f32[10,4,16,128]{3,2,1,0:T(8,128)S(1)}, u32[]{:S(2)}, u32[]{:S(2)}) collective-permute-start(f32[10,4,16,128]{3,2,1,0:T(8,128)S(1)} %get-tuple-element.28), channel_id=1, source_target_pairs={{16,32},{32,16},{48,64},{64,48},{80,96},{96,80},{112,128},{128,112... | collective-permute-start | bytes 983048 | tf_op jit(solution)/shard_map/ppermute | solution.py:476
  41.5 16.3 %collective-permute-start.9 = (f32[5,2,16,128]{3,2,1,0:T(8,128)S(1)}, f32[5,2,16,128]{3,2,1,0:T(8,128)S(1)}, u32[]{:S(2)}, u32[]{:S(2)}) collective-permute-start(f32[5,2,16,128]{3,2,1,0:T(8,128)S(1)} %get-tuple-element.33), channel_id=1, source_target_pairs={{0,1},{1,0},{2,3},{3,2},{4,5},{5,4},{6,7},{7,6},{8,9},{9,8},{10,11... | collective-permute-start | bytes 245768 | tf_op jit(solution)/shard_map/ppermute | solution.py:480

commit v3 on v2

--- a/solution.py
+++ b/solution.py
@@ -113,14 +113,12 @@
 
 def t_own(hi, lo, coef, out):
     bhi, blo = split(band(coef))
-    both = jnp.concatenate([bhi, blo], axis=1)
+    mat = jnp.concatenate([bhi, bhi, blo], axis=0)
     step = 8
     for g in range(NX // step):
         h = hi[pl.ds(g * step, step)].reshape(step * C * NR, NT)
         l = lo[pl.ds(g * step, step)].reshape(step * C * NR, NT)
-        first = jnp.dot(h, both, preferred_element_type=F32)
-        second = jnp.dot(l, bhi, preferred_element_type=F32)
-        total = first[:, :NT] + first[:, NT:] + second
+        total = jnp.dot(jnp.concatenate([h, l, h], axis=1), mat, preferred_element_type=F32)
         out[pl.ds(g * step, step)] = total.reshape(step, C, NR, NT)
 
 
@@ -220,30 +218,27 @@
         body(x)
 
 
-def loop(lo, hi, body):
+def loop(lo, hi, body, unroll=1):
     def step(k, carry):
         body(k)
         return carry
 
-    lax.fori_loop(lo, hi, step, 0)
-
-
-def rims_x(state, seed, xe, xo):
+    lax.fori_loop(lo, hi, step, 0, unroll=unroll)
+
+
+def rims(state_hbm, seed_hbm, state, seed, xe, xo, re, ro, th, sems):
+    moves = [
+        pltpu.make_async_copy(state_hbm, state, sems.at[0]),
+        pltpu.make_async_copy(seed_hbm, seed, sems.at[1]),
+    ]
+    for move in moves:
+        move.start()
+    th[...] = jnp.zeros(th.shape, F32)
+    even_r = is_even("row")
     even = parity("gx") == 0
     first = jnp.where(even, NX - W, 0)
     second = jnp.where(even, 0, NX - W)
-    for start, out in ((first, xe), (second, xo)):
-        for i in range(W):
-            q = [state[c, start + i] for c in range(C)]
-            f = flux_x(q, prims(q))
-            for c in range(C):
-                out[c, i] = f[c]
-                out[C + c, i] = seed[c, start + i]
-
-
-def rims_rt(state, re, ro, th):
-    even = is_even("row")
-    th[...] = jnp.zeros(th.shape, F32)
+    moves[0].wait()
 
     def pair(k):
         keep = []
@@ -253,9 +248,20 @@
             keep.append(flux_r(q, pr))
             t_pack_into(th, flux_t(q, pr), xx, k)
         for c in range(C):
-            re[c, k], ro[c, k] = r_pack(keep[0][c], keep[1][c], even)
-
-    loop(0, NX // 2, pair)
+            re[c, k], ro[c, k] = r_pack(keep[0][c], keep[1][c], even_r)
+
+    loop(0, NX // 2, pair, 2)
+    for start, out in ((first, xe), (second, xo)):
+        for i in range(W):
+            q = [state[c, start + i] for c in range(C)]
+            f = flux_x(q, prims(q))
+            for c in range(C):
+                out[c, i] = f[c]
+    moves[1].wait()
+    for start, out in ((first, xe), (second, xo)):
+        for i in range(W):
+            for c in range(C):
+                out[C + c, i] = seed[c, start + i]
 
 
 def own(cx, cr, ct, cf, met, state, seed, psec, plam, fx, fr, hi, lo, tt):
@@ -274,17 +280,19 @@
             hi[x, c], lo[x, c] = split(h[c])
 
     loop(0, NX, fill)
-    t_own(hi, lo, ct, tt)
-    fc = [cf[TAPS - 1 - j] for j in range(TAPS)]
-    xc = [cx[j] for j in range(TAPS)]
+    t_own(hi, lo, [-DT * ct[j] for j in range(TAPS)], tt)
+    fc = [-cf[TAPS - 1 - j] for j in range(TAPS)]
+    xc = [-DT * cx[j] for j in range(TAPS)]
+    rc = [-DT * cr[j] for j in range(TAPS)]
 
     def plane(x):
         for c in range(C):
-            acc = x_taps(lambda at: fx[c, at], x, xc) + mt * tt[x, c]
+            acc = state[c, x] + mt * tt[x, c]
+            acc += x_taps(lambda at: fx[c, at], x, xc)
             for j in range(TAPS):
-                acc += cr[j] * fr[c, x, 4 + j : 20 + j]
-            psec[c, x] = state[c, x] - DT * acc
-            plam[c, x] = seed[c, x] - x_taps(lambda at: seed[c, at], x, fc)
+                acc += rc[j] * fr[c, x, 4 + j : 20 + j]
+            psec[c, x] = acc
+            plam[c, x] = seed[c, x] + x_taps(lambda at: seed[c, at], x, fc)
 
     over_planes(plane)
 
@@ -485,10 +493,21 @@
 
 
 def shards(state, seed, cx, cr, ct, cf, met):
-    xe, xo = call(rims_x, [], [state, seed], [XPAY, XPAY])
-    xe, xo = swap(xe, "gx", 0), swap(xo, "gx", 1)
-    re, ro, th = call(rims_rt, [], [state], [RPAY, RPAY, TPAY])
-    re, ro, th = swap(re, "row", 0), swap(ro, "row", 1), across(th)
+    shapes = [FULL, FULL, XPAY, XPAY, RPAY, RPAY, TPAY]
+    state, seed, xe, xo, re, ro, th = pl.pallas_call(
+        rims,
+        in_specs=[pl.BlockSpec(memory_space=pltpu.HBM)] * 2,
+        out_specs=[VM] * len(shapes),
+        out_shape=[pltpu.VMEM(s, F32) for s in shapes],
+        scratch_shapes=[pltpu.SemaphoreType.DMA((2,))],
+        name="rims",
+        compiler_params=LIMIT,
+    )(*[pltpu.with_memory_space_constraint(v, pltpu.HBM) for v in (state, seed)])
+    th = across(th)
+    xe = swap(xe, "gx", 0)
+    xo = swap(xo, "gx", 1)
+    re = swap(re, "row", 0)
+    ro = swap(ro, "row", 1)
     psec, plam = call(
         own,
         [cx, cr, ct, cf, met],

time: 67.4 us -> 64.8 us (0.961)
  the two profiles are of different devices: /device:TPU:99 before, /device:TPU:227 now
where the time goes in v3:
time: 64.8 us; the launch traced here: 64.4 us
  starting transfers between devices  31 us (48%)
  Pallas kernels  19 us (29%)
  waiting for transfers between devices  13.6 us (21%)
  between operations  0.85 us (1%)
    ppermute x8, starting transfers between devices, swap(): return lax.ppermute(value, axis, pairs)  22.6 us
    ppermute x2, waiting for transfers between devices, across(): return lax.ppermute(value, 'th', [(0, 1), (1, 0)])  13.6 us
    ppermute x2, starting transfers between devices, across(): return lax.ppermute(value, 'th', [(0, 1), (1, 0)])  8.39 us
    pallas_call x1, Pallas kernels, shards(): pl.pallas_call(finish, in_specs=[SM] * 5 + [VM] * 6, out_specs=[ANY, ANY,...  7.65 us
    pallas_call x2, Pallas kernels, call(): return run(*smem, *[near(v) for v in vmem])  7.39 us
    pallas_call x1, Pallas kernels, shards(): pl.pallas_call(rims, in_specs=[pl.BlockSpec(memory_space=pltpu.HBM)] * 2,...  2.36 us
    pallas_call x1, Pallas kernels, shards(): pl.pallas_call(edges, in_specs=[SM] * 2 + [VM] * 5 + [ANY] * 2, out_specs...  1.57 us
  transfers between devices with their start and end apart: 10, of which 2 were waited for; matrix products, arithmetic and copies ran while one was open for 0% of the time, Pallas kernels for 19%

profile of v3, /device:TPU:227, one launch (start us, length us, event | category | flops | bytes accessed | tf_op | source)
XLA Modules:
  0.0 64.4 jit_solution(11712818625305428210)
XLA Ops:
  0.6 0.0 copy-start.1
  0.6 0.0 copy-start
  0.7 0.0 copy-start.4
  0.7 0.0 copy-start.3
  0.7 0.0 copy-start.2
  0.7 2.4 %rims.1 = (f32[5,32,16,128]{3,2,1,0:T(8,128)S(1)}, f32[5,32,16,128]{3,2,1,0:T(8,128)S(1)}, f32[10,4,16,128]{3,2,1,0:T(8,128)S(1)}, f32[10,4,16,128]{3,2,1,0:T(8,...) custom-call(f32[5,32,16,128]{3,2,1,0:T(8,128)} %state_hbm.1, ...), custom_call_target="tpu_custom_call" | custom-call | tf_op jit(solution)/shard_map/rims/pallas_call | solution.py:497
  3.1 3.2 %collective-permute-start = (f32[10,4,16,128]{3,2,1,0:T(8,128)S(1)}, f32[10,4,16,128]{3,2,1,0:T(8,128)S(1)}, u32[]{:S(2)}, u32[]{:S(2)}) collective-permute-start(f32[10,4,16,128]{3,2,1,0:T(8,128)S(1)} %get-tuple-element.26), channel_id=1, source_target_pairs={{0,16},{16,0},{32,48},{48,32},{64,80},{80,64},{96,112},{112,96},{1... | collective-permute-start | bytes 983048 | tf_op jit(solution)/shard_map/ppermute | solution.py:484
  6.3 1.9 %collective-permute-start.1 = (f32[10,4,16,128]{3,2,1,0:T(8,128)S(1)}, f32[10,4,16,128]{3,2,1,0:T(8,128)S(1)}, u32[]{:S(2)}, u32[]{:S(2)}) collective-permute-start(f32[10,4,16,128]{3,2,1,0:T(8,128)S(1)} %get-tuple-element.27), channel_id=1, source_target_pairs={{16,32},{32,16},{48,64},{64,48},{80,96},{96,80},{112,128},{128,112... | collective-permute-start | bytes 983048 | tf_op jit(solution)/shard_map/ppermute | solution.py:484
  8.2 2.9 %collective-permute-start.2 = (f32[5,16,8,128]{3,2,1,0:T(8,128)S(1)}, f32[5,16,8,128]{3,2,1,0:T(8,128)S(1)}, u32[]{:S(2)}, u32[]{:S(2)}) collective-permute-start(f32[5,16,8,128]{3,2,1,0:T(8,128)S(1)} %get-tuple-element.28), channel_id=1, source_target_pairs={{0,2},{2,0},{4,6},{6,4},{8,10},{10,8},{12,14},{14,12},{1,3},{3,1},... | collective-permute-start | bytes 983048 | tf_op jit(solution)/shard_map/ppermute | solution.py:484
  11.1 3.0 %collective-permute-start.3 = (f32[5,16,8,128]{3,2,1,0:T(8,128)S(1)}, f32[5,16,8,128]{3,2,1,0:T(8,128)S(1)}, u32[]{:S(2)}, u32[]{:S(2)}) collective-permute-start(f32[5,16,8,128]{3,2,1,0:T(8,128)S(1)} %get-tuple-element.29), channel_id=1, source_target_pairs={{2,4},{4,2},{6,8},{8,6},{10,12},{12,10},{3,5},{5,3},{7,9},{9,7},{1... | collective-permute-start | bytes 983048 | tf_op jit(solution)/shard_map/ppermute | solution.py:484
  14.1 4.8 %collective-permute-start.4 = (f32[5,2,16,128]{3,2,1,0:T(8,128)S(1)}, f32[5,2,16,128]{3,2,1,0:T(8,128)S(1)}, u32[]{:S(2)}, u32[]{:S(2)}) collective-permute-start(f32[5,2,16,128]{3,2,1,0:T(8,128)S(1)} %get-tuple-element.30), channel_id=1, source_target_pairs={{0,1},{1,0},{2,3},{3,2},{4,5},{5,4},{6,7},{7,6},{8,9},{9,8},{10,11... | collective-permute-start | bytes 245768 | tf_op jit(solution)/shard_map/ppermute | solution.py:488
  18.9 0.0 copy-done.1
  18.9 0.0 copy-done
  18.9 0.0 copy-done.4
  18.9 0.0 copy-done.3
  18.9 0.0 copy-done.2
  19.0 4.7 %shard_map.86 = (f32[5,32,16,128]{3,2,1,0:T(8,128)S(1)}, f32[5,32,16,128]{3,2,1,0:T(8,128)S(1)}) custom-call(f32[9]{0:T(128)S(1)} %copy-done, f32[9]{0:T(128)S(1)} %copy-done.2, f32[9]{0:T(128)S(1)} %copy-done.3, f32[9]{0:T(128)S(1)} %copy-done.1, f32[16]{0:T(128)S(1)} %copy-done.4, f32[5,32,16,128]{3,2,1,0:T(8,128)S(1)} %get-tuple-element.22.state, ...), custom_call_target="tpu_custom_call" | custom-call | tf_op jit(solution)/shard_map/pallas_call | solution.py:476
  23.6 0.8 %collective-permute-done.4.th = f32[5,2,16,128]{3,2,1,0:T(8,128)S(1)} collective-permute-done((f32[5,2,16,128]{3,2,1,0:T(8,128)S(1)}, f32[5,2,16,128]{3,2,1,0:T(8,128)S(1)}, u32[]{:S(2)}, u32[]{:S(2)}) %collective-permute-start.4) | collective-permute-done | bytes 81952 | tf_op jit(solution)/shard_map/ppermute | solution.py:488
  24.5 0.0 collective-permute-done.xe
  24.5 0.0 collective-permute-done.1.xo
  24.5 0.0 collective-permute-done.2.re
  24.5 0.0 collective-permute-done.3.ro
  24.5 2.7 %shard_map.87 = (f32[5,32,16,128]{3,2,1,0:T(8,128)S(1)}, f32[5,32,16,128]{3,2,1,0:T(8,128)S(1)}, f32[10,4,16,128]{3,2,1,0:T(8,128)S(1)}, f32[10,4,16,128]{3,2,1,...) custom-call(f32[9]{0:T(128)S(1)} %copy-done, ...), custom_call_target="tpu_custom_call" | custom-call | tf_op jit(solution)/shard_map/pallas_call | solution.py:476
  27.2 3.7 %collective-permute-start.7 = (f32[5,16,8,128]{3,2,1,0:T(8,128)S(1)}, f32[5,16,8,128]{3,2,1,0:T(8,128)S(1)}, u32[]{:S(2)}, u32[]{:S(2)}) collective-permute-start(f32[5,16,8,128]{3,2,1,0:T(8,128)S(1)} %get-tuple-element.35), channel_id=1, source_target_pairs={{0,2},{2,0},{4,6},{6,4},{8,10},{10,8},{12,14},{14,12},{1,3},{3,1},... | collective-permute-start | bytes 983048 | tf_op jit(solution)/shard_map/ppermute | solution.py:484
  31.0 3.0 %collective-permute-start.8 = (f32[5,16,8,128]{3,2,1,0:T(8,128)S(1)}, f32[5,16,8,128]{3,2,1,0:T(8,128)S(1)}, u32[]{:S(2)}, u32[]{:S(2)}) collective-permute-start(f32[5,16,8,128]{3,2,1,0:T(8,128)S(1)} %get-tuple-element.36), channel_id=1, source_target_pairs={{2,4},{4,2},{6,8},{8,6},{10,12},{12,10},{3,5},{5,3},{7,9},{9,7},{1... | collective-permute-start | bytes 983048 | tf_op jit(solution)/shard_map/ppermute | solution.py:484
  34.0 2.9 %collective-permute-start.5 = (f32[10,4,16,128]{3,2,1,0:T(8,128)S(1)}, f32[10,4,16,128]{3,2,1,0:T(8,128)S(1)}, u32[]{:S(2)}, u32[]{:S(2)}) collective-permute-start(f32[10,4,16,128]{3,2,1,0:T(8,128)S(1)} %get-tuple-element.31), channel_id=1, source_target_pairs={{0,16},{16,0},{32,48},{48,32},{64,80},{80,64},{96,112},{112,96},{1... | collective-permute-start | bytes 983048 | tf_op jit(solution)/shard_map/ppermute | solution.py:484
  36.9 1.9 %collective-permute-start.6 = (f32[10,4,16,128]{3,2,1,0:T(8,128)S(1)}, f32[10,4,16,128]{3,2,1,0:T(8,128)S(1)}, u32[]{:S(2)}, u32[]{:S(2)}) collective-permute-start(f32[10,4,16,128]{3,2,1,0:T(8,128)S(1)} %get-tuple-element.32), channel_id=1, source_target_pairs={{16,32},{32,16},{48,64},{64,48},{80,96},{96,80},{112,128},{128,112... | collective-permute-start | bytes 983048 | tf_op jit(solution)/shard_map/ppermute | solution.py:484
  38.8 3.6 %collective-permute-start.9 = (f32[5,2,16,128]{3,2,1,0:T(8,128)S(1)}, f32[5,2,16,128]{3,2,1,0:T(8,128)S(1)}, u32[]{:S(2)}, u32[]{:S(2)}) collective-permute-start(f32[5,2,16,128]{3,2,1,0:T(8,128)S(1)} %get-tuple-element.37), channel_id=1, source_target_pairs={{0,1},{1,0},{2,3},{3,2},{4,5},{5,4},{6,7},{7,6},{8,9},{9,8},{10,11... | collective-permute-start | bytes 245768 | tf_op jit(solution)/shard_map/ppermute | solution.py:488
  42.4 12.7 %collective-permute-done.9.th2 = f32[5,2,16,128]{3,2,1,0:T(8,128)S(1)} collective-permute-done((f32[5,2,16,128]{3,2,1,0:T(8,128)S(1)}, f32[5,2,16,128]{3,2,1,0:T(8,128)S(1)}, u32[]{:S(2)}, u32[]{:S(2)}) %collective-permute-start.9) | collective-permute-done | bytes 81952 | tf_op jit(solution)/shard_map/ppermute | solution.py:488
  55.1 0.0 collective-permute-done.7.re2
  55.1 0.0 collective-permute-done.8.ro2
  55.1 7.7 %finish.1 = (f32[5,32,16,128]{3,2,1,0:T(8,128)}, f32[5,32,16,128]{3,2,1,0:T(8,128)}, f32[2,5,4,16,128]{4,3,2,1,0:T(8,128)S(1)}, f32[2,5,4,16,128]{4,3,2,1,0:T(8,128)S(1)}) custom-call(f32[9]{0:T(128)S(1)} %copy-done, f32[9]{0:T(128)S(1)} %copy-done.2, f32[9]{0:T(128)S(1)} %copy-done.3, f32[9]{0:T(128)S(1)} %copy-done.1, f32[16]{0:T(128)S(1)} %copy-done.4, ...), custom_call_target="tpu_custom_call" | custom-call | tf_op jit(solution)/shard_map/finish/pallas_call | solution.py:532
  62.8 0.0 collective-permute-done.5.xe2
  62.8 0.0 collective-permute-done.6.xo2
  62.8 1.6 %edges.1 = (f32[5,32,16,128]{3,2,1,0:T(8,128)}, f32[5,32,16,128]{3,2,1,0:T(8,128)}) custom-call(f32[9]{0:T(128)S(1)} %copy-done, f32[9]{0:T(128)S(1)} %copy-done.1, f32[5,32,16,128]{3,2,1,0:T(8,128)S(1)} %get-tuple-element.22.state, f32[10,4,16,128]{3,2,1,0:T(8,128)S(1)} %collective-permute-done.5.xe2, ...), custom_call_target="tpu_custom_call", output_to_operand_aliasing={{0}: (7, {}), {1}: (8, {})} | custom-call | tf_op jit(solution)/shard_map/edges/pallas_call | solution.py:541
Async XLA Ops:
  0.6 18.3 %copy-start.1 = (f32[9]{0:T(128)S(1)}, f32[9]{0:T(128)}, u32[]{:S(2)}) copy-start(f32[9]{0:T(128)} %cf.7) | copy-start | bytes 112
  0.6 18.3 %copy-start = (f32[9]{0:T(128)S(1)}, f32[9]{0:T(128)}, u32[]{:S(2)}) copy-start(f32[9]{0:T(128)} %cx.7) | copy-start | bytes 112
  0.7 18.3 %copy-start.4 = (f32[16]{0:T(128)S(1)}, f32[16]{0:T(128)}, u32[]{:S(2)}) copy-start(f32[16]{0:T(128)} %met.5) | copy-start | bytes 196
  0.7 18.3 %copy-start.3 = (f32[9]{0:T(128)S(1)}, f32[9]{0:T(128)}, u32[]{:S(2)}) copy-start(f32[9]{0:T(128)} %ct.5) | copy-start | bytes 112
  0.7 18.3 %copy-start.2 = (f32[9]{0:T(128)S(1)}, f32[9]{0:T(128)}, u32[]{:S(2)}) copy-start(f32[9]{0:T(128)} %cr.5) | copy-start | bytes 112
  3.1 21.4 %collective-permute-start = (f32[10,4,16,128]{3,2,1,0:T(8,128)S(1)}, f32[10,4,16,128]{3,2,1,0:T(8,128)S(1)}, u32[]{:S(2)}, u32[]{:S(2)}) collective-permute-start(f32[10,4,16,128]{3,2,1,0:T(8,128)S(1)} %get-tuple-element.26), channel_id=1, source_target_pairs={{0,16},{16,0},{32,48},{48,32},{64,80},{80,64},{96,112},{112,96},{1... | collective-permute-start | bytes 983048 | tf_op jit(solution)/shard_map/ppermute | solution.py:484
  6.3 18.2 %collective-permute-start.1 = (f32[10,4,16,128]{3,2,1,0:T(8,128)S(1)}, f32[10,4,16,128]{3,2,1,0:T(8,128)S(1)}, u32[]{:S(2)}, u32[]{:S(2)}) collective-permute-start(f32[10,4,16,128]{3,2,1,0:T(8,128)S(1)} %get-tuple-element.27), channel_id=1, source_target_pairs={{16,32},{32,16},{48,64},{64,48},{80,96},{96,80},{112,128},{128,112... | collective-permute-start | bytes 983048 | tf_op jit(solution)/shard_map/ppermute | solution.py:484
  8.2 16.3 %collective-permute-start.2 = (f32[5,16,8,128]{3,2,1,0:T(8,128)S(1)}, f32[5,16,8,128]{3,2,1,0:T(8,128)S(1)}, u32[]{:S(2)}, u32[]{:S(2)}) collective-permute-start(f32[5,16,8,128]{3,2,1,0:T(8,128)S(1)} %get-tuple-element.28), channel_id=1, source_target_pairs={{0,2},{2,0},{4,6},{6,4},{8,10},{10,8},{12,14},{14,12},{1,3},{3,1},... | collective-permute-start | bytes 983048 | tf_op jit(solution)/shard_map/ppermute | solution.py:484
  11.1 13.4 %collective-permute-start.3 = (f32[5,16,8,128]{3,2,1,0:T(8,128)S(1)}, f32[5,16,8,128]{3,2,1,0:T(8,128)S(1)}, u32[]{:S(2)}, u32[]{:S(2)}) collective-permute-start(f32[5,16,8,128]{3,2,1,0:T(8,128)S(1)} %get-tuple-element.29), channel_id=1, source_target_pairs={{2,4},{4,2},{6,8},{8,6},{10,12},{12,10},{3,5},{5,3},{7,9},{9,7},{1... | collective-permute-start | bytes 983048 | tf_op jit(solution)/shard_map/ppermute | solution.py:484
  14.1 10.4 %collective-permute-start.4 = (f32[5,2,16,128]{3,2,1,0:T(8,128)S(1)}, f32[5,2,16,128]{3,2,1,0:T(8,128)S(1)}, u32[]{:S(2)}, u32[]{:S(2)}) collective-permute-start(f32[5,2,16,128]{3,2,1,0:T(8,128)S(1)} %get-tuple-element.30), channel_id=1, source_target_pairs={{0,1},{1,0},{2,3},{3,2},{4,5},{5,4},{6,7},{7,6},{8,9},{9,8},{10,11... | collective-permute-start | bytes 245768 | tf_op jit(solution)/shard_map/ppermute | solution.py:488
  27.2 27.9 %collective-permute-start.7 = (f32[5,16,8,128]{3,2,1,0:T(8,128)S(1)}, f32[5,16,8,128]{3,2,1,0:T(8,128)S(1)}, u32[]{:S(2)}, u32[]{:S(2)}) collective-permute-start(f32[5,16,8,128]{3,2,1,0:T(8,128)S(1)} %get-tuple-element.35), channel_id=1, source_target_pairs={{0,2},{2,0},{4,6},{6,4},{8,10},{10,8},{12,14},{14,12},{1,3},{3,1},... | collective-permute-start | bytes 983048 | tf_op jit(solution)/shard_map/ppermute | solution.py:484
  31.0 24.2 %collective-permute-start.8 = (f32[5,16,8,128]{3,2,1,0:T(8,128)S(1)}, f32[5,16,8,128]{3,2,1,0:T(8,128)S(1)}, u32[]{:S(2)}, u32[]{:S(2)}) collective-permute-start(f32[5,16,8,128]{3,2,1,0:T(8,128)S(1)} %get-tuple-element.36), channel_id=1, source_target_pairs={{2,4},{4,2},{6,8},{8,6},{10,12},{12,10},{3,5},{5,3},{7,9},{9,7},{1... | collective-permute-start | bytes 983048 | tf_op jit(solution)/shard_map/ppermute | solution.py:484
  34.0 28.8 %collective-permute-start.5 = (f32[10,4,16,128]{3,2,1,0:T(8,128)S(1)}, f32[10,4,16,128]{3,2,1,0:T(8,128)S(1)}, u32[]{:S(2)}, u32[]{:S(2)}) collective-permute-start(f32[10,4,16,128]{3,2,1,0:T(8,128)S(1)} %get-tuple-element.31), channel_id=1, source_target_pairs={{0,16},{16,0},{32,48},{48,32},{64,80},{80,64},{96,112},{112,96},{1... | collective-permute-start | bytes 983048 | tf_op jit(solution)/shard_map/ppermute | solution.py:484
  36.9 25.9 %collective-permute-start.6 = (f32[10,4,16,128]{3,2,1,0:T(8,128)S(1)}, f32[10,4,16,128]{3,2,1,0:T(8,128)S(1)}, u32[]{:S(2)}, u32[]{:S(2)}) collective-permute-start(f32[10,4,16,128]{3,2,1,0:T(8,128)S(1)} %get-tuple-element.32), channel_id=1, source_target_pairs={{16,32},{32,16},{48,64},{64,48},{80,96},{96,80},{112,128},{128,112... | collective-permute-start | bytes 983048 | tf_op jit(solution)/shard_map/ppermute | solution.py:484
  38.8 16.3 %collective-permute-start.9 = (f32[5,2,16,128]{3,2,1,0:T(8,128)S(1)}, f32[5,2,16,128]{3,2,1,0:T(8,128)S(1)}, u32[]{:S(2)}, u32[]{:S(2)}) collective-permute-start(f32[5,2,16,128]{3,2,1,0:T(8,128)S(1)} %get-tuple-element.37), channel_id=1, source_target_pairs={{0,1},{1,0},{2,3},{3,2},{4,5},{5,4},{6,7},{7,6},{8,9},{9,8},{10,11... | collective-permute-start | bytes 245768 | tf_op jit(solution)/shard_map/ppermute | solution.py:488

commit v4 on v3

--- a/solution.py
+++ b/solution.py
@@ -62,17 +62,17 @@
     return [o0, o1, o2, o3, o4]
 
 
-def pull_x(q, pr, a):
+def pull_rt(q, pr, b, c):
     inv, u, v, w, _, h = pr
-    hb = a[4] * u
-    pb = a[1] + hb
+    hb = b[4] * v + c[4] * w
+    pb = b[2] + c[3] + hb
     s = (-0.5 * GAM) * pb
-    ub = (a[1] * q[1] + a[2] * q[2] + a[3] * q[3] + a[4] * h + s * q[1]) * inv
-    vb = s * v
-    wb = s * w
-    o1 = a[0] + (a[1] + s) * u + ub
-    o2 = a[2] * u + s * v + vb
-    o3 = a[3] * u + s * w + wb
+    ub = s * u
+    vb = (b[1] * q[1] + b[2] * q[2] + b[3] * q[3] + b[4] * h + s * q[2]) * inv
+    wb = (c[1] * q[1] + c[2] * q[2] + c[3] * q[3] + c[4] * h + s * q[3]) * inv
+    o1 = s * u + b[1] * v + c[1] * w + ub
+    o2 = b[0] + (b[2] + s) * v + c[2] * w + vb
+    o3 = c[0] + b[3] * v + (c[3] + s) * w + wb
     o4 = hb + GAM * pb
     o0 = -(ub * u + vb * v + wb * w)
     return [o0, o1, o2, o3, o4]
@@ -146,11 +146,18 @@
     return jnp.where((lane < 4) | (lane >= 124), moved, 0.0)
 
 
-def t_pack_into(ref, fields, xx, k):
-    lane = iota((NR, NT), 1)
+def t_pack_one(ref, at, field, k):
+    moved = pltpu.roll(field, (8 * k + 4) % NT, 1)
+    ref[at] = jnp.where(lane_block() == k, moved, ref[at])
+
+
+def lane_block():
+    return lax.shift_right_logical(iota((NR, NT), 1), 3)
+
+
+def t_pack_into(ref, base, fields, xx, k):
     for c in range(C):
-        moved = pltpu.roll(fields[c], 8 * k + 4, 1)
-        ref[c, xx] = jnp.where(lane // 8 == k, moved, ref[c, xx])
+        t_pack_one(ref, base + 2 * c + xx, fields[c], k)
 
 
 def r_pack(first, second, even):
@@ -168,16 +175,16 @@
     return low, high
 
 
-def r_halo(low, high, xx, coefs):
+def r_halo(low, high, xlo, xhi, coefs):
     lo_c, hi_c = coefs
     top = None
     for j in range(W):
-        shift = (8 - (4 * xx + j)) % 8
+        shift = (8 - (4 * xlo + j)) % 8
         term = lo_c[j] * (pltpu.roll(low, shift, 0) if shift else low)
         top = term if top is None else top + term
     bottom = None
     for j in range(W + 1, TAPS):
-        shift = (12 - j - 4 * xx) % 8
+        shift = (12 - j - 4 * xhi) % 8
         term = hi_c[j] * (pltpu.roll(high, shift, 0) if shift else high)
         bottom = term if bottom is None else bottom + term
     return jnp.concatenate([top, bottom], axis=0)
@@ -226,19 +233,53 @@
     lax.fori_loop(lo, hi, step, 0, unroll=unroll)
 
 
-def rims(state_hbm, seed_hbm, state, seed, xe, xo, re, ro, th, sems):
+def rim_starts():
+    even = parity("gx") == 0
+    return jnp.where(even, NX - W, 0), jnp.where(even, 0, NX - W)
+
+
+def first(cf, state_hbm, seed_hbm, state, seed, prim, xe, xo, sems):
     moves = [
-        pltpu.make_async_copy(state_hbm, state, sems.at[0]),
-        pltpu.make_async_copy(seed_hbm, seed, sems.at[1]),
+        pltpu.make_async_copy(seed_hbm, seed, sems.at[0]),
+        pltpu.make_async_copy(state_hbm, state, sems.at[1]),
     ]
     for move in moves:
         move.start()
+    fc = [-cf[TAPS - 1 - j] for j in range(TAPS)]
+    moves[0].wait()
+    for side, base in enumerate((0, NX - W)):
+        for i in range(W):
+            for c in range(C):
+                prim[side, c, i] = seed[c, base + i] + x_taps(lambda at: seed[c, at], base + i, fc)
+    starts = rim_starts()
+    even = parity("gx") == 0
+    sides = jnp.where(even, 1, 0), jnp.where(even, 0, 1)
+    moves[1].wait()
+    for start, side, out in zip(starts, sides, (xe, xo)):
+        for i in range(W):
+            q = [state[c, start + i] for c in range(C)]
+            f = flux_x(q, prims(q))
+            for c in range(C):
+                out[c, i] = f[c]
+                out[C + c, i] = seed[c, start + i]
+                out[2 * C + c, i] = prim[side, c, i]
+
+
+def second(cf, met, state, seed, prim, plam, re, ro, th):
+    fc = [-cf[TAPS - 1 - j] for j in range(TAPS)]
+    mt = metric_tile(met)
+    even = is_even("row")
     th[...] = jnp.zeros(th.shape, F32)
-    even_r = is_even("row")
-    even = parity("gx") == 0
-    first = jnp.where(even, NX - W, 0)
-    second = jnp.where(even, 0, NX - W)
-    moves[0].wait()
+    for side, base in enumerate((0, NX - W)):
+        for i in range(W):
+            for c in range(C):
+                plam[c, base + i] = prim[side, c, i]
+
+    def plane(x):
+        for c in range(C):
+            plam[c, x] = seed[c, x] + x_taps(lambda at: seed[c, at], x, fc)
+
+    loop(W, NX - W, plane, 2)
 
     def pair(k):
         keep = []
@@ -246,25 +287,23 @@
             q = [state[c, 2 * k + xx] for c in range(C)]
             pr = prims(q)
             keep.append(flux_r(q, pr))
-            t_pack_into(th, flux_t(q, pr), xx, k)
-        for c in range(C):
-            re[c, k], ro[c, k] = r_pack(keep[0][c], keep[1][c], even_r)
+            t_pack_into(th, 0, flux_t(q, pr), xx, k)
+            t_pack_into(th, 2 * C, [mt * plam[c, 2 * k + xx] for c in range(C)], xx, k)
+        for c in range(C):
+            re[c, k], ro[c, k] = r_pack(keep[0][c], keep[1][c], even)
+            at = NX // 2 + k
+            re[c, at], ro[c, at] = r_pack(plam[c, 2 * k], plam[c, 2 * k + 1], even)
 
     loop(0, NX // 2, pair, 2)
-    for start, out in ((first, xe), (second, xo)):
-        for i in range(W):
-            q = [state[c, start + i] for c in range(C)]
-            f = flux_x(q, prims(q))
-            for c in range(C):
-                out[c, i] = f[c]
-    moves[1].wait()
-    for start, out in ((first, xe), (second, xo)):
-        for i in range(W):
-            for c in range(C):
-                out[C + c, i] = seed[c, start + i]
-
-
-def own(cx, cr, ct, cf, met, state, seed, psec, plam, fx, fr, hi, lo, tt):
+    for n, k in enumerate(RIM_PAIRS):
+        for c in range(C):
+            at = NX + n
+            re[c, at], ro[c, at] = r_pack(seed[c, 2 * k], seed[c, 2 * k + 1], even)
+            for xx in range(2):
+                t_pack_one(th, 4 * C + 2 * (c // 4) + xx, seed[c, 2 * k + xx], n + 4 * (c % 4))
+
+
+def own(cx, cr, ct, met, state, psec, fx, fr, hi, lo, tt):
     mt = metric_tile(met)
     zero = jnp.zeros((8, NT), F32)
 
@@ -281,7 +320,6 @@
 
     loop(0, NX, fill)
     t_own(hi, lo, [-DT * ct[j] for j in range(TAPS)], tt)
-    fc = [-cf[TAPS - 1 - j] for j in range(TAPS)]
     xc = [-DT * cx[j] for j in range(TAPS)]
     rc = [-DT * cr[j] for j in range(TAPS)]
 
@@ -292,63 +330,72 @@
             for j in range(TAPS):
                 acc += rc[j] * fr[c, x, 4 + j : 20 + j]
             psec[c, x] = acc
-            plam[c, x] = seed[c, x] + x_taps(lambda at: seed[c, at], x, fc)
 
     over_planes(plane)
 
 
-def join(cx, cr, ct, cf, met, psec, plam, xe, xo, re, ro, th, sec, lam, xe2, xo2, re2, ro2, th2):
+def join(cx, cr, ct, cf, met, seed, psec, plam, xe, xo, re, ro, th, sec, lam, lamh, xe2, xo2):
     mt = metric_tile(met)
     evx, evr = is_even("gx"), is_even("row")
-    fc = [cf[TAPS - 1 - j] for j in range(TAPS)]
-    xc = [cx[j] for j in range(TAPS)]
-    for low in (True, False):
-        base = 0 if low else NX - W
-        for c in range(2 * C):
-            near, far = (xo, xe) if low else (xe, xo)
-            planes = [jnp.where(evx, near[c, i], far[c, i]) for i in range(W)]
+    fc = [-cf[TAPS - 1 - j] for j in range(TAPS)]
+    xc = [-DT * cx[j] for j in range(TAPS)]
+    place = jnp.full((NR, NT), lax.axis_index("gx"), jnp.int32)
+    has = place > 0, place < lax.axis_size("gx") - 1
+    for side, base in enumerate((0, NX - W)):
+        low = side == 0
+        near_, far = (xo, xe) if low else (xe, xo)
+
+        def halo(c):
+            return [jnp.where(evx, near_[c, i], far[c, i]) for i in range(W)]
+
+        for c in range(C):
+            flux, seeds, share = halo(c), halo(C + c), halo(2 * C + c)
+            mine = [seed[c, base + i] for i in range(W)]
             for i in range(W):
-                if c < C:
-                    sec[c, base + i] = psec[c, base + i] - DT * x_halo(planes, i, low, xc)
-                else:
-                    lam[c - C, base + i] = plam[c - C, base + i] - x_halo(planes, i, low, fc)
-    th2[...] = jnp.zeros(th2.shape, F32)
-    rc = r_coefs(cr)
-    tc = t_pack_coefs(ct)
-    packed = [[mt * t_halo_packed(th[c, xx], tc) for xx in range(2)] for c in range(C)]
+                sec[c, base + i] = psec[c, base + i] + x_halo(flux, i, low, xc)
+                lam[c, base + i] = plam[c, base + i] + x_halo(seeds, i, low, fc)
+                value = share[i] + x_halo(mine, i, not low, fc)
+                lamh[side, c, i] = jnp.where(has[side], value, 0.0)
+    rc = r_coefs([-DT * cr[j] for j in range(TAPS)])
+    tc = t_pack_coefs([-DT * ct[j] for j in range(TAPS)])
+    packed = [[mt * t_halo_packed(th[2 * c + xx], tc) for xx in range(2)] for c in range(C)]
     ev8 = evr[:8]
 
-    def pair(k, s_ref, l_ref):
-        lams = [[], []]
+    def pair(k, s_ref, inside):
         for c in range(C):
             a, b = re[c, k], ro[c, k]
             low, high = jnp.where(ev8, b, a), jnp.where(ev8, a, b)
             for xx in range(2):
                 x = 2 * k + xx
-                share = r_halo(low, high, xx, rc) + t_unpack(packed[c][xx], k)
-                sec[c, x] = s_ref[c, x] - DT * share
-                value = l_ref[c, x]
-                lam[c, x] = value
-                lams[xx].append(value)
-        for c in range(C):
-            re2[c, k], ro2[c, k] = r_pack(lams[0][c], lams[1][c], evr)
-        for xx in range(2):
-            t_pack_into(th2, [mt * v for v in lams[xx]], xx, k)
-
-    loop(0, 2, functools.partial(pair, s_ref=sec, l_ref=lam))
-    loop(2, 14, functools.partial(pair, s_ref=psec, l_ref=plam))
-    loop(14, 16, functools.partial(pair, s_ref=sec, l_ref=lam))
-    even = parity("gx") == 0
-    first = jnp.where(even, NX - W, 0)
-    second = jnp.where(even, 0, NX - W)
-    for start, out in ((first, xe2), (second, xo2)):
-        for i in range(W):
+                share = r_halo(low, high, xx, xx, rc) + t_unpack(packed[c][xx], k)
+                sec[c, x] = s_ref[c, x] + share
+                if inside:
+                    lam[c, x] = plam[c, x]
+
+    def send():
+        starts = rim_starts()
+        even = parity("gx") == 0
+        corners = NX + jnp.where(even, 2, 0), NX + jnp.where(even, 0, 2)
+        for start, corner, out in zip(starts, corners, (xe2, xo2)):
             for c in range(C):
-                out[c, i] = sec[c, start + i]
-                out[C + c, i] = lam[c, start + i]
-
-
-def finish(cx, cr, ct, cf, met, state, sec, lam, re2, ro2, th2, new, adj, nrim, arim, lr, hi, lo, tt, nb, ab, sems):
+                for i in range(W):
+                    out[W * c + i] = sec[c, start + i]
+                for eo, src in enumerate((re, ro)):
+                    for p in range(2):
+                        out[W * C + 2 * c + eo, 8 * p : 8 * p + 8] = src[c, corner + p]
+            for t in range(4):
+                out[(W + 2) * C + t] = th[4 * C + t]
+
+    loop(0, 2, functools.partial(pair, s_ref=sec, inside=False))
+    loop(14, 16, functools.partial(pair, s_ref=sec, inside=False))
+    send()
+    loop(2, 14, functools.partial(pair, s_ref=psec, inside=True))
+
+
+def finish(
+    cx, cr, ct, cf, met, state, sec, lam, lamh, re, ro, th,
+    new, adj, nrim, arim, lr, hi, lo, tt, nb, ab, sems,
+):
     mt = metric_tile(met)
     evr = is_even("row")
     ev8 = evr[:8]
@@ -356,11 +403,12 @@
     rr = [-DT * cr[TAPS - 1 - j] for j in range(TAPS)]
     rt = [-DT * ct[TAPS - 1 - j] for j in range(TAPS)]
     tc = t_pack_coefs(rt)
-    packed = [[t_halo_packed(th2[c, xx], tc) for xx in range(2)] for c in range(C)]
+    packed = [[t_halo_packed(th[2 * C + 2 * c + xx], tc) for xx in range(2)] for c in range(C)]
 
     def fill(k):
         for c in range(C):
-            a, b = re2[c, k], ro2[c, k]
+            at = NX // 2 + k
+            a, b = re[c, at], ro[c, at]
             low, high = jnp.where(ev8, b, a), jnp.where(ev8, a, b)
             for xx in range(2):
                 x = 2 * k + xx
@@ -384,9 +432,14 @@
     def plane(x):
         q = [state[c, x] for c in range(C)]
         pr = prims(q)
+        rim = isinstance(x, int)
+        side, at = (0, x) if rim and x < W else (1, x - NX + W)
         a, b, g = [], [], []
         for c in range(C):
-            a.append(x_taps(lambda at: lam[c, at], x, rx))
+            acc = x_taps(lambda at: lam[c, at], x, rx)
+            if rim:
+                acc += x_halo([lamh[side, c, h] for h in range(W)], at, side == 0, rx)
+            a.append(acc)
             acc = None
             for j in range(TAPS):
                 term = rr[j] * lr[c, x, 4 + j : 20 + j]
@@ -397,8 +450,7 @@
         for c in range(C):
             av = lam[c, x] + out[c]
             nv = sec[c, x] - x_taps(lambda at: sec[c, at], x, fcs)
-            if isinstance(x, int):
-                side, at = (0, x) if x < W else (1, x - NX + W)
+            if rim:
                 arim[side, c, at], nrim[side, c, at] = av, nv
             else:
                 ab[c, x - W], nb[c, x - W] = av, nv
@@ -417,10 +469,15 @@
         move.wait()
 
 
-def edges(cx, cf, state, xe2, xo2, nrim, arim, nin, ain, nout, aout, nb, ab, sems):
-    evx = is_even("gx")
-    rx = [-DT * cx[TAPS - 1 - j] for j in range(TAPS)]
+def edges(cr, ct, cf, met, state, xe2, xo2, nrim, arim, nin, ain, nout, aout, nb, ab, sems):
+    mt = metric_tile(met)
+    evx, evr = is_even("gx"), is_even("row")
+    ev8 = evr[:8]
+    sub = iota((8, NT), 0)
+    fc = [-cf[TAPS - 1 - j] for j in range(TAPS)]
     fcs = [cf[j] for j in range(TAPS)]
+    rc = r_coefs([-DT * cr[TAPS - 1 - j] for j in range(TAPS)])
+    tc = t_pack_coefs([-DT * ct[TAPS - 1 - j] for j in range(TAPS)])
     starts = (0, NX - W)
     moves = []
 
@@ -434,21 +491,42 @@
     for side, at in enumerate(starts):
         low = side == 0
         mine, other = (xo2, xe2) if low else (xe2, xo2)
+
+        def got(n):
+            return jnp.where(evx, mine[n], other[n])
+
+        for c in range(C):
+            planes = [got(W * c + i) for i in range(W)]
+            for i in range(W):
+                nb[side, c, i] = nrim[side, c, i] - x_halo(planes, i, low, fcs)
+        put(nb, nout, side, 0)
+        b, g = [], []
+        for c in range(C):
+            one, two = got(W * C + 2 * c), got(W * C + 2 * c + 1)
+            rows, lanes = [], []
+            for p in range(2):
+                e, o = one[8 * p : 8 * p + 8], two[8 * p : 8 * p + 8]
+                lt, ht = jnp.where(ev8, o, e), jnp.where(ev8, e, o)
+                rows.append(jnp.where(sub < 4, lt, pltpu.roll(ht, 4, 0)))
+                rows.append(jnp.where(sub < 4, pltpu.roll(lt, 4, 0), ht))
+                block = (2 if low else 0) + p + 4 * (c % 4)
+                for xx in range(2):
+                    tile = got((W + 2) * C + 2 * (c // 4) + xx)
+                    lanes.append(pltpu.roll(tile, NT - 8 * block, 1) if block else tile)
+            bc, gc = [], []
+            for i in range(W):
+                row = x_halo(rows, i, low, fc)
+                bc.append(r_halo(row, row, 0, 1, rc))
+                lane = mt * x_halo(lanes, i, low, fc)
+                gc.append(t_unpack(t_halo_packed(lane, tc), 0))
+            b.append(bc)
+            g.append(gc)
         for i in range(W):
             q = [state[c, at + i] for c in range(C)]
-            a = []
-            for c in range(C):
-                planes = [jnp.where(evx, mine[C + c, h], other[C + c, h]) for h in range(W)]
-                a.append(x_halo(planes, i, low, rx))
-            out = pull_x(q, prims(q), a)
+            out = pull_rt(q, prims(q), [b[c][i] for c in range(C)], [g[c][i] for c in range(C)])
             for c in range(C):
                 ab[side, c, i] = arim[side, c, i] + out[c]
         put(ab, aout, side, 2)
-        for c in range(C):
-            planes = [jnp.where(evx, mine[c, i], other[c, i]) for i in range(W)]
-            for i in range(W):
-                nb[side, c, i] = nrim[side, c, i] - x_halo(planes, i, low, fcs)
-        put(nb, nout, side, 0)
     for move in moves:
         move.wait()
 
@@ -459,9 +537,12 @@
 
 LIMIT = pltpu.CompilerParams(vmem_limit_bytes=24 << 20)
 FULL = (C, NX, NR, NT)
-XPAY = (2 * C, W, NR, NT)
-RPAY = (C, NX // 2, 8, NT)
-TPAY = (C, 2, NR, NT)
+XPAY = (3 * C, W, NR, NT)
+XPAY2 = ((W + 2) * C + 4, NR, NT)
+RPAY = (C, NX + 4, 8, NT)
+TPAY = (4 * C + 4, NR, NT)
+RIM = (2, C, W, NR, NT)
+RIM_PAIRS = (0, 1, NX // 2 - 2, NX // 2 - 1)
 
 
 def call(kernel, smem, vmem, outs, scratch=()):
@@ -493,61 +574,54 @@
 
 
 def shards(state, seed, cx, cr, ct, cf, met):
-    shapes = [FULL, FULL, XPAY, XPAY, RPAY, RPAY, TPAY]
-    state, seed, xe, xo, re, ro, th = pl.pallas_call(
-        rims,
-        in_specs=[pl.BlockSpec(memory_space=pltpu.HBM)] * 2,
+    shapes = [FULL, FULL, RIM, XPAY, XPAY]
+    state, seed, prim, xe, xo = pl.pallas_call(
+        first,
+        in_specs=[SM] + [pl.BlockSpec(memory_space=pltpu.HBM)] * 2,
         out_specs=[VM] * len(shapes),
         out_shape=[pltpu.VMEM(s, F32) for s in shapes],
         scratch_shapes=[pltpu.SemaphoreType.DMA((2,))],
-        name="rims",
+        name="first",
         compiler_params=LIMIT,
-    )(*[pltpu.with_memory_space_constraint(v, pltpu.HBM) for v in (state, seed)])
-    th = across(th)
+    )(cf, *[pltpu.with_memory_space_constraint(v, pltpu.HBM) for v in (state, seed)])
     xe = swap(xe, "gx", 0)
     xo = swap(xo, "gx", 1)
+    plam, re, ro, th = call(second, [cf, met], [state, seed, prim], [FULL, RPAY, RPAY, TPAY])
+    th = across(th)
     re = swap(re, "row", 0)
     ro = swap(ro, "row", 1)
-    psec, plam = call(
-        own,
-        [cx, cr, ct, cf, met],
-        [state, seed],
-        [FULL, FULL],
-        [pltpu.VMEM(FULL, F32), WIDE_R] + SPLIT,
+    (psec,) = call(
+        own, [cx, cr, ct, met], [state], [FULL], [pltpu.VMEM(FULL, F32), WIDE_R] + SPLIT
     )
-    sec, lam, xe2, xo2, re2, ro2, th2 = call(
+    sec, lam, lamh, xe2, xo2 = call(
         join,
         [cx, cr, ct, cf, met],
-        [psec, plam, xe, xo, re, ro, th],
-        [FULL, FULL, XPAY, XPAY, RPAY, RPAY, TPAY],
+        [seed, psec, plam, xe, xo, re, ro, th],
+        [FULL, FULL, RIM, XPAY2, XPAY2],
     )
-    th2 = across(th2)
-    re2 = swap(re2, "row", 0)
-    ro2 = swap(ro2, "row", 1)
     xe2 = swap(xe2, "gx", 0)
     xo2 = swap(xo2, "gx", 1)
-    rim = (2, C, W, NR, NT)
     inner = pltpu.VMEM((C, NX - 2 * W, NR, NT), F32)
     whole = jax.ShapeDtypeStruct(FULL, F32)
     new, adj, nrim, arim = pl.pallas_call(
         finish,
-        in_specs=[SM] * 5 + [VM] * 6,
+        in_specs=[SM] * 5 + [VM] * 7,
         out_specs=[ANY, ANY, VM, VM],
-        out_shape=[whole, whole, pltpu.VMEM(rim, F32), pltpu.VMEM(rim, F32)],
+        out_shape=[whole, whole, pltpu.VMEM(RIM, F32), pltpu.VMEM(RIM, F32)],
         scratch_shapes=[WIDE_R] + SPLIT + [inner, inner, pltpu.SemaphoreType.DMA((2,))],
         name="finish",
         compiler_params=LIMIT,
-    )(cx, cr, ct, cf, met, *map(near, (state, sec, lam, re2, ro2, th2)))
+    )(cx, cr, ct, cf, met, *map(near, (state, sec, lam, lamh, re, ro, th)))
     return pl.pallas_call(
         edges,
-        in_specs=[SM] * 2 + [VM] * 5 + [ANY] * 2,
+        in_specs=[SM] * 4 + [VM] * 5 + [ANY] * 2,
         out_specs=[ANY, ANY],
         out_shape=[whole, whole],
-        scratch_shapes=[pltpu.VMEM(rim, F32), pltpu.VMEM(rim, F32), pltpu.SemaphoreType.DMA((4,))],
-        input_output_aliases={7: 0, 8: 1},
+        scratch_shapes=[pltpu.VMEM(RIM, F32), pltpu.VMEM(RIM, F32), pltpu.SemaphoreType.DMA((4,))],
+        input_output_aliases={9: 0, 10: 1},
         name="edges",
         compiler_params=LIMIT,
-    )(cx, cf, *map(near, (state, xe2, xo2, nrim, arim)), new, adj)
+    )(cr, ct, cf, met, *map(near, (state, xe2, xo2, nrim, arim)), new, adj)
 
 
 def solution(mesh):

time: 64.8 us -> 68.1 us (1.051)
  the two profiles are of different devices: /device:TPU:227 before, /device:TPU:450 now
where the time goes in v4:
time: 68.1 us; the launch traced here: 67.8 us
  Pallas kernels  23.8 us (35%)
  starting transfers between devices  22.1 us (32%)
  waiting for transfers between devices  20.3 us (30%)
  between operations  0.81 us (1%)
    ppermute x1, waiting for transfers between devices, across(): return lax.ppermute(value, 'th', [(0, 1), (1, 0)])  17.8 us
    ppermute x6, starting transfers between devices, swap(): return lax.ppermute(value, axis, pairs)  17 us
    pallas_call x3, Pallas kernels, call(): return run(*smem, *[near(v) for v in vmem])  9.19 us
    pallas_call x1, Pallas kernels, shards(): pl.pallas_call(finish, in_specs=[SM] * 5 + [VM] * 7, out_specs=[ANY, ANY,...  7.7 us
    ppermute x1, starting transfers between devices, across(): return lax.ppermute(value, 'th', [(0, 1), (1, 0)])  5.1 us
    pallas_call x1, Pallas kernels, shards(): pl.pallas_call(edges, in_specs=[SM] * 4 + [VM] * 5 + [ANY] * 2, out_specs...  4.62 us
    ppermute x6, waiting for transfers between devices, swap(): return lax.ppermute(value, axis, pairs)  2.54 us
    pallas_call x1, Pallas kernels, shards(): pl.pallas_call(first, in_specs=[SM] + [pl.BlockSpec(memory_space=pltpu.HB...  2.34 us
  transfers between devices with their start and end apart: 7, of which 2 were waited for; matrix products, arithmetic and copies ran while one was open for 0% of the time, Pallas kernels for 17%

profile of v4, /device:TPU:450, one launch (start us, length us, event | category | flops | bytes accessed | tf_op | source)
XLA Modules:
  0.0 67.8 jit_solution(2954091496913831574)
XLA Ops:
  0.6 0.0 copy-start
  0.6 0.0 copy-start.1
  0.7 0.7 copy-done.1
  1.3 2.3 %first.1 = (f32[5,32,16,128]{3,2,1,0:T(8,128)S(1)}, f32[5,32,16,128]{3,2,1,0:T(8,128)S(1)}, f32[2,5,4,16,128]{4,3,2,1,0:T(8,128)S(1)}, f32[15,4,16,128]{3,2,1,0:T(8,128)S(1)}, f32[15,4,16,128]{3,2,1,0:T(8,128)S(1)}) custom-call(f32[9]{0:T(128)S(1)} %copy-done.1, f32[5,32,16,128]{3,2,1,0:T(8,128)} %state_hbm.1, f32[5,32,16,128]{3,2,1,0:T(8,128)} %seed_hbm.1), custom_call_target="tpu_custom_call" | custom-call | tf_op jit(solution)/shard_map/first/pallas_call | solution.py:578
  3.6 0.0 copy-done
  3.7 0.0 copy-start.2
  3.7 0.0 copy-start.3
  3.7 0.0 copy-start.4
  3.7 2.7 %shard_map.87 = (f32[5,32,16,128]{3,2,1,0:T(8,128)S(1)}, f32[5,36,8,128]{3,2,1,0:T(8,128)S(1)}, f32[5,36,8,128]{3,2,1,0:T(8,128)S(1)}, f32[24,16,128]{2,1,0:T(8,128)S(1)}) custom-call(f32[9]{0:T(128)S(1)} %copy-done.1, f32[16]{0:T(128)S(1)} %copy-done, f32[5,32,16,128]{3,2,1,0:T(8,128)S(1)} %get-tuple-element.20.state, ...), custom_call_target="tpu_custom_call" | custom-call | tf_op jit(solution)/shard_map/pallas_call | solution.py:557
  6.4 1.9 %collective-permute-start.2 = (f32[5,36,8,128]{3,2,1,0:T(8,128)S(1)}, f32[5,36,8,128]{3,2,1,0:T(8,128)S(1)}, u32[]{:S(2)}, u32[]{:S(2)}) collective-permute-start(f32[5,36,8,128]{3,2,1,0:T(8,128)S(1)} %get-tuple-element.26), channel_id=1, source_target_pairs={{0,2},{2,0},{4,6},{6,4},{8,10},{10,8},{12,14},{14,12},{1,3},{3,1},... | collective-permute-start | bytes 2211848 | tf_op jit(solution)/shard_map/ppermute | solution.py:565
  8.3 2.5 %collective-permute-start.3 = (f32[5,36,8,128]{3,2,1,0:T(8,128)S(1)}, f32[5,36,8,128]{3,2,1,0:T(8,128)S(1)}, u32[]{:S(2)}, u32[]{:S(2)}) collective-permute-start(f32[5,36,8,128]{3,2,1,0:T(8,128)S(1)} %get-tuple-element.27), channel_id=1, source_target_pairs={{2,4},{4,2},{6,8},{8,6},{10,12},{12,10},{3,5},{5,3},{7,9},{9,7},{1... | collective-permute-start | bytes 2211848 | tf_op jit(solution)/shard_map/ppermute | solution.py:565
  10.9 3.5 %collective-permute-start = (f32[15,4,16,128]{3,2,1,0:T(8,128)S(1)}, f32[15,4,16,128]{3,2,1,0:T(8,128)S(1)}, u32[]{:S(2)}, u32[]{:S(2)}) collective-permute-start(f32[15,4,16,128]{3,2,1,0:T(8,128)S(1)} %get-tuple-element.24), channel_id=1, source_target_pairs={{0,16},{16,0},{32,48},{48,32},{64,80},{80,64},{96,112},{112,96},{1... | collective-permute-start | bytes 1474568 | tf_op jit(solution)/shard_map/ppermute | solution.py:565
  14.3 2.8 %collective-permute-start.1 = (f32[15,4,16,128]{3,2,1,0:T(8,128)S(1)}, f32[15,4,16,128]{3,2,1,0:T(8,128)S(1)}, u32[]{:S(2)}, u32[]{:S(2)}) collective-permute-start(f32[15,4,16,128]{3,2,1,0:T(8,128)S(1)} %get-tuple-element.25), channel_id=1, source_target_pairs={{16,32},{32,16},{48,64},{64,48},{80,96},{96,80},{112,128},{128,112... | collective-permute-start | bytes 1474568 | tf_op jit(solution)/shard_map/ppermute | solution.py:565
  17.2 5.1 %collective-permute-start.4 = (f32[24,16,128]{2,1,0:T(8,128)S(1)}, f32[24,16,128]{2,1,0:T(8,128)S(1)}, u32[]{:S(2)}, u32[]{:S(2)}) collective-permute-start(f32[24,16,128]{2,1,0:T(8,128)S(1)} %get-tuple-element.28), channel_id=1, source_target_pairs={{0,1},{1,0},{2,3},{3,2},{4,5},{5,4},{6,7},{7,6},{8,9},{9,8},{10,11... | collective-permute-start | bytes 589832 | tf_op jit(solution)/shard_map/ppermute | solution.py:569
  22.3 0.0 copy-done.2
  22.3 0.0 copy-done.3
  22.3 0.0 copy-done.4
  22.3 4.0 %shard_map.86.psec = f32[5,32,16,128]{3,2,1,0:T(8,128)S(1)} custom-call(f32[9]{0:T(128)S(1)} %copy-done.4, f32[9]{0:T(128)S(1)} %copy-done.2, f32[9]{0:T(128)S(1)} %copy-done.3, f32[16]{0:T(128)S(1)} %copy-done, f32[5,32,16,128]{3,2,1,0:T(8,128)S(1)} %get-tuple-element.20.state), custom_call_target="tpu_custom_call" | custom-call | tf_op jit(solution)/shard_map/pallas_call | solution.py:557
  26.3 17.8 %collective-permute-done.4.th = f32[24,16,128]{2,1,0:T(8,128)S(1)} collective-permute-done((f32[24,16,128]{2,1,0:T(8,128)S(1)}, f32[24,16,128]{2,1,0:T(8,128)S(1)}, u32[]{:S(2)}, u32[]{:S(2)}) %collective-permute-start.4) | collective-permute-done | bytes 196640 | tf_op jit(solution)/shard_map/ppermute | solution.py:569
  44.0 0.0 collective-permute-done.xe
  44.0 0.0 collective-permute-done.1.xo
  44.1 0.0 collective-permute-done.2.re
  44.1 0.0 collective-permute-done.3.ro
  44.1 2.5 %shard_map.88 = (f32[5,32,16,128]{3,2,1,0:T(8,128)S(1)}, f32[5,32,16,128]{3,2,1,0:T(8,128)S(1)}, f32[2,5,4,16,128]{4,3,2,1,0:T(8,128)S(1)}, f32[34,16,128]{2,1,0:T(8,128)S(1)}, f32[34,16,128]{2,1,0:T(8,128)S(1)}) custom-call(f32[9]{0:T(128)S(1)} %copy-done.4, f32[9]{0:T(128)S(1)} %copy-done.2, f32[9]{0:T(128)S(1)} %copy-done.3, f32[9]{0:T(128)S(1)} %copy-done.1, ...), custom_call_target="tpu_custom_call" | custom-call | tf_op jit(solution)/shard_map/pallas_call | solution.py:557
  46.6 2.0 %collective-permute-start.5 = (f32[34,16,128]{2,1,0:T(8,128)S(1)}, f32[34,16,128]{2,1,0:T(8,128)S(1)}, u32[]{:S(2)}, u32[]{:S(2)}) collective-permute-start(f32[34,16,128]{2,1,0:T(8,128)S(1)} %get-tuple-element.29), channel_id=1, source_target_pairs={{0,16},{16,0},{32,48},{48,32},{64,80},{80,64},{96,112},{112,96},{1... | collective-permute-start | bytes 835592 | tf_op jit(solution)/shard_map/ppermute | solution.py:565
  48.7 4.2 %collective-permute-start.6 = (f32[34,16,128]{2,1,0:T(8,128)S(1)}, f32[34,16,128]{2,1,0:T(8,128)S(1)}, u32[]{:S(2)}, u32[]{:S(2)}) collective-permute-start(f32[34,16,128]{2,1,0:T(8,128)S(1)} %get-tuple-element.30), channel_id=1, source_target_pairs={{16,32},{32,16},{48,64},{64,48},{80,96},{96,80},{112,128},{128,112... | collective-permute-start | bytes 835592 | tf_op jit(solution)/shard_map/ppermute | solution.py:565
  52.9 7.7 %finish.1 = (f32[5,32,16,128]{3,2,1,0:T(8,128)}, f32[5,32,16,128]{3,2,1,0:T(8,128)}, f32[2,5,4,16,128]{4,3,2,1,0:T(8,128)S(1)}, f32[2,5,4,16,128]{4,3,2,1,0:T(8,128)S(1)}) custom-call(f32[9]{0:T(128)S(1)} %copy-done.4, f32[9]{0:T(128)S(1)} %copy-done.2, f32[9]{0:T(128)S(1)} %copy-done.3, f32[9]{0:T(128)S(1)} %copy-done.1, f32[16]{0:T(128)S(1)} %copy-done, ...), custom_call_target="tpu_custom_call" | custom-call | tf_op jit(solution)/shard_map/finish/pallas_call | solution.py:606
  60.6 2.5 %collective-permute-done.5.xe2 = f32[34,16,128]{2,1,0:T(8,128)S(1)} collective-permute-done((f32[34,16,128]{2,1,0:T(8,128)S(1)}, f32[34,16,128]{2,1,0:T(8,128)S(1)}, u32[]{:S(2)}, u32[]{:S(2)}) %collective-permute-start.5) | collective-permute-done | bytes 278560 | tf_op jit(solution)/shard_map/ppermute | solution.py:565
  63.1 0.0 collective-permute-done.6.xo2
  63.1 4.6 %edges.1 = (f32[5,32,16,128]{3,2,1,0:T(8,128)}, f32[5,32,16,128]{3,2,1,0:T(8,128)}) custom-call(f32[9]{0:T(128)S(1)} %copy-done.2, f32[9]{0:T(128)S(1)} %copy-done.3, f32[9]{0:T(128)S(1)} %copy-done.1, f32[16]{0:T(128)S(1)} %copy-done, f32[5,32,16,128]{3,2,1,0:T(8,128)S(1)} %get-tuple-element.20.state, ...), custom_call_target="tpu_custom_call", output_to_operand_aliasing={{0}: (9, {}), {1}: (10, {})} | custom-call | tf_op jit(solution)/shard_map/edges/pallas_call | solution.py:615
Async XLA Ops:
  0.6 3.0 %copy-start = (f32[16]{0:T(128)S(1)}, f32[16]{0:T(128)}, u32[]{:S(2)}) copy-start(f32[16]{0:T(128)} %met.9) | copy-start | bytes 196
  0.6 0.7 copy-start.1
  3.7 18.6 %copy-start.2 = (f32[9]{0:T(128)S(1)}, f32[9]{0:T(128)}, u32[]{:S(2)}) copy-start(f32[9]{0:T(128)} %cr.7) | copy-start | bytes 112
  3.7 18.6 %copy-start.3 = (f32[9]{0:T(128)S(1)}, f32[9]{0:T(128)}, u32[]{:S(2)}) copy-start(f32[9]{0:T(128)} %ct.7) | copy-start | bytes 112
  3.7 18.6 %copy-start.4 = (f32[9]{0:T(128)S(1)}, f32[9]{0:T(128)}, u32[]{:S(2)}) copy-start(f32[9]{0:T(128)} %cx.5) | copy-start | bytes 112
  6.4 37.7 %collective-permute-start.2 = (f32[5,36,8,128]{3,2,1,0:T(8,128)S(1)}, f32[5,36,8,128]{3,2,1,0:T(8,128)S(1)}, u32[]{:S(2)}, u32[]{:S(2)}) collective-permute-start(f32[5,36,8,128]{3,2,1,0:T(8,128)S(1)} %get-tuple-element.26), channel_id=1, source_target_pairs={{0,2},{2,0},{4,6},{6,4},{8,10},{10,8},{12,14},{14,12},{1,3},{3,1},... | collective-permute-start | bytes 2211848 | tf_op jit(solution)/shard_map/ppermute | solution.py:565
  8.3 35.8 %collective-permute-start.3 = (f32[5,36,8,128]{3,2,1,0:T(8,128)S(1)}, f32[5,36,8,128]{3,2,1,0:T(8,128)S(1)}, u32[]{:S(2)}, u32[]{:S(2)}) collective-permute-start(f32[5,36,8,128]{3,2,1,0:T(8,128)S(1)} %get-tuple-element.27), channel_id=1, source_target_pairs={{2,4},{4,2},{6,8},{8,6},{10,12},{12,10},{3,5},{5,3},{7,9},{9,7},{1... | collective-permute-start | bytes 2211848 | tf_op jit(solution)/shard_map/ppermute | solution.py:565
  10.9 33.2 %collective-permute-start = (f32[15,4,16,128]{3,2,1,0:T(8,128)S(1)}, f32[15,4,16,128]{3,2,1,0:T(8,128)S(1)}, u32[]{:S(2)}, u32[]{:S(2)}) collective-permute-start(f32[15,4,16,128]{3,2,1,0:T(8,128)S(1)} %get-tuple-element.24), channel_id=1, source_target_pairs={{0,16},{16,0},{32,48},{48,32},{64,80},{80,64},{96,112},{112,96},{1... | collective-permute-start | bytes 1474568 | tf_op jit(solution)/shard_map/ppermute | solution.py:565
  14.3 29.7 %collective-permute-start.1 = (f32[15,4,16,128]{3,2,1,0:T(8,128)S(1)}, f32[15,4,16,128]{3,2,1,0:T(8,128)S(1)}, u32[]{:S(2)}, u32[]{:S(2)}) collective-permute-start(f32[15,4,16,128]{3,2,1,0:T(8,128)S(1)} %get-tuple-element.25), channel_id=1, source_target_pairs={{16,32},{32,16},{48,64},{64,48},{80,96},{96,80},{112,128},{128,112... | collective-permute-start | bytes 1474568 | tf_op jit(solution)/shard_map/ppermute | solution.py:565
  17.2 26.9 %collective-permute-start.4 = (f32[24,16,128]{2,1,0:T(8,128)S(1)}, f32[24,16,128]{2,1,0:T(8,128)S(1)}, u32[]{:S(2)}, u32[]{:S(2)}) collective-permute-start(f32[24,16,128]{2,1,0:T(8,128)S(1)} %get-tuple-element.28), channel_id=1, source_target_pairs={{0,1},{1,0},{2,3},{3,2},{4,5},{5,4},{6,7},{7,6},{8,9},{9,8},{10,11... | collective-permute-start | bytes 589832 | tf_op jit(solution)/shard_map/ppermute | solution.py:569
  46.6 16.5 %collective-permute-start.5 = (f32[34,16,128]{2,1,0:T(8,128)S(1)}, f32[34,16,128]{2,1,0:T(8,128)S(1)}, u32[]{:S(2)}, u32[]{:S(2)}) collective-permute-start(f32[34,16,128]{2,1,0:T(8,128)S(1)} %get-tuple-element.29), channel_id=1, source_target_pairs={{0,16},{16,0},{32,48},{48,32},{64,80},{80,64},{96,112},{112,96},{1... | collective-permute-start | bytes 835592 | tf_op jit(solution)/shard_map/ppermute | solution.py:565
  48.7 14.5 %collective-permute-start.6 = (f32[34,16,128]{2,1,0:T(8,128)S(1)}, f32[34,16,128]{2,1,0:T(8,128)S(1)}, u32[]{:S(2)}, u32[]{:S(2)}) collective-permute-start(f32[34,16,128]{2,1,0:T(8,128)S(1)} %get-tuple-element.30), channel_id=1, source_target_pairs={{16,32},{32,16},{48,64},{64,48},{80,96},{96,80},{112,128},{128,112... | collective-permute-start | bytes 835592 | tf_op jit(solution)/shard_map/ppermute | solution.py:565

commit v5 on v4

--- a/solution.py
+++ b/solution.py
@@ -1,5 +1,3 @@
-import functools
-
 import jax
 import jax.numpy as jnp
 from jax import lax
@@ -238,13 +236,15 @@
     return jnp.where(even, NX - W, 0), jnp.where(even, 0, NX - W)
 
 
-def first(cf, state_hbm, seed_hbm, state, seed, prim, xe, xo, sems):
+def first(cf_hbm, state_hbm, seed_hbm, state, seed, prim, xe, xo, cf, sems):
     moves = [
         pltpu.make_async_copy(seed_hbm, seed, sems.at[0]),
         pltpu.make_async_copy(state_hbm, state, sems.at[1]),
+        pltpu.make_async_copy(cf_hbm, cf, sems.at[2]),
     ]
     for move in moves:
         move.start()
+    moves[2].wait()
     fc = [-cf[TAPS - 1 - j] for j in range(TAPS)]
     moves[0].wait()
     for side, base in enumerate((0, NX - W)):
@@ -300,7 +300,7 @@
             at = NX + n
             re[c, at], ro[c, at] = r_pack(seed[c, 2 * k], seed[c, 2 * k + 1], even)
             for xx in range(2):
-                t_pack_one(th, 4 * C + 2 * (c // 4) + xx, seed[c, 2 * k + xx], n + 4 * (c % 4))
+                t_pack_one(th, 4 * C + 2 * (n // 2) + xx, seed[c, 2 * k + xx], n % 2 + 2 * c)
 
 
 def own(cx, cr, ct, met, state, psec, fx, fr, hi, lo, tt):
@@ -334,7 +334,7 @@
     over_planes(plane)
 
 
-def join(cx, cr, ct, cf, met, seed, psec, plam, xe, xo, re, ro, th, sec, lam, lamh, xe2, xo2):
+def join(cx, cr, ct, cf, met, seed, psec, plam, xe, xo, re, ro, th, srim, lrim, lamh, xe2, xo2):
     mt = metric_tile(met)
     evx, evr = is_even("gx"), is_even("row")
     fc = [-cf[TAPS - 1 - j] for j in range(TAPS)]
@@ -352,49 +352,44 @@
             flux, seeds, share = halo(c), halo(C + c), halo(2 * C + c)
             mine = [seed[c, base + i] for i in range(W)]
             for i in range(W):
-                sec[c, base + i] = psec[c, base + i] + x_halo(flux, i, low, xc)
-                lam[c, base + i] = plam[c, base + i] + x_halo(seeds, i, low, fc)
+                srim[side, c, i] = psec[c, base + i] + x_halo(flux, i, low, xc)
+                lrim[side, c, i] = plam[c, base + i] + x_halo(seeds, i, low, fc)
                 value = share[i] + x_halo(mine, i, not low, fc)
                 lamh[side, c, i] = jnp.where(has[side], value, 0.0)
+    share = rt_share(cr, ct, mt, evr[:8], re, ro, th)
+    for n, k in enumerate(RIM_PAIRS):
+        for c in range(C):
+            for xx, value in enumerate(share(c, k)):
+                srim[n // 2, c, 2 * (n % 2) + xx] += value
+    even = parity("gx") == 0
+    sides = jnp.where(even, 1, 0), jnp.where(even, 0, 1)
+    for side, out in zip(sides, (xe2, xo2)):
+        for c in range(C):
+            for i in range(W):
+                out[W * c + i] = srim[side, c, i]
+            for eo, src in enumerate((re, ro)):
+                for p in range(2):
+                    out[W * C + 2 * c + eo, 8 * p : 8 * p + 8] = src[c, NX + 2 * side + p]
+        for xx in range(2):
+            out[(W + 2) * C + xx] = th[4 * C + 2 * side + xx]
+
+
+def rt_share(cr, ct, mt, ev8, re, ro, th):
     rc = r_coefs([-DT * cr[j] for j in range(TAPS)])
     tc = t_pack_coefs([-DT * ct[j] for j in range(TAPS)])
     packed = [[mt * t_halo_packed(th[2 * c + xx], tc) for xx in range(2)] for c in range(C)]
-    ev8 = evr[:8]
-
-    def pair(k, s_ref, inside):
-        for c in range(C):
-            a, b = re[c, k], ro[c, k]
-            low, high = jnp.where(ev8, b, a), jnp.where(ev8, a, b)
-            for xx in range(2):
-                x = 2 * k + xx
-                share = r_halo(low, high, xx, xx, rc) + t_unpack(packed[c][xx], k)
-                sec[c, x] = s_ref[c, x] + share
-                if inside:
-                    lam[c, x] = plam[c, x]
-
-    def send():
-        starts = rim_starts()
-        even = parity("gx") == 0
-        corners = NX + jnp.where(even, 2, 0), NX + jnp.where(even, 0, 2)
-        for start, corner, out in zip(starts, corners, (xe2, xo2)):
-            for c in range(C):
-                for i in range(W):
-                    out[W * c + i] = sec[c, start + i]
-                for eo, src in enumerate((re, ro)):
-                    for p in range(2):
-                        out[W * C + 2 * c + eo, 8 * p : 8 * p + 8] = src[c, corner + p]
-            for t in range(4):
-                out[(W + 2) * C + t] = th[4 * C + t]
-
-    loop(0, 2, functools.partial(pair, s_ref=sec, inside=False))
-    loop(14, 16, functools.partial(pair, s_ref=sec, inside=False))
-    send()
-    loop(2, 14, functools.partial(pair, s_ref=psec, inside=True))
+
+    def share(c, k):
+        a, b = re[c, k], ro[c, k]
+        low, high = jnp.where(ev8, b, a), jnp.where(ev8, a, b)
+        return [r_halo(low, high, xx, xx, rc) + t_unpack(packed[c][xx], k) for xx in range(2)]
+
+    return share
 
 
 def finish(
-    cx, cr, ct, cf, met, state, sec, lam, lamh, re, ro, th,
-    new, adj, nrim, arim, lr, hi, lo, tt, nb, ab, sems,
+    cx, cr, ct, cf, met, state, psec, plam, srim, lrim, lamh, re, ro, th,
+    new, adj, nrim, arim, sec, lam, pk, lr, hi, lo, tt, nb, ab, sems,
 ):
     mt = metric_tile(met)
     evr = is_even("row")
@@ -403,7 +398,22 @@
     rr = [-DT * cr[TAPS - 1 - j] for j in range(TAPS)]
     rt = [-DT * ct[TAPS - 1 - j] for j in range(TAPS)]
     tc = t_pack_coefs(rt)
-    packed = [[t_halo_packed(th[2 * C + 2 * c + xx], tc) for xx in range(2)] for c in range(C)]
+    for c in range(C):
+        for xx in range(2):
+            pk[xx, c] = t_halo_packed(th[2 * C + 2 * c + xx], tc)
+        for side, base in enumerate((0, NX - W)):
+            for i in range(W):
+                sec[c, base + i], lam[c, base + i] = srim[side, c, i], lrim[side, c, i]
+    share = rt_share(cr, ct, mt, ev8, re, ro, th)
+
+    def inner(k):
+        for c in range(C):
+            for xx, value in enumerate(share(c, k)):
+                x = 2 * k + xx
+                sec[c, x] = psec[c, x] + value
+                lam[c, x] = plam[c, x]
+
+    loop(2, 14, inner)
 
     def fill(k):
         for c in range(C):
@@ -421,12 +431,6 @@
     loop(0, NX // 2, fill)
     t_own(hi, lo, rt, tt)
 
-    def add(k):
-        for c in range(C):
-            for xx in range(2):
-                tt[2 * k + xx, c] += t_unpack(packed[c][xx], k)
-
-    loop(0, NX // 2, add)
     fcs = [cf[j] for j in range(TAPS)]
 
     def plane(x):
@@ -445,7 +449,7 @@
                 term = rr[j] * lr[c, x, 4 + j : 20 + j]
                 acc = term if acc is None else acc + term
             b.append(acc)
-            g.append(tt[x, c])
+            g.append(tt[x, c] + t_unpack(pk[x % 2, c], x // 2))
         out = pull(q, pr, a, b, g)
         for c in range(C):
             av = lam[c, x] + out[c]
@@ -469,7 +473,7 @@
         move.wait()
 
 
-def edges(cr, ct, cf, met, state, xe2, xo2, nrim, arim, nin, ain, nout, aout, nb, ab, sems):
+def edges(cr, ct, cf, met, state, xe2, xo2, nrim, arim, nin, ain, nout, aout, nb, ab, bs, gs, sems):
     mt = metric_tile(met)
     evx, evr = is_even("gx"), is_even("row")
     ev8 = evr[:8]
@@ -500,7 +504,7 @@
             for i in range(W):
                 nb[side, c, i] = nrim[side, c, i] - x_halo(planes, i, low, fcs)
         put(nb, nout, side, 0)
-        b, g = [], []
+        turned = [t_halo_packed(got((W + 2) * C + xx), tc) for xx in range(2)]
         for c in range(C):
             one, two = got(W * C + 2 * c), got(W * C + 2 * c + 1)
             rows, lanes = [], []
@@ -509,21 +513,15 @@
                 lt, ht = jnp.where(ev8, o, e), jnp.where(ev8, e, o)
                 rows.append(jnp.where(sub < 4, lt, pltpu.roll(ht, 4, 0)))
                 rows.append(jnp.where(sub < 4, pltpu.roll(lt, 4, 0), ht))
-                block = (2 if low else 0) + p + 4 * (c % 4)
                 for xx in range(2):
-                    tile = got((W + 2) * C + 2 * (c // 4) + xx)
-                    lanes.append(pltpu.roll(tile, NT - 8 * block, 1) if block else tile)
-            bc, gc = [], []
+                    lanes.append(mt * t_unpack(turned[xx], p + 2 * c))
             for i in range(W):
                 row = x_halo(rows, i, low, fc)
-                bc.append(r_halo(row, row, 0, 1, rc))
-                lane = mt * x_halo(lanes, i, low, fc)
-                gc.append(t_unpack(t_halo_packed(lane, tc), 0))
-            b.append(bc)
-            g.append(gc)
+                bs[c, i] = r_halo(row, row, 0, 1, rc)
+                gs[c, i] = x_halo(lanes, i, low, fc)
         for i in range(W):
             q = [state[c, at + i] for c in range(C)]
-            out = pull_rt(q, prims(q), [b[c][i] for c in range(C)], [g[c][i] for c in range(C)])
+            out = pull_rt(q, prims(q), [bs[c, i] for c in range(C)], [gs[c, i] for c in range(C)])
             for c in range(C):
                 ab[side, c, i] = arim[side, c, i] + out[c]
         put(ab, aout, side, 2)
@@ -538,7 +536,7 @@
 LIMIT = pltpu.CompilerParams(vmem_limit_bytes=24 << 20)
 FULL = (C, NX, NR, NT)
 XPAY = (3 * C, W, NR, NT)
-XPAY2 = ((W + 2) * C + 4, NR, NT)
+XPAY2 = ((W + 2) * C + 2, NR, NT)
 RPAY = (C, NX + 4, 8, NT)
 TPAY = (4 * C + 4, NR, NT)
 RIM = (2, C, W, NR, NT)
@@ -577,13 +575,13 @@
     shapes = [FULL, FULL, RIM, XPAY, XPAY]
     state, seed, prim, xe, xo = pl.pallas_call(
         first,
-        in_specs=[SM] + [pl.BlockSpec(memory_space=pltpu.HBM)] * 2,
+        in_specs=[pl.BlockSpec(memory_space=pltpu.HBM)] * 3,
         out_specs=[VM] * len(shapes),
         out_shape=[pltpu.VMEM(s, F32) for s in shapes],
-        scratch_shapes=[pltpu.SemaphoreType.DMA((2,))],
+        scratch_shapes=[pltpu.SMEM((TAPS,), F32), pltpu.SemaphoreType.DMA((3,))],
         name="first",
         compiler_params=LIMIT,
-    )(cf, *[pltpu.with_memory_space_constraint(v, pltpu.HBM) for v in (state, seed)])
+    )(*[pltpu.with_memory_space_constraint(v, pltpu.HBM) for v in (cf, state, seed)])
     xe = swap(xe, "gx", 0)
     xo = swap(xo, "gx", 1)
     plam, re, ro, th = call(second, [cf, met], [state, seed, prim], [FULL, RPAY, RPAY, TPAY])
@@ -593,31 +591,36 @@
     (psec,) = call(
         own, [cx, cr, ct, met], [state], [FULL], [pltpu.VMEM(FULL, F32), WIDE_R] + SPLIT
     )
-    sec, lam, lamh, xe2, xo2 = call(
+    srim, lrim, lamh, xe2, xo2 = call(
         join,
         [cx, cr, ct, cf, met],
         [seed, psec, plam, xe, xo, re, ro, th],
-        [FULL, FULL, RIM, XPAY2, XPAY2],
+        [RIM, RIM, RIM, XPAY2, XPAY2],
     )
     xe2 = swap(xe2, "gx", 0)
     xo2 = swap(xo2, "gx", 1)
+    full = pltpu.VMEM(FULL, F32)
     inner = pltpu.VMEM((C, NX - 2 * W, NR, NT), F32)
     whole = jax.ShapeDtypeStruct(FULL, F32)
     new, adj, nrim, arim = pl.pallas_call(
         finish,
-        in_specs=[SM] * 5 + [VM] * 7,
+        in_specs=[SM] * 5 + [VM] * 9,
         out_specs=[ANY, ANY, VM, VM],
         out_shape=[whole, whole, pltpu.VMEM(RIM, F32), pltpu.VMEM(RIM, F32)],
-        scratch_shapes=[WIDE_R] + SPLIT + [inner, inner, pltpu.SemaphoreType.DMA((2,))],
+        scratch_shapes=[full, full, pltpu.VMEM((2, C, NR, NT), F32), WIDE_R]
+        + SPLIT
+        + [inner, inner, pltpu.SemaphoreType.DMA((2,))],
         name="finish",
         compiler_params=LIMIT,
-    )(cx, cr, ct, cf, met, *map(near, (state, sec, lam, lamh, re, ro, th)))
+    )(cx, cr, ct, cf, met, *map(near, (state, psec, plam, srim, lrim, lamh, re, ro, th)))
     return pl.pallas_call(
         edges,
         in_specs=[SM] * 4 + [VM] * 5 + [ANY] * 2,
         out_specs=[ANY, ANY],
         out_shape=[whole, whole],
-        scratch_shapes=[pltpu.VMEM(RIM, F32), pltpu.VMEM(RIM, F32), pltpu.SemaphoreType.DMA((4,))],
+        scratch_shapes=[pltpu.VMEM(RIM, F32)] * 2
+        + [pltpu.VMEM((C, W, NR, NT), F32)] * 2
+        + [pltpu.SemaphoreType.DMA((4,))],
         input_output_aliases={9: 0, 10: 1},
         name="edges",
         compiler_params=LIMIT,

time: 68.1 us -> 62.1 us (0.912)
  the two profiles are of different devices: /device:TPU:450 before, /device:TPU:322 now
where the time goes in v5:
time: 62.1 us; the launch traced here: 61.8 us
  starting transfers between devices  22.1 us (36%)
  waiting for transfers between devices  19.8 us (32%)
  Pallas kernels  19 us (31%)
  between operations  0.82 us (1%)
    ppermute x1, waiting for transfers between devices, across(): return lax.ppermute(value, 'th', [(0, 1), (1, 0)])  17.8 us
    ppermute x6, starting transfers between devices, swap(): return lax.ppermute(value, axis, pairs)  17 us
    pallas_call x3, Pallas kernels, call(): return run(*smem, *[near(v) for v in vmem])  7.84 us
    pallas_call x1, Pallas kernels, shards(): pl.pallas_call(finish, in_specs=[SM] * 5 + [VM] * 9, out_specs=[ANY, ANY,...  7.45 us
    ppermute x1, starting transfers between devices, across(): return lax.ppermute(value, 'th', [(0, 1), (1, 0)])  5.1 us
    ppermute x6, waiting for transfers between devices, swap(): return lax.ppermute(value, axis, pairs)  2.09 us
    pallas_call x1, Pallas kernels, shards(): pl.pallas_call(edges, in_specs=[SM] * 4 + [VM] * 5 + [ANY] * 2, out_specs...  1.87 us
    pallas_call x1, Pallas kernels, shards(): pl.pallas_call(first, in_specs=[pl.BlockSpec(memory_space=pltpu.HBM)] * 3...  1.83 us
  transfers between devices with their start and end apart: 7, of which 2 were waited for; matrix products, arithmetic and copies ran while one was open for 0% of the time, Pallas kernels for 19%

profile of v5, /device:TPU:322, one launch (start us, length us, event | category | flops | bytes accessed | tf_op | source)
XLA Modules:
  0.0 61.8 jit_solution(13626106050368764681)
XLA Ops:
  0.6 0.0 copy-start.1
  0.6 0.0 copy-start
  0.7 1.8 %first.1 = (f32[5,32,16,128]{3,2,1,0:T(8,128)S(1)}, f32[5,32,16,128]{3,2,1,0:T(8,128)S(1)}, f32[2,5,4,16,128]{4,3,2,1,0:T(8,128)S(1)}, f32[15,4,16,128]{3,2,1,0:T(8,128)S(1)}, f32[15,4,16,128]{3,2,1,0:T(8,128)S(1)}) custom-call(f32[9]{0:T(128)} %cf.7, f32[5,32,16,128]{3,2,1,0:T(8,128)} %state_hbm.1, f32[5,32,16,128]{3,2,1,0:T(8,128)} %seed_hbm.1), custom_call_target="tpu_custom_call" | custom-call | tf_op jit(solution)/shard_map/first/pallas_call | solution.py:576
  2.5 0.0 copy-done.1
  2.5 0.0 copy-done
  2.5 0.0 copy-start.2
  2.5 0.0 copy-start.3
  2.5 0.0 copy-start.4
  2.5 2.7 %shard_map.87 = (f32[5,32,16,128]{3,2,1,0:T(8,128)S(1)}, f32[5,36,8,128]{3,2,1,0:T(8,128)S(1)}, f32[5,36,8,128]{3,2,1,0:T(8,128)S(1)}, f32[24,16,128]{2,1,0:T(8,128)S(1)}) custom-call(f32[9]{0:T(128)S(1)} %copy-done.1, f32[16]{0:T(128)S(1)} %copy-done, f32[5,32,16,128]{3,2,1,0:T(8,128)S(1)} %get-tuple-element.20.state, ...), custom_call_target="tpu_custom_call" | custom-call | tf_op jit(solution)/shard_map/pallas_call | solution.py:555
  5.2 1.9 %collective-permute-start.2 = (f32[5,36,8,128]{3,2,1,0:T(8,128)S(1)}, f32[5,36,8,128]{3,2,1,0:T(8,128)S(1)}, u32[]{:S(2)}, u32[]{:S(2)}) collective-permute-start(f32[5,36,8,128]{3,2,1,0:T(8,128)S(1)} %get-tuple-element.26), channel_id=1, source_target_pairs={{0,2},{2,0},{4,6},{6,4},{8,10},{10,8},{12,14},{14,12},{1,3},{3,1},... | collective-permute-start | bytes 2211848 | tf_op jit(solution)/shard_map/ppermute | solution.py:563
  7.2 2.5 %collective-permute-start.3 = (f32[5,36,8,128]{3,2,1,0:T(8,128)S(1)}, f32[5,36,8,128]{3,2,1,0:T(8,128)S(1)}, u32[]{:S(2)}, u32[]{:S(2)}) collective-permute-start(f32[5,36,8,128]{3,2,1,0:T(8,128)S(1)} %get-tuple-element.27), channel_id=1, source_target_pairs={{2,4},{4,2},{6,8},{8,6},{10,12},{12,10},{3,5},{5,3},{7,9},{9,7},{1... | collective-permute-start | bytes 2211848 | tf_op jit(solution)/shard_map/ppermute | solution.py:563
  9.7 3.5 %collective-permute-start = (f32[15,4,16,128]{3,2,1,0:T(8,128)S(1)}, f32[15,4,16,128]{3,2,1,0:T(8,128)S(1)}, u32[]{:S(2)}, u32[]{:S(2)}) collective-permute-start(f32[15,4,16,128]{3,2,1,0:T(8,128)S(1)} %get-tuple-element.24), channel_id=1, source_target_pairs={{0,16},{16,0},{32,48},{48,32},{64,80},{80,64},{96,112},{112,96},{1... | collective-permute-start | bytes 1474568 | tf_op jit(solution)/shard_map/ppermute | solution.py:563
  13.2 2.8 %collective-permute-start.1 = (f32[15,4,16,128]{3,2,1,0:T(8,128)S(1)}, f32[15,4,16,128]{3,2,1,0:T(8,128)S(1)}, u32[]{:S(2)}, u32[]{:S(2)}) collective-permute-start(f32[15,4,16,128]{3,2,1,0:T(8,128)S(1)} %get-tuple-element.25), channel_id=1, source_target_pairs={{16,32},{32,16},{48,64},{64,48},{80,96},{96,80},{112,128},{128,112... | collective-permute-start | bytes 1474568 | tf_op jit(solution)/shard_map/ppermute | solution.py:563
  16.0 5.1 %collective-permute-start.4 = (f32[24,16,128]{2,1,0:T(8,128)S(1)}, f32[24,16,128]{2,1,0:T(8,128)S(1)}, u32[]{:S(2)}, u32[]{:S(2)}) collective-permute-start(f32[24,16,128]{2,1,0:T(8,128)S(1)} %get-tuple-element.28), channel_id=1, source_target_pairs={{0,1},{1,0},{2,3},{3,2},{4,5},{5,4},{6,7},{7,6},{8,9},{9,8},{10,11... | collective-permute-start | bytes 589832 | tf_op jit(solution)/shard_map/ppermute | solution.py:567
  21.1 0.0 copy-done.2
  21.1 0.0 copy-done.3
  21.1 0.0 copy-done.4
  21.1 4.0 %shard_map.86.psec = f32[5,32,16,128]{3,2,1,0:T(8,128)S(1)} custom-call(f32[9]{0:T(128)S(1)} %copy-done.4, f32[9]{0:T(128)S(1)} %copy-done.2, f32[9]{0:T(128)S(1)} %copy-done.3, f32[16]{0:T(128)S(1)} %copy-done, f32[5,32,16,128]{3,2,1,0:T(8,128)S(1)} %get-tuple-element.20.state), custom_call_target="tpu_custom_call" | custom-call | tf_op jit(solution)/shard_map/pallas_call | solution.py:555
  25.1 17.8 %collective-permute-done.4.th = f32[24,16,128]{2,1,0:T(8,128)S(1)} collective-permute-done((f32[24,16,128]{2,1,0:T(8,128)S(1)}, f32[24,16,128]{2,1,0:T(8,128)S(1)}, u32[]{:S(2)}, u32[]{:S(2)}) %collective-permute-start.4) | collective-permute-done | bytes 196640 | tf_op jit(solution)/shard_map/ppermute | solution.py:567
  42.9 0.0 collective-permute-done.xe
  42.9 0.0 collective-permute-done.1.xo
  42.9 0.0 collective-permute-done.2.re
  42.9 0.0 collective-permute-done.3.ro
  42.9 1.2 %shard_map.88 = (f32[2,5,4,16,128]{4,3,2,1,0:T(8,128)S(1)}, f32[2,5,4,16,128]{4,3,2,1,0:T(8,128)S(1)}, f32[2,5,4,16,128]{4,3,2,1,0:T(8,128)S(1)}, f32[32,16,128]{2,1,0:T(8,128)S(1)}, f32[32,16,128]{2,1,0:T(8,128)S(1)}) custom-call(f32[9]{0:T(128)S(1)} %copy-done.4, f32[9]{0:T(128)S(1)} %copy-done.2, f32[9]{0:T(128)S(1)} %copy-done.3, f32[9]{0:T(128)S(1)} %copy-done.1, ...), custom_call_target="tpu_custom_call" | custom-call | tf_op jit(solution)/shard_map/pallas_call | solution.py:555
  44.1 2.0 %collective-permute-start.5 = (f32[32,16,128]{2,1,0:T(8,128)S(1)}, f32[32,16,128]{2,1,0:T(8,128)S(1)}, u32[]{:S(2)}, u32[]{:S(2)}) collective-permute-start(f32[32,16,128]{2,1,0:T(8,128)S(1)} %get-tuple-element.29), channel_id=1, source_target_pairs={{0,16},{16,0},{32,48},{48,32},{64,80},{80,64},{96,112},{112,96},{1... | collective-permute-start | bytes 786440 | tf_op jit(solution)/shard_map/ppermute | solution.py:563
  46.2 4.2 %collective-permute-start.6 = (f32[32,16,128]{2,1,0:T(8,128)S(1)}, f32[32,16,128]{2,1,0:T(8,128)S(1)}, u32[]{:S(2)}, u32[]{:S(2)}) collective-permute-start(f32[32,16,128]{2,1,0:T(8,128)S(1)} %get-tuple-element.30), channel_id=1, source_target_pairs={{16,32},{32,16},{48,64},{64,48},{80,96},{96,80},{112,128},{128,112... | collective-permute-start | bytes 786440 | tf_op jit(solution)/shard_map/ppermute | solution.py:563
  50.4 7.4 %finish.1 = (f32[5,32,16,128]{3,2,1,0:T(8,128)}, f32[5,32,16,128]{3,2,1,0:T(8,128)}, f32[2,5,4,16,128]{4,3,2,1,0:T(8,128)S(1)}, f32[2,5,4,16,128]{4,3,2,1,0:T(8,128)S(1)}) custom-call(f32[9]{0:T(128)S(1)} %copy-done.4, f32[9]{0:T(128)S(1)} %copy-done.2, f32[9]{0:T(128)S(1)} %copy-done.3, f32[9]{0:T(128)S(1)} %copy-done.1, f32[16]{0:T(128)S(1)} %copy-done, ...), custom_call_target="tpu_custom_call" | custom-call | tf_op jit(solution)/shard_map/finish/pallas_call | solution.py:605
  57.9 2.1 %collective-permute-done.5.xe2 = f32[32,16,128]{2,1,0:T(8,128)S(1)} collective-permute-done((f32[32,16,128]{2,1,0:T(8,128)S(1)}, f32[32,16,128]{2,1,0:T(8,128)S(1)}, u32[]{:S(2)}, u32[]{:S(2)}) %collective-permute-start.5) | collective-permute-done | bytes 262176 | tf_op jit(solution)/shard_map/ppermute | solution.py:563
  59.9 0.0 collective-permute-done.6.xo2
  59.9 1.9 %edges.1 = (f32[5,32,16,128]{3,2,1,0:T(8,128)}, f32[5,32,16,128]{3,2,1,0:T(8,128)}) custom-call(f32[9]{0:T(128)S(1)} %copy-done.2, f32[9]{0:T(128)S(1)} %copy-done.3, f32[9]{0:T(128)S(1)} %copy-done.1, f32[16]{0:T(128)S(1)} %copy-done, f32[5,32,16,128]{3,2,1,0:T(8,128)S(1)} %get-tuple-element.20.state, ...), custom_call_target="tpu_custom_call", output_to_operand_aliasing={{0}: (9, {}), {1}: (10, {})} | custom-call | tf_op jit(solution)/shard_map/edges/pallas_call | solution.py:616
Async XLA Ops:
  0.6 1.9 %copy-start.1 = (f32[9]{0:T(128)S(1)}, f32[9]{0:T(128)}, u32[]{:S(2)}) copy-start(f32[9]{0:T(128)} %cf.7) | copy-start | bytes 112
  0.6 1.9 %copy-start = (f32[16]{0:T(128)S(1)}, f32[16]{0:T(128)}, u32[]{:S(2)}) copy-start(f32[16]{0:T(128)} %met.9) | copy-start | bytes 196
  2.5 18.6 %copy-start.2 = (f32[9]{0:T(128)S(1)}, f32[9]{0:T(128)}, u32[]{:S(2)}) copy-start(f32[9]{0:T(128)} %cr.7) | copy-start | bytes 112
  2.5 18.6 %copy-start.3 = (f32[9]{0:T(128)S(1)}, f32[9]{0:T(128)}, u32[]{:S(2)}) copy-start(f32[9]{0:T(128)} %ct.7) | copy-start | bytes 112
  2.5 18.6 %copy-start.4 = (f32[9]{0:T(128)S(1)}, f32[9]{0:T(128)}, u32[]{:S(2)}) copy-start(f32[9]{0:T(128)} %cx.5) | copy-start | bytes 112
  5.2 37.7 %collective-permute-start.2 = (f32[5,36,8,128]{3,2,1,0:T(8,128)S(1)}, f32[5,36,8,128]{3,2,1,0:T(8,128)S(1)}, u32[]{:S(2)}, u32[]{:S(2)}) collective-permute-start(f32[5,36,8,128]{3,2,1,0:T(8,128)S(1)} %get-tuple-element.26), channel_id=1, source_target_pairs={{0,2},{2,0},{4,6},{6,4},{8,10},{10,8},{12,14},{14,12},{1,3},{3,1},... | collective-permute-start | bytes 2211848 | tf_op jit(solution)/shard_map/ppermute | solution.py:563
  7.2 35.8 %collective-permute-start.3 = (f32[5,36,8,128]{3,2,1,0:T(8,128)S(1)}, f32[5,36,8,128]{3,2,1,0:T(8,128)S(1)}, u32[]{:S(2)}, u32[]{:S(2)}) collective-permute-start(f32[5,36,8,128]{3,2,1,0:T(8,128)S(1)} %get-tuple-element.27), channel_id=1, source_target_pairs={{2,4},{4,2},{6,8},{8,6},{10,12},{12,10},{3,5},{5,3},{7,9},{9,7},{1... | collective-permute-start | bytes 2211848 | tf_op jit(solution)/shard_map/ppermute | solution.py:563
  9.7 33.2 %collective-permute-start = (f32[15,4,16,128]{3,2,1,0:T(8,128)S(1)}, f32[15,4,16,128]{3,2,1,0:T(8,128)S(1)}, u32[]{:S(2)}, u32[]{:S(2)}) collective-permute-start(f32[15,4,16,128]{3,2,1,0:T(8,128)S(1)} %get-tuple-element.24), channel_id=1, source_target_pairs={{0,16},{16,0},{32,48},{48,32},{64,80},{80,64},{96,112},{112,96},{1... | collective-permute-start | bytes 1474568 | tf_op jit(solution)/shard_map/ppermute | solution.py:563
  13.2 29.7 %collective-permute-start.1 = (f32[15,4,16,128]{3,2,1,0:T(8,128)S(1)}, f32[15,4,16,128]{3,2,1,0:T(8,128)S(1)}, u32[]{:S(2)}, u32[]{:S(2)}) collective-permute-start(f32[15,4,16,128]{3,2,1,0:T(8,128)S(1)} %get-tuple-element.25), channel_id=1, source_target_pairs={{16,32},{32,16},{48,64},{64,48},{80,96},{96,80},{112,128},{128,112... | collective-permute-start | bytes 1474568 | tf_op jit(solution)/shard_map/ppermute | solution.py:563
  16.0 26.9 %collective-permute-start.4 = (f32[24,16,128]{2,1,0:T(8,128)S(1)}, f32[24,16,128]{2,1,0:T(8,128)S(1)}, u32[]{:S(2)}, u32[]{:S(2)}) collective-permute-start(f32[24,16,128]{2,1,0:T(8,128)S(1)} %get-tuple-element.28), channel_id=1, source_target_pairs={{0,1},{1,0},{2,3},{3,2},{4,5},{5,4},{6,7},{7,6},{8,9},{9,8},{10,11... | collective-permute-start | bytes 589832 | tf_op jit(solution)/shard_map/ppermute | solution.py:567
  44.1 15.8 %collective-permute-start.5 = (f32[32,16,128]{2,1,0:T(8,128)S(1)}, f32[32,16,128]{2,1,0:T(8,128)S(1)}, u32[]{:S(2)}, u32[]{:S(2)}) collective-permute-start(f32[32,16,128]{2,1,0:T(8,128)S(1)} %get-tuple-element.29), channel_id=1, source_target_pairs={{0,16},{16,0},{32,48},{48,32},{64,80},{80,64},{96,112},{112,96},{1... | collective-permute-start | bytes 786440 | tf_op jit(solution)/shard_map/ppermute | solution.py:563
  46.2 13.8 %collective-permute-start.6 = (f32[32,16,128]{2,1,0:T(8,128)S(1)}, f32[32,16,128]{2,1,0:T(8,128)S(1)}, u32[]{:S(2)}, u32[]{:S(2)}) collective-permute-start(f32[32,16,128]{2,1,0:T(8,128)S(1)} %get-tuple-element.30), channel_id=1, source_target_pairs={{16,32},{32,16},{48,64},{64,48},{80,96},{96,80},{112,128},{128,112... | collective-permute-start | bytes 786440 | tf_op jit(solution)/shard_map/ppermute | solution.py:563
